TPU v7x, 32 devices: a whole 2x2x4 slice. The times are simulated.
32 devices in a mesh: dp: 8 (over z, y), seq: 4 (over x, core).
Axes of the slice: x: 2, y: 2, z: 4, core: 2. Of those that a mesh axis runs over, the one named last changes fastest.
Arguments:
- tokens: float32 [16, 2048, 768], P('dp', 'seq'), may hold values from -6 to 6
- timesteps: int32 [16], P('dp'), may hold values from 0 to 1999
- lengths: int32 [16], P('dp'), may hold values from 512 to 2048, as said below
- time_weight: float32 [768, 768], P('dp'), may hold values from -0.21875 to 0.21875
- attn_gain: float32 [768], P('dp'), may hold values from 0.5 to 1.5
- attn_shift: float32 [768], P('dp'), may hold values from -4 to 4
- qkv_weight: float32 [768, 2304], P('dp'), may hold values from -0.21875 to 0.21875
- out_weight: float32 [768, 768], P('dp'), may hold values from -6 to 6
- out_bias: float32 [768], P('dp'), may hold values from -4 to 4
- mlp_gain: float32 [768], P('dp'), may hold values from 0.5 to 1.5
- mlp_shift: float32 [768], P('dp'), may hold values from -4 to 4
- up_weight: float32 [768, 3072], P('dp'), may hold values from -0.21875 to 0.21875
- up_bias: float32 [3072], P('dp'), may hold values from -6 to 6
- down_weight: float32 [3072, 768], P('dp'), may hold values from -0.109375 to 0.109375
- down_bias: float32 [768], P('dp'), may hold values from -4 to 4
- cotangent: float32 [16, 2048, 768], P('dp', 'seq'), may hold values from -6 to 6
Outputs:
- result: float32 [16, 2048, 768], P('dp', 'seq')
- tokens_grad: float32 [16, 2048, 768], P('dp', 'seq')
- time_weight_grad: float32 [768, 768], P('dp')
- attn_gain_grad: float32 [768], P('dp')
- attn_shift_grad: float32 [768], P('dp')
- qkv_weight_grad: float32 [768, 2304], P('dp')
- out_weight_grad: float32 [768, 768], P('dp')
- out_bias_grad: float32 [768], P('dp')
- mlp_gain_grad: float32 [768], P('dp')
- mlp_shift_grad: float32 [768], P('dp')
- up_weight_grad: float32 [768, 3072], P('dp')
- up_bias_grad: float32 [3072], P('dp')
- down_weight_grad: float32 [3072, 768], P('dp')
- down_bias_grad: float32 [768], P('dp')
Inputs may be any that keep to these rules, and one draw needn't show every extreme that they name: Slots of sequence s at positions below lengths[s] hold tokens, the others are padding; some sequence is full and some has 512 used slots.
All inputs are finite; a program needn't handle non-finite values.
Results may differ from a plain program's by a relative error of at most 0.013.
Values may be sent and summed in bfloat16 or wider, within the bound.
No kernel may reach another device: no remote copies, remote signals or barrier semaphores. Data moves between devices by JAX's collectives and lax.ppermute only.
A program may use at most 192 MiB of HBM per device.

v0:
```python
import functools, math
import jax, jax.numpy as jnp
from jax import lax
from jax.experimental import pallas as pl
from jax.experimental.pallas import tpu as pltpu
from jax.sharding import PartitionSpec as P


HEAD = 64
PAIR = 2 * HEAD
NT = (((1,), (1,)), ((), ()))
NN = (((1,), (0,)), ((), ()))
SCALE = 1.0 / math.sqrt(HEAD)


def dot32(left, right, dims):
    return lax.dot_general(left, right, dims, preferred_element_type=jnp.float32)


def one_head(block, which):
    lane = lax.broadcasted_iota(jnp.int32, block.shape, 1)
    return jnp.where(lane // HEAD == which, block.astype(jnp.float32), 0.0)


def attention_forward_kernel(bias_ref, q_ref, k_ref, v_ref, out_ref, wide_ref, log_ref, vt_ref, *, chunk):
    @pl.when(pl.program_id(1) == 0)
    def _():
        vt_ref[...] = v_ref[...].T

    total = k_ref.shape[0]
    mixed = []
    for which in range(2):
        query = (one_head(q_ref[...], which) * SCALE).astype(jnp.bfloat16)
        scores = []
        for start in range(0, total, chunk):
            rows = pl.ds(start, chunk)
            part = dot32(k_ref[rows, :], query, NT) + bias_ref[rows, :]
            scores.append(part)
        top = jnp.max(scores[0], axis=0, keepdims=True)
        for part in scores[1:]:
            top = jnp.maximum(top, jnp.max(part, axis=0, keepdims=True))
        totals = 0.0
        acc = 0.0
        for index, part in enumerate(scores):
            weights = jnp.exp(part - top)
            totals = totals + jnp.sum(weights, axis=0, keepdims=True)
            values = vt_ref[which * HEAD : (which + 1) * HEAD, index * chunk : (index + 1) * chunk]
            acc = acc + dot32(values, weights.astype(jnp.bfloat16), NN)
        mixed.append(acc / totals)
        log_ref[0, which : which + 1, :] = top + jnp.log(totals)
    joined = jnp.concatenate(mixed, axis=0)
    wide_ref[0] = joined
    out_ref[...] = joined.T.astype(jnp.bfloat16)


def attention_backward_kernel(
    bias_ref, q_ref, k_ref, v_ref, mixed_ref, grad_ref, log_ref,
    dq_ref, dk_ref, dv_ref, kt_ref, dk_acc, dv_acc, *, chunk
):
    step = pl.program_id(1)

    @pl.when(step == 0)
    def _():
        kt_ref[...] = k_ref[...].T
        dk_acc[...] = jnp.zeros_like(dk_acc)
        dv_acc[...] = jnp.zeros_like(dv_acc)

    total = k_ref.shape[0]
    centre_t = grad_ref[...].astype(jnp.float32).T * mixed_ref[0]
    queries = []
    grads = []
    for which in range(2):
        queries.append((one_head(q_ref[...], which) * SCALE).astype(jnp.bfloat16))
        grads.append(one_head(grad_ref[...], which).astype(jnp.bfloat16))
    dq_parts = [0.0, 0.0]
    for start in range(0, total, chunk):
        rows = pl.ds(start, chunk)
        dk_part = dk_acc[rows, :]
        dv_part = dv_acc[rows, :]
        for which in range(2):
            head = slice(which * HEAD, (which + 1) * HEAD)
            centre = jnp.sum(centre_t[head, :], axis=0, keepdims=True)
            scores = dot32(k_ref[rows, :], queries[which], NT) + bias_ref[rows, :]
            probs = jnp.exp(scores - log_ref[0, which : which + 1, :])
            grad_probs = dot32(v_ref[rows, :], grads[which], NT)
            grad_scores = (probs * (grad_probs - centre)).astype(jnp.bfloat16)
            dv_part = dv_part + dot32(probs.astype(jnp.bfloat16), grads[which], NN)
            dk_part = dk_part + dot32(grad_scores, queries[which], NN)
            dq_parts[which] = dq_parts[which] + dot32(
                kt_ref[head, start : start + chunk], grad_scores, NN
            )
        dk_acc[rows, :] = dk_part
        dv_acc[rows, :] = dv_part
    dq_ref[...] = (jnp.concatenate(dq_parts, axis=0).T * SCALE).astype(jnp.bfloat16)

    @pl.when(step == pl.num_programs(1) - 1)
    def _():
        dk_ref[...] = dk_acc[...].astype(jnp.bfloat16)
        dv_ref[...] = dv_acc[...].astype(jnp.bfloat16)


def cost_of(total, pairs, products):
    return pl.CostEstimate(
        flops=pairs * 2 * products * 2 * total * total * 4 * HEAD,
        transcendentals=pairs * 2 * total * total,
        bytes_accessed=pairs * total * PAIR * 16,
    )


def attention_forward(projected, bias, first, pairs, block=512, chunk=512):
    total = projected.shape[0]
    every = projected.shape[1] // (3 * PAIR)
    block = min(block, total)
    return pl.pallas_call(
        functools.partial(attention_forward_kernel, chunk=min(chunk, total)),
        name="attention_forward",
        cost_estimate=cost_of(total, pairs, 2),
        grid=(pairs, total // block),
        in_specs=[
            pl.BlockSpec((total, 1), lambda p, i: (0, 0)),
            pl.BlockSpec((block, PAIR), lambda p, i: (i, first + p)),
            pl.BlockSpec((total, PAIR), lambda p, i: (0, every + first + p)),
            pl.BlockSpec((total, PAIR), lambda p, i: (0, 2 * every + first + p)),
        ],
        out_specs=[
            pl.BlockSpec((block, PAIR), lambda p, i: (i, p)),
            pl.BlockSpec((1, PAIR, block), lambda p, i: (p, 0, i)),
            pl.BlockSpec((1, 2, block), lambda p, i: (p, 0, i)),
        ],
        out_shape=[
            jax.ShapeDtypeStruct((total, pairs * PAIR), jnp.bfloat16),
            jax.ShapeDtypeStruct((pairs, PAIR, total), jnp.float32),
            jax.ShapeDtypeStruct((pairs, 2, total), jnp.float32),
        ],
        scratch_shapes=[pltpu.VMEM((PAIR, total), jnp.bfloat16)],
    )(bias, projected, projected, projected)


def attention_backward(projected, mixed, grad_mixed, logs, bias, first, block=512, chunk=256):
    total = projected.shape[0]
    every = projected.shape[1] // (3 * PAIR)
    pairs = mixed.shape[0]
    block = min(block, total)
    out = jax.ShapeDtypeStruct((total, pairs * PAIR), jnp.bfloat16)
    return pl.pallas_call(
        functools.partial(attention_backward_kernel, chunk=min(chunk, total)),
        name="attention_backward",
        cost_estimate=cost_of(total, pairs, 5),
        grid=(pairs, total // block),
        in_specs=[
            pl.BlockSpec((total, 1), lambda p, i: (0, 0)),
            pl.BlockSpec((block, PAIR), lambda p, i: (i, first + p)),
            pl.BlockSpec((total, PAIR), lambda p, i: (0, every + first + p)),
            pl.BlockSpec((total, PAIR), lambda p, i: (0, 2 * every + first + p)),
            pl.BlockSpec((1, PAIR, block), lambda p, i: (p, 0, i)),
            pl.BlockSpec((block, PAIR), lambda p, i: (i, first + p)),
            pl.BlockSpec((1, 2, block), lambda p, i: (p, 0, i)),
        ],
        out_specs=[
            pl.BlockSpec((block, PAIR), lambda p, i: (i, p)),
            pl.BlockSpec((total, PAIR), lambda p, i: (0, p)),
            pl.BlockSpec((total, PAIR), lambda p, i: (0, p)),
        ],
        out_shape=[out, out, out],
        scratch_shapes=[
            pltpu.VMEM((PAIR, total), jnp.bfloat16),
            pltpu.VMEM((total, PAIR), jnp.float32),
            pltpu.VMEM((total, PAIR), jnp.float32),
        ],
    )(bias, projected, projected, projected, mixed, grad_mixed, logs)


epsilon = 1e-05

CORE_SWAP = ((0, 1), (1, 0), (2, 3), (3, 2))
CHIP_SWAP = ((0, 2), (2, 0), (1, 3), (3, 1))
LOW = jnp.bfloat16
F32 = jnp.float32


def swap_core(values):
    return lax.ppermute(values, "seq", CORE_SWAP)


def swap_chip(values):
    return lax.ppermute(values, "seq", CHIP_SWAP)


def swap_bit(values, size, bit):
    return lax.ppermute(values, "dp", [(i, i ^ bit) for i in range(size)])


def bits_of(size):
    return [1 << b for b in range(size.bit_length() - 1)]


def gather_dp(values, size):
    me = lax.axis_index("dp")
    held = values[None]
    for bit in reversed(bits_of(size)):
        got = swap_bit(held, size, bit)
        upper = (me & bit) != 0
        first = jnp.where(upper, got, held)
        second = jnp.where(upper, held, got)
        held = jnp.stack([first, second], axis=1).reshape((-1,) + values.shape)
    return held


def scatter_dp(values, size, wire):
    me = lax.axis_index("dp")
    held = values
    for bit in bits_of(size):
        upper = (me & bit) != 0
        halves = held.reshape((held.shape[0] // 2, 2) + held.shape[1:])
        send = jnp.where(upper, halves[:, 0], halves[:, 1]).astype(wire)
        keep = jnp.where(upper, halves[:, 1], halves[:, 0])
        held = keep + swap_bit(send, size, bit).astype(F32)
    return held[0]


def sinusoid(steps_given, width):
    half = width // 2
    freqs = jnp.exp(-math.log(10000.0) * jnp.arange(half, dtype=F32) / half)
    angles = steps_given.astype(F32)[..., None] * freqs
    return jnp.concatenate([jnp.sin(angles), jnp.cos(angles)], axis=-1)


def norm_parts(values):
    center = values - jnp.mean(values, axis=-1, keepdims=True)
    rate = lax.rsqrt(jnp.mean(center * center, axis=-1, keepdims=True) + epsilon)
    return center * rate, rate


def norm_pull(grad, xhat, rate, gain):
    c = grad * gain
    return rate * (
        c - jnp.mean(c, axis=-1, keepdims=True) - xhat * jnp.mean(c * xhat, axis=-1, keepdims=True)
    )


def gelu_both(values):
    cdf = 0.5 * (1.0 + lax.erf(values * math.sqrt(0.5)))
    slope = cdf + values * (jnp.exp(-0.5 * values * values) * (1.0 / math.sqrt(2.0 * math.pi)))
    return (values * cdf).astype(LOW), slope.astype(LOW)


def rows_dot(left, right):
    return dot32(left, right, (((0,), (0,)), ((), ())))


def column_sums(values):
    return rows_dot(jnp.ones((values.shape[0], 8), LOW), values)[0]


def take_half(values, which, axis):
    size = values.shape[axis] // 2
    return lax.dynamic_slice_in_dim(values, which * size, size, axis)


def layer(
    tokens, timesteps, lengths, time_weight, attn_gain, attn_shift, qkv_weight, out_weight,
    out_bias, mlp_gain, mlp_shift, up_weight, up_bias, down_weight, down_bias, cotangent, *, size
):
    local = tokens.shape[1]
    width = tokens.shape[2]
    half = width // 2
    wide = up_weight.shape[1]
    shard = time_weight.shape[0]
    deep = down_weight.shape[0]
    spot = lax.axis_index("seq")
    row = lax.axis_index("dp")
    chip = spot // 2
    core = spot % 2
    on_one = core == 1

    def natural(own, other, axis):
        return jnp.where(
            on_one,
            jnp.concatenate([other, own], axis=axis),
            jnp.concatenate([own, other], axis=axis),
        )

    pieces = [qkv_weight[:, k * half : (k + 1) * half] for k in range(6)]
    qkv_shard = jnp.where(
        on_one, jnp.concatenate(pieces[1::2], axis=1), jnp.concatenate(pieces[0::2], axis=1)
    ).astype(LOW)
    vectors = jnp.concatenate(
        [attn_gain, attn_shift, out_bias, mlp_gain, mlp_shift, down_bias, up_bias]
    ).astype(LOW).astype(F32)
    vectors = jnp.concatenate([timesteps.astype(F32), vectors])[None]
    qkv_shard, vectors, tokens, time_weight, up_weight, down_weight, out_weight = (
        lax.optimization_barrier(
            (qkv_shard, vectors, tokens, time_weight, up_weight, down_weight, out_weight)
        )
    )
    qkv_own = gather_dp(qkv_shard, size).reshape(width, 3 * half)

    up_pairs = up_weight.astype(LOW).reshape(shard, size, 2, deep // 2)
    up_shard = lax.dynamic_index_in_dim(up_pairs, core, 2, False).reshape(shard, wide // 2)
    down_shard = take_half(down_weight.astype(LOW), core, 0)
    out_shard = take_half(out_weight.astype(LOW), core, 1)
    packed = jnp.concatenate(
        [
            up_shard[:, :width],
            up_shard[:, width:],
            down_shard,
            jnp.concatenate([out_shard[: shard // 2], out_shard[shard // 2 :]], axis=1),
        ],
        axis=0,
    )
    own_pack = lax.all_gather(packed, "dp", axis=0, tiled=False)

    def unpack(pack):
        a = pack[:, :shard].reshape(width, width)
        b = pack[:, shard : 2 * shard].reshape(width, width)
        up = jnp.concatenate([a, b], axis=1)
        down = pack[:, 2 * shard : 2 * shard + deep // 2].reshape(wide // 2, width)
        last = pack[:, 2 * shard + deep // 2 :]
        out = jnp.concatenate([last[:, :, :half], last[:, :, half:]], axis=1).reshape(width, half)
        return up, down, out

    mine = lax.dynamic_index_in_dim(tokens, chip, 0, False)
    source = jnp.concatenate(
        [mine, swap_chip(lax.dynamic_index_in_dim(tokens, 1 - chip, 0, False))], axis=0
    )
    small = gather_dp(vectors, size)[:, 0]
    steps = small[:, :2]
    gain_a, shift_a, bias_out, gain_m, shift_m, bias_down = [
        small[:, 2 + k * shard : 2 + (k + 1) * shard].reshape(width) for k in range(6)
    ]
    bias_up = small[:, 2 + 6 * shard :].reshape(size, 2, deep // 2)
    embedded = sinusoid(steps, width).astype(LOW)
    embedded = jnp.where(chip == 1, embedded[:, ::-1], embedded)
    own_rows = lax.dynamic_slice_in_dim(embedded, row * shard, shard, 2)
    time_parts = jnp.dot(own_rows[:, 0], time_weight.astype(LOW), preferred_element_type=F32)
    time_shift = scatter_dp(time_parts[:, None], size, F32)

    length = lax.dynamic_index_in_dim(lengths, chip, 0, False)
    places = jnp.arange(local, dtype=jnp.int32)

    def positions(which):
        return jnp.concatenate(
            [(2 * chip + which) * local + places, (2 * (1 - chip) + which) * local + places]
        )

    own_places = positions(core)
    valid = (own_places < length)[:, None]
    bias = jnp.where(
        jnp.concatenate([own_places, positions(1 - core)]) < length, 0.0, -1e30
    ).astype(F32)[:, None]

    hidden = source + time_shift
    xhat_a, rate_a = norm_parts(hidden)
    normed_own = (xhat_a * gain_a + shift_a).astype(LOW)
    normed_all = jnp.concatenate([normed_own, swap_core(normed_own)], axis=0)
    projected = jnp.dot(normed_all, qkv_own, preferred_element_type=F32).astype(LOW)
    projected, cotangent = lax.optimization_barrier((projected, cotangent))
    count = hidden.shape[0]
    lead = half // PAIR - 1
    mixed_one, wide_one, logs_one = attention_forward(projected, bias, 0, lead)
    mixed_one, own_pack, projected_late = lax.optimization_barrier((mixed_one, own_pack, projected))
    other_pack = swap_core(own_pack)
    sent_one = swap_core(mixed_one[count:])
    mixed_two, wide_two, logs_two = attention_forward(projected_late, bias, lead, 1)
    attended = natural(
        jnp.concatenate([mixed_one[:count], mixed_two[:count]], axis=1),
        jnp.concatenate([sent_one, swap_core(mixed_two[count:])], axis=1),
        1,
    )
    wide_mixed = jnp.concatenate([wide_one, wide_two], axis=0)
    logs = jnp.concatenate([logs_one, logs_two], axis=0)

    cot_mine = lax.dynamic_index_in_dim(cotangent, chip, 0, False)
    cot_send = lax.dynamic_index_in_dim(cotangent, 1 - chip, 0, False)
    cot = jnp.concatenate([cot_mine, swap_chip(cot_send)], axis=0)
    up_a, down_a, out_a = unpack(own_pack)
    up_b, down_b, out_b = unpack(other_pack)
    bias_up_a = lax.dynamic_index_in_dim(bias_up, core, 1, False).reshape(wide // 2)
    bias_up_b = lax.dynamic_index_in_dim(bias_up, 1 - core, 1, False).reshape(wide // 2)
    out_full = natural(out_a, out_b, 1)

    middle = hidden + jnp.dot(attended, out_full, preferred_element_type=F32) + bias_out
    xhat_m, rate_m = norm_parts(middle)
    normed_two = (xhat_m * gain_m + shift_m).astype(LOW)
    act_a, slope_a = gelu_both(jnp.dot(normed_two, up_a, preferred_element_type=F32) + bias_up_a)
    act_b, slope_b = gelu_both(jnp.dot(normed_two, up_b, preferred_element_type=F32) + bias_up_b)
    branch = (
        jnp.dot(act_a, down_a, preferred_element_type=F32)
        + jnp.dot(act_b, down_b, preferred_element_type=F32)
        + bias_down
    )
    result = jnp.where(valid, middle + branch, 0.0)

    grad_out = jnp.where(valid, cot, 0.0)
    grad_low = grad_out.astype(LOW)
    pre_a = (dot32(grad_low, down_a, NT) * slope_a.astype(F32)).astype(LOW)
    pre_b = (dot32(grad_low, down_b, NT) * slope_b.astype(F32)).astype(LOW)
    pre_a, pre_b = lax.optimization_barrier((pre_a, pre_b))
    grad_normed_two = dot32(pre_a, up_a, NT) + dot32(pre_b, up_b, NT)
    grad_middle = grad_out + norm_pull(grad_normed_two, xhat_m, rate_m, gain_m)
    grad_branch = grad_middle.astype(LOW)
    grad_attended = dot32(grad_branch, out_full, NT).astype(LOW)
    low_half, high_half = grad_attended[:, :half], grad_attended[:, half:]
    heads_own = jnp.where(on_one, high_half, low_half)
    heads_other = swap_core(jnp.where(on_one, low_half, high_half))
    grad_heads = jnp.concatenate([heads_own, heads_other], axis=0)

    def pack_grads(up, down, out):
        parts = [
            up[:, :width].reshape(size, shard, width),
            up[:, width:].reshape(size, shard, width),
            down.reshape(size, deep // 2, width),
        ]
        last = out.reshape(size, shard, half)
        parts.append(jnp.concatenate([last[:, : shard // 2], last[:, shard // 2 :]], axis=2))
        return jnp.concatenate([part.astype(LOW) for part in parts], axis=1)

    out_grad = rows_dot(attended, grad_branch)
    out_low, out_high = out_grad[:, :half], out_grad[:, half:]
    grads_a = pack_grads(
        rows_dot(normed_two, pre_a), rows_dot(act_a, grad_low), jnp.where(on_one, out_high, out_low)
    )
    grads_b = pack_grads(
        rows_dot(normed_two, pre_b), rows_dot(act_b, grad_low), jnp.where(on_one, out_low, out_high)
    )
    summed = (grads_a.astype(F32) + swap_core(grads_b).astype(F32)).astype(LOW)
    grad_heads, summed = lax.optimization_barrier((grad_heads, summed))
    shards = lax.psum_scatter(summed, "dp", scatter_dimension=0, tiled=False)
    dq, dk, dv = attention_backward(projected, wide_mixed, grad_heads, logs, bias, 0)
    grad_projected = jnp.concatenate([dq, dk, dv], axis=1)
    part_other = swap_core(dot32(grad_projected[count:], qkv_own, NT).astype(LOW))
    grad_projected, part_other = lax.optimization_barrier((grad_projected, part_other))
    qkv_grad = rows_dot(normed_all, grad_projected).reshape(size, 2, shard // 2, 3 * half)
    on_chip_one = chip == 1
    qkv_keep = jnp.where(on_chip_one, qkv_grad[:, 1], qkv_grad[:, 0])
    qkv_send = jnp.where(on_chip_one, qkv_grad[:, 0], qkv_grad[:, 1]).astype(LOW)
    qkv_mine = scatter_dp(qkv_keep + swap_chip(qkv_send).astype(F32), size, LOW)
    qkv_more = swap_chip(qkv_mine)
    qkv_mine = jnp.where(
        on_chip_one,
        jnp.concatenate([qkv_more, qkv_mine], axis=0),
        jnp.concatenate([qkv_mine, qkv_more], axis=0),
    )
    qkv_other = swap_core(qkv_mine)
    qkv_out = jnp.concatenate(
        [
            natural(
                qkv_mine[:, k * half : (k + 1) * half], qkv_other[:, k * half : (k + 1) * half], 1
            )
            for k in range(3)
        ],
        axis=1,
    )

    part_own = dot32(grad_projected[:count], qkv_own, NT)
    grad_normed_one = part_own + part_other.astype(F32)
    tokens_grad = grad_middle + norm_pull(grad_normed_one, xhat_a, rate_a, gain_a)

    sum_bias_up = natural(
        column_sums(pre_a).reshape(size, 1, deep // 2),
        column_sums(pre_b).reshape(size, 1, deep // 2),
        1,
    ).reshape(size, deep)
    vector_sums = jnp.concatenate(
        [
            jnp.sum(grad_normed_one * xhat_a, axis=0).reshape(size, shard),
            jnp.sum(grad_normed_one, axis=0).reshape(size, shard),
            column_sums(grad_branch).reshape(size, shard),
            jnp.sum(grad_normed_two * xhat_m, axis=0).reshape(size, shard),
            jnp.sum(grad_normed_two, axis=0).reshape(size, shard),
            column_sums(grad_low).reshape(size, shard),
            sum_bias_up,
        ],
        axis=1,
    )
    token_sum = jnp.sum(tokens_grad, axis=0, keepdims=True)
    sums = jnp.concatenate([vector_sums.reshape(1, -1), token_sum], axis=1)
    sums = sums + swap_core(sums)
    sums_there = swap_chip(sums)
    tokens_grad, sums_there = lax.optimization_barrier((tokens_grad, sums_there))
    vector_sums = (sums + sums_there)[:, : vector_sums.size].reshape(vector_sums.shape)
    vector_mine = scatter_dp(vector_sums[:, None], size, F32)[0]
    vector_out = [vector_mine[k * shard : (k + 1) * shard] for k in range(6)]
    both = jnp.concatenate([sums, sums_there], axis=0)[:, -width:]
    gathered = gather_dp(both, size)
    sums_own = gathered[:, 0]
    sums_other = gathered[:, 1]
    exact = dict(precision=lax.Precision.HIGHEST, preferred_element_type=F32)
    contract = (((0,), (0,)), ((), ()))
    time_grad = lax.dot_general(
        own_rows[:, 0].astype(F32), sums_own, contract, **exact
    ) + lax.dot_general(own_rows[:, 1].astype(F32), sums_other, contract, **exact)

    shards = shards.astype(F32)
    shards = shards + swap_chip(shards.astype(LOW)).astype(F32)
    shards_other = swap_core(shards.astype(LOW)).astype(F32)

    def unpack_grads(pack):
        up = jnp.concatenate([pack[:shard], pack[shard : 2 * shard]], axis=1)
        down = pack[2 * shard : 2 * shard + deep // 2]
        last = pack[2 * shard + deep // 2 :]
        return up, down, jnp.concatenate([last[:, :half], last[:, half:]], axis=0)

    up_ga, down_ga, out_ga = unpack_grads(shards)
    up_gb, down_gb, out_gb = unpack_grads(shards_other)
    up_out = natural(
        up_ga.reshape(shard, size, 1, deep // 2), up_gb.reshape(shard, size, 1, deep // 2), 2
    ).reshape(shard, wide)

    def hand_back(values, wire):
        kept = values[:local]
        got = swap_chip(values[local:].astype(wire)).astype(F32)
        return jnp.where(chip == 1, jnp.stack([got, kept]), jnp.stack([kept, got]))

    return (
        hand_back(result, F32),
        hand_back(tokens_grad, LOW),
        time_grad,
        vector_out[0],
        vector_out[1],
        qkv_out,
        natural(out_ga, out_gb, 1),
        vector_out[2],
        vector_out[3],
        vector_out[4],
        up_out,
        vector_mine[6 * shard :],
        natural(down_ga, down_gb, 0),
        vector_out[5],
    )


def solution(mesh):
    batch = P("dp", "seq", None)
    flat = P("dp")
    grid = P("dp", None)
    in_specs = (
        batch, flat, flat, grid, flat, flat, grid, grid, flat, flat, flat, grid, flat, grid, flat,
        batch,
    )
    out_specs = (
        batch, batch, grid, flat, flat, grid, grid, flat, flat, flat, grid, flat, grid, flat,
    )
    body = functools.partial(layer, size=mesh.shape["dp"])
    return jax.shard_map(
        body, mesh=mesh, in_specs=in_specs, out_specs=out_specs, check_vma=False
    )
```

profile of v0, /device:TPU:0, one launch (start us, length us, event | category | flops | bytes accessed | tf_op | source)
XLA Modules:
  0.0 562.3 jit_solution(2776336901322528921)
XLA Ops:
  14.2 4.1 collective-permute-start.1
  18.3 3.2 constant_dynamic-slice_fusion.3
  27.3 2.5 dynamic-slice_reduce_fusion
  34.4 2.7 collective-permute-done.2
  38.7 2.2 collective-permute-done.3
  43.2 2.5 collective-permute-done.4
  50.7 4.0 collective-permute-start.6
  54.9 14.4 %collective-permute-done.6 = f32[1,1,768]{2,1,0:T(1,128)S(1)} collective-permute-done((f32[1,1,768]{2,1,0:T(1,128)S(1)}, f32[1,1,768]{2,1,0:T(1,128)S(1)}, u32[]{:S(2)}, u32[]{:S(2)}) %collective-permute-start.6) | collective-permute-done | bytes 3104 | tf_op jit(solution)/shard_map/ppermute | solution.py:190
  69.4 5.3 collective-permute-done.9
  80.1 3.1 add_convert_fusion.2
  85.5 25.9 %collective-permute-done.10 = bf16[4,96,1152]{2,1,0:T(8,128)(2,1)} collective-permute-done((bf16[4,96,1152]{2,1,0:T(8,128)(2,1)S(1)}, bf16[4,96,1152]{2,1,0:T(8,128)(2,1)}, u32[]{:S(2)}, u32[]{:S(2)}) %collective-permute-start.10) | collective-permute-done | bytes 884768 | tf_op jit(solution)/shard_map/ppermute | solution.py:190
  114.5 8.6 %convolution_convert_fusion.q_ref.k_ref.v_ref = bf16[2048,1152]{1,0:T(8,128)(2,1)} fusion(bf16[768,1152]{1,0:T(8,128)(2,1)S(1)} %bitcast.366, bf16[1024,768]{0,1:T(8,128)(2,1)} %collective-permute-done.7, bf16[1024,768]{0,1:T(8,128)(2,1)} %add_convert_fusion.2), kind=kOutput, calls=%fused_computation.3 | convolution fusion | flops 3632529408 | bytes 9633792 | tf_op jit(solution)/shard_map/dot_general | solution.py:356
  123.2 32.3 %attention_forward.2 = (bf16[2048,256]{1,0:T(8,128)(2,1)}, f32[2,128,2048]{2,1,0:T(8,128)}, f32[2,2,2048]{2,1,0:T(2,128)}) custom-call(f32[2048,1]{1,0:T(8,128)} %broadcast_select_fusion.2.bias_ref, bf16[2048,1152]{1,0:T(8,128)(2,1)} %convolution_convert_fusion.q_ref.k_ref.v_ref, bf16[2048,1152]{1,0:T(8,128)(2,1)} %convolution_convert_fusion.q_ref.k_ref.v_ref, ...), custom_call_target="tpu_custom_call" | custom-call | flops 17179869184 | bytes 8388608 | tf_op jit(solution)/shard_map/attention_forward/pallas_call | solution.py:114
  155.6 3.8 constant_dynamic-slice_fusion.1
  159.3 3.0 copy.260
  164.9 3.0 copy.259
  167.9 31.6 %collective-permute-done.15 = f32[512,768]{0,1:T(8,128)} collective-permute-done((f32[512,768]{0,1:T(8,128)}, f32[512,768]{0,1:T(8,128)}, u32[]{:S(2)}, u32[]{:S(2)}) %collective-permute-start.15) | collective-permute-done | bytes 1572896 | tf_op jit(solution)/shard_map/ppermute | solution.py:186
  199.5 3.6 fusion.10
  205.5 17.6 %attention_forward.3 = (bf16[2048,128]{1,0:T(8,128)(2,1)}, f32[1,128,2048]{2,1,0:T(8,128)}, f32[1,2,2048]{2,1,0:T(2,128)}) custom-call(f32[2048,1]{1,0:T(8,128)} %broadcast_select_fusion.2.bias_ref, bf16[2048,1152]{1,0:T(8,128)(2,1)} %convolution_convert_fusion.q_ref.k_ref.v_ref, bf16[2048,1152]{1,0:T(8,128)(2,1)} %convolution_convert_fusion.q_ref.k_ref.v_ref, ...), custom_call_target="tpu_custom_call" | custom-call | flops 8589934592 | bytes 4194304 | tf_op jit(solution)/shard_map/attention_forward/pallas_call | solution.py:114
  228.3 3.6 fusion.122
  232.9 2.5 fusion.100
  235.4 5.6 multiply_convert_fusion.2
  241.0 1.9 slice.512
  243.1 5.7 %multiply_convert_fusion = bf16[1024,1536]{1,0:T(8,128)(2,1)S(1)} fusion(bf16[1024,768]{0,1:T(8,128)(2,1)S(1)} %copy-done.11, bf16[1536,768]{1,0:T(8,128)(2,1)S(1)} %bitcast.362, f32[1024,1536]{1,0:T(8,128)S(1)} %get-tuple-element.249, f32[1536]{0:T(1024)S(1)} %add.306), kind=kOutput, calls=%fused_computation.14 | convolution fusion | flops 2436366336 | bytes 13375488 | tf_op jit(solution)/shard_map/dot_general | solution.py:17
  248.8 5.5 multiply_convert_fusion.3
  254.3 5.9 %multiply_convert_fusion.1 = bf16[1024,1536]{1,0:T(8,128)(2,1)S(1)} fusion(bf16[1024,768]{0,1:T(8,128)(2,1)S(1)} %copy-done.11, bf16[1536,768]{1,0:T(8,128)(2,1)S(1)} %bitcast.360, f32[1024,1536]{1,0:T(8,128)S(1)} %get-tuple-element.247, f32[1536]{0:T(1024)S(1)} %add.301), kind=kOutput, calls=%fused_computation.15 | convolution fusion | flops 2436366336 | bytes 13375488 | tf_op jit(solution)/shard_map/dot_general | solution.py:17
  260.2 2.8 convolution_convert_fusion.2
  264.9 2.9 convolution_convert_fusion.1
  267.9 2.6 fusion.22
  270.5 3.3 multiply_reduce_fusion
  273.9 2.4 multiply_add_fusion.1
  276.3 3.4 fusion.93
  279.9 4.8 maximum_maximum_fusion
  285.6 4.0 pad_maximum_fusion.1.mixed_ref
  293.0 2.7 fusion.123
  296.5 3.1 add_select_fusion
  299.6 2.0 fusion.104
  303.1 2.8 convolution_convert_fusion.4
  306.1 2.9 convolution_convert_fusion.3
  310.4 7.3 %add_convert_fusion = bf16[8,432,768]{2,1,0:T(8,128)(2,1)} fusion(bf16[8,432,768]{2,1,0:T(8,128)(2,1)} %collective-permute-done.17, bf16[8,48,384]{2,1,0:T(8,128)(2,1)S(1)} %get-tuple-element.199, bf16[8,48,384]{2,1,0:T(8,128)(2,1)S(1)} %get-tuple-element.198, bf16[8,192,768]{2,1,0:T(8,128)(2,1)S(1)} %bitcast.365, bf16[8,96,768]{2,1,0:T(8,128)(2,1)S(1)} %bitcast.356, ...), kind=kLoop, calls=%fused_computation | loop fusion | flops 34504704 | bytes 15925248 | tf_op jit(solution)/shard_map/convert_element_type | solution.py:426
  317.6 73.7 %attention_backward.1 = (bf16[2048,384]{1,0:T(8,128)(2,1)}, bf16[2048,384]{1,0:T(8,128)(2,1)}, bf16[2048,384]{1,0:T(8,128)(2,1)}) custom-call(f32[2048,1]{1,0:T(8,128)} %broadcast_select_fusion.2.bias_ref, bf16[2048,1152]{1,0:T(8,128)(2,1)} %convolution_convert_fusion.q_ref.k_ref.v_ref, bf16[2048,1152]{1,0:T(8,128)(2,1)} %convolution_convert_fusion.q_ref.k_ref.v_ref, ...), custom_call_target="tpu_custom_call" | custom-call | flops 64424509440 | bytes 12582912 | tf_op jit(solution)/shard_map/attention_backward/pallas_call | solution.py:145
  394.9 3.4 fusion.18
  399.2 2.5 convolution_reduce_fusion.1
  401.7 2.6 convolution_reduce_fusion
  404.5 2.4 convolution_reduce_fusion.3
  407.2 4.3 maximum_select_fusion
  411.5 3.7 copy.290
  416.6 7.7 %multiply_reduce_fusion.1 = (f32[768]{0:T(1024)S(1)}, f32[1024]{0:T(1024)S(1)}, f32[1024]{0:T(1024)S(1)}, f32[768]{0:T(1024)S(1)}, f32[1024,768]{0,1:T(8,128)}) fusion(f32[1024]{0:T(1024)S(1)} %copy-done.48, f32[1024]{0:T(1024)S(1)} %copy-done.44, f32[768]{0:T(1024)S(1)} %copy-done.42, f32[512,768]{0,1:T(8,128)} %collective-permute-done, ...), kind=kOutput, calls=%fused_computation.32 | convolution fusion | flops 1822159360 | bytes 12021760 | tf_op jit(solution)/shard_map/dot_general | solution.py:17
  424.6 5.3 fusion.99
  430.1 7.3 %fusion.15 = f32[768,1152]{1,0:T(8,128)S(1)} fusion(bf16[2048,1152]{1,0:T(8,128)(2,1)} %copy-done.37, bf16[1024,768]{0,1:T(8,128)(2,1)} %collective-permute-done.7, bf16[1024,768]{0,1:T(8,128)(2,1)} %add_convert_fusion.2), kind=kOutput, calls=%fused_computation.55 | convolution fusion | flops 3630170112 | bytes 11403264 | tf_op jit(solution)/shard_map/dot_general | solution.py:17
  445.0 2.7 collective-permute-start.25
  451.3 2.5 collective-permute-done.23
  458.6 1.9 collective-permute-done.27
  462.4 2.7 collective-permute-start.29
  465.8 15.7 %collective-permute-done.29 = bf16[4,48,1152]{2,1,0:T(8,128)(2,1)S(1)} collective-permute-done((bf16[4,48,1152]{2,1,0:T(8,128)(2,1)S(1)}, bf16[4,48,1152]{2,1,0:T(8,128)(2,1)S(1)}, u32[]{:S(2)}, u32[]{:S(2)}) %collective-permute-start.29) | collective-permute-done | bytes 442400 | tf_op jit(solution)/shard_map/ppermute | solution.py:190
  481.8 6.3 %collective-permute-done.30 = bf16[2,48,1152]{2,1,0:T(8,128)(2,1)S(1)} collective-permute-done((bf16[2,48,1152]{2,1,0:T(8,128)(2,1)S(1)}, bf16[2,48,1152]{2,1,0:T(8,128)(2,1)S(1)}, u32[]{:S(2)}, u32[]{:S(2)}) %collective-permute-start.30) | collective-permute-done | bytes 221216 | tf_op jit(solution)/shard_map/ppermute | solution.py:190
  488.5 6.2 %collective-permute-done.31 = bf16[1,48,1152]{2,1,0:T(8,128)(2,1)S(1)} collective-permute-done((bf16[1,48,1152]{2,1,0:T(8,128)(2,1)S(1)}, bf16[1,48,1152]{2,1,0:T(8,128)(2,1)S(1)}, u32[]{:S(2)}, u32[]{:S(2)}) %collective-permute-start.31) | collective-permute-done | bytes 110624 | tf_op jit(solution)/shard_map/ppermute | solution.py:190
  496.4 4.3 collective-permute-done.32
  501.1 2.2 maximum_select_fusion.2
  503.3 3.8 copy.291
  507.1 19.2 %reduce-scatter.2.cloned.1.call-done = bf16[1,432,768]{2,1,0:T(8,128)(2,1)} async-done(((bf16[8,432,768]{2,1,0:T(8,128)(2,1)}), bf16[1,432,768]{2,1,0:T(8,128)(2,1)}) %reduce-scatter.2.cloned.1.call-update) | async-done | bytes 663568 | tf_op jit(solution)/shard_map/reduce_scatter | solution.py:428
  528.9 13.9 %collective-permute-done.34 = bf16[432,768]{1,0:T(8,128)(2,1)S(1)} collective-permute-done((bf16[432,768]{1,0:T(8,128)(2,1)}, bf16[432,768]{1,0:T(8,128)(2,1)S(1)}, u32[]{:S(2)}, u32[]{:S(2)}) %collective-permute-start.34) | collective-permute-done | bytes 663584 | tf_op jit(solution)/shard_map/ppermute | solution.py:186
  549.3 2.6 select_n.690
  551.9 2.4 maximum_select_fusion.6
  (347 shorter events, 95.8 us)
Async XLA Ops:
  7.2 23.9 %copy-start = (f32[384,768]{1,0:T(8,128)S(1)}, f32[384,768]{1,0:T(8,128)}, u32[]{:S(2)}) copy-start(f32[384,768]{1,0:T(8,128)} %param.29) | copy-start | bytes 3538948
  7.2 148.3 %all-gather.3.cloned.1.call-start = ((), (), s32[]{:S(2)}) async-start(), calls=%async_computation.2 | async-start | bytes 5971968 | tf_op jit(solution)/shard_map/all_gather | solution.py:311
  14.2 18.5 %collective-permute-start.1 = (f32[1,1,962]{2,1,0:T(1,128)S(1)}, f32[1,1,962]{2,1,0:T(1,128)S(1)}, u32[]{:S(2)}, u32[]{:S(2)}) collective-permute-start(f32[1,1,962]{2,1,0:T(1,128)S(1)} %bitcast.399), channel_id=1, source_target_pairs={{0,16},{4,20},{8,24},{12,28},{16,0},{20,4},{24,8},{28,12},{1,17},{... | collective-permute-start | bytes 11552 | tf_op jit(solution)/shard_map/ppermute | solution.py:190
  23.1 53.4 %collective-permute-start = (f32[512,768]{0,1:T(8,128)}, f32[512,768]{0,1:T(8,128)}, u32[]{:S(2)}, u32[]{:S(2)}) collective-permute-start(f32[512,768]{0,1:T(8,128)} %bitcast.369), channel_id=1, source_target_pairs={{0,2},{2,0},{1,3},{3,1},{4,6},{6,4},{5,7},{7,5},{8,10},{10,8},{9,1... | collective-permute-start | bytes 4718600 | tf_op jit(solution)/shard_map/ppermute | solution.py:186
  24.6 25.1 %collective-permute-start.8 = (bf16[1,96,1152]{2,1,0:T(8,128)(2,1)S(1)}, bf16[1,96,1152]{2,1,0:T(8,128)(2,1)S(1)}, u32[]{:S(2)}, u32[]{:S(2)}) collective-permute-start(bf16[1,96,1152]{2,1,0:T(8,128)(2,1)S(1)} %bitcast.379), channel_id=1, source_target_pairs={{0,16},{4,20},{8,24},{12,28},{16,0},{20,4},{24,8},{28,12},{1,17},{... | collective-permute-start | bytes 663560 | tf_op jit(solution)/shard_map/ppermute | solution.py:190
  27.3 14.2 %copy-start.39 = (f32[96,768]{1,0:T(8,128)S(1)}, f32[96,768]{1,0:T(8,128)}, u32[]{:S(2)}) copy-start(f32[96,768]{1,0:T(8,128)} %param.19) | copy-start | bytes 884740
  31.2 17.4 %copy-start.53 = (s32[2]{0:T(128)S(1)}, s32[2]{0:T(128)}, u32[]{:S(2)}) copy-start(s32[2]{0:T(128)} %param.18) | copy-start | bytes 28
  32.1 494.2 %reduce-scatter.2.cloned.1.call-start = ((), (), s32[]{:S(2)}) async-start(), calls=%async_computation.1 | async-start | bytes 5971968 | tf_op jit(solution)/shard_map/reduce_scatter | solution.py:428
  32.7 4.3 collective-permute-start.2
  37.1 3.8 collective-permute-start.3
  41.6 4.1 collective-permute-start.4
  45.8 4.0 collective-permute-start.5
  48.6 179.7 %copy-start.2 = (f32[1,512,768]{1,2,0:T(8,128)}, f32[1,512,768]{1,2,0:T(8,128)S(1)}, u32[]{:S(2)}) copy-start(f32[1,512,768]{1,2,0:T(8,128)S(1)} %copy.237) | copy-start | bytes 4718596
  49.9 24.9 %collective-permute-start.9 = (bf16[2,96,1152]{2,1,0:T(8,128)(2,1)S(1)}, bf16[2,96,1152]{2,1,0:T(8,128)(2,1)S(1)}, u32[]{:S(2)}, u32[]{:S(2)}) collective-permute-start(bf16[2,96,1152]{2,1,0:T(8,128)(2,1)S(1)} %maximum_bitcast_fusion), channel_id=1, source_target_pairs={{0,8},{4,12},{8,0},{12,4},{16,24},{20,28},{24,16},{28,20},{1,9},{5... | collective-permute-start | bytes 1327112 | tf_op jit(solution)/shard_map/ppermute | solution.py:190
  50.7 18.7 %collective-permute-start.6 = (f32[1,1,768]{2,1,0:T(1,128)S(1)}, f32[1,1,768]{2,1,0:T(1,128)S(1)}, u32[]{:S(2)}, u32[]{:S(2)}) collective-permute-start(f32[1,1,768]{2,1,0:T(1,128)S(1)} %fusion.77), channel_id=1, source_target_pairs={{0,16},{4,20},{8,24},{12,28},{16,0},{20,4},{24,8},{28,12},{1,17},{... | collective-permute-start | bytes 9224 | tf_op jit(solution)/shard_map/ppermute | solution.py:190
  54.9 25.2 %copy-start.45 = (f32[768]{0:T(1024)}, f32[768]{0:T(1024)S(1)}, u32[]{:S(2)}) copy-start(f32[768]{0:T(1024)S(1)} %mul.200) | copy-start | bytes 9220
  69.4 158.9 %copy-start.41 = (f32[768]{0:T(1024)}, f32[768]{0:T(1024)S(1)}, u32[]{:S(2)}) copy-start(f32[768]{0:T(1024)S(1)} %fusion.76) | copy-start | bytes 9220
  74.9 5.2 copy-start.14
  75.0 36.4 %collective-permute-start.10 = (bf16[4,96,1152]{2,1,0:T(8,128)(2,1)S(1)}, bf16[4,96,1152]{2,1,0:T(8,128)(2,1)}, u32[]{:S(2)}, u32[]{:S(2)}) collective-permute-start(bf16[4,96,1152]{2,1,0:T(8,128)(2,1)S(1)} %bitcast.357), channel_id=1, source_target_pairs={{0,4},{4,0},{8,12},{12,8},{16,20},{20,16},{24,28},{28,24},{1,5},{5... | collective-permute-start | bytes 2654216 | tf_op jit(solution)/shard_map/ppermute | solution.py:190
  78.2 5.1 copy-start.43
  80.1 5.3 copy-start.47
  83.3 30.1 %collective-permute-start.7 = (bf16[1024,768]{0,1:T(8,128)(2,1)}, bf16[1024,768]{0,1:T(8,128)(2,1)}, u32[]{:S(2)}, u32[]{:S(2)}) collective-permute-start(bf16[1024,768]{0,1:T(8,128)(2,1)} %add_convert_fusion.2), channel_id=1, source_target_pairs={{0,1},{1,0},{2,3},{3,2},{4,5},{5,4},{6,7},{7,6},{8,9},{9,8},{10,11... | collective-permute-start | bytes 4718600 | tf_op jit(solution)/shard_map/ppermute | solution.py:182
  155.5 71.2 %collective-permute-start.13 = (bf16[8,432,768]{2,1,0:T(8,128)(2,1)}, bf16[8,432,768]{2,1,0:T(8,128)(2,1)}, u32[]{:S(2)}, u32[]{:S(2)}) collective-permute-start(bf16[8,432,768]{2,1,0:T(8,128)(2,1)} %bitcast.349), channel_id=1, source_target_pairs={{0,1},{1,0},{2,3},{3,2},{4,5},{5,4},{6,7},{7,6},{8,9},{9,8},{10,11... | collective-permute-start | bytes 15925256 | tf_op jit(solution)/shard_map/ppermute | solution.py:182
  162.4 37.1 %collective-permute-start.15 = (f32[512,768]{0,1:T(8,128)}, f32[512,768]{0,1:T(8,128)}, u32[]{:S(2)}, u32[]{:S(2)}) collective-permute-start(f32[512,768]{0,1:T(8,128)} %bitcast.370), channel_id=1, source_target_pairs={{0,2},{2,0},{1,3},{3,1},{4,6},{6,4},{5,7},{7,5},{8,10},{10,8},{9,1... | collective-permute-start | bytes 4718600 | tf_op jit(solution)/shard_map/ppermute | solution.py:186
  167.9 35.2 %copy-start.31 = (bf16[2048,256]{1,0:T(8,128)(2,1)S(1)}, bf16[2048,256]{1,0:T(8,128)(2,1)}, u32[]{:S(2)}) copy-start(bf16[2048,256]{1,0:T(8,128)(2,1)} %get-tuple-element.52) | copy-start | bytes 3145732
  204.1 24.2 %collective-permute-start.11 = (bf16[1024,256]{1,0:T(8,128)(2,1)}, bf16[1024,256]{1,0:T(8,128)(2,1)}, u32[]{:S(2)}, u32[]{:S(2)}) collective-permute-start(bf16[1024,256]{1,0:T(8,128)(2,1)} %get-tuple-element.184), channel_id=1, source_target_pairs={{0,1},{1,0},{2,3},{3,2},{4,5},{5,4},{6,7},{7,6},{8,9},{9,8},{10,11... | collective-permute-start | bytes 1572872 | tf_op jit(solution)/shard_map/ppermute | solution.py:182
  205.4 43.3 %copy-start.28 = (bf16[8,96,768]{2,1,0:T(8,128)(2,1)}, bf16[8,96,768]{2,1,0:T(8,128)(2,1)S(1)}, u32[]{:S(2)}) copy-start(bf16[8,96,768]{2,1,0:T(8,128)(2,1)S(1)} %get-tuple-element.156) | copy-start | bytes 3538948
  226.1 28.2 %copy-start.18 = (bf16[8,192,768]{2,1,0:T(8,128)(2,1)}, bf16[8,192,768]{2,1,0:T(8,128)(2,1)S(1)}, u32[]{:S(2)}) copy-start(bf16[8,192,768]{2,1,0:T(8,128)(2,1)S(1)} %slice.406) | copy-start | bytes 7077892
  226.1 2.2 collective-permute-start.12
  226.7 5.2 copy-start.33
  231.9 41.9 %copy-start.4 = (f32[1024,768]{0,1:T(8,128)}, f32[1024,768]{0,1:T(8,128)S(1)}, u32[]{:S(2)}) copy-start(f32[1024,768]{0,1:T(8,128)S(1)} %get-tuple-element.245) | copy-start | bytes 9437188
  232.9 27.3 %copy-start.26 = (bf16[1024,768]{0,1:T(8,128)(2,1)}, bf16[1024,768]{0,1:T(8,128)(2,1)S(1)}, u32[]{:S(2)}) copy-start(bf16[1024,768]{0,1:T(8,128)(2,1)S(1)} %add_convert_fusion.1) | copy-start | bytes 4718596
  242.9 5.8 %copy-start.20 = (bf16[8,192,768]{2,1,0:T(8,128)(2,1)}, bf16[8,192,768]{2,1,0:T(8,128)(2,1)S(1)}, u32[]{:S(2)}) copy-start(bf16[8,192,768]{2,1,0:T(8,128)(2,1)S(1)} %slice.512) | copy-start | bytes 7077892
  243.1 5.7 %copy-start.30 = (bf16[8,96,768]{2,1,0:T(8,128)(2,1)S(1)}, bf16[8,96,768]{2,1,0:T(8,128)(2,1)}, u32[]{:S(2)}) copy-start(bf16[8,96,768]{2,1,0:T(8,128)(2,1)} %get-tuple-element.157) | copy-start | bytes 3538948
  248.7 21.8 %copy-start.15 = (bf16[1024,1536]{1,0:T(8,128)(2,1)}, bf16[1024,1536]{1,0:T(8,128)(2,1)S(1)}, u32[]{:S(2)}) copy-start(bf16[1024,1536]{1,0:T(8,128)(2,1)S(1)} %multiply_convert_fusion) | copy-start | bytes 9437188
  260.2 7.7 %copy-start.16 = (bf16[1024,1536]{1,0:T(8,128)(2,1)}, bf16[1024,1536]{1,0:T(8,128)(2,1)S(1)}, u32[]{:S(2)}) copy-start(bf16[1024,1536]{1,0:T(8,128)(2,1)S(1)} %multiply_convert_fusion.1) | copy-start | bytes 9437188
  279.9 5.1 copy-start.49
  279.9 5.1 copy-start.52
  284.7 25.7 %collective-permute-start.17 = (bf16[8,432,768]{2,1,0:T(8,128)(2,1)}, bf16[8,432,768]{2,1,0:T(8,128)(2,1)}, u32[]{:S(2)}, u32[]{:S(2)}) collective-permute-start(bf16[8,432,768]{2,1,0:T(8,128)(2,1)} %maximum_maximum_fusion), channel_id=1, source_target_pairs={{0,1},{1,0},{2,3},{3,2},{4,5},{5,4},{6,7},{7,6},{8,9},{9,8},{10,11... | collective-permute-start | bytes 15925256 | tf_op jit(solution)/shard_map/ppermute | solution.py:182
  291.4 17.7 %collective-permute-start.16 = (bf16[1024,384]{1,0:T(8,128)(2,1)S(1)}, bf16[1024,384]{1,0:T(8,128)(2,1)S(1)}, u32[]{:S(2)}, u32[]{:S(2)}) collective-permute-start(bf16[1024,384]{1,0:T(8,128)(2,1)S(1)} %get-tuple-element.175), channel_id=1, source_target_pairs={{0,1},{1,0},{2,3},{3,2},{4,5},{5,4},{6,7},{7,6},{8,9},{9,8},{10,11... | collective-permute-start | bytes 2359304 | tf_op jit(solution)/shard_map/ppermute | solution.py:182
  301.6 105.6 %collective-permute-start.14 = (f32[512,768]{0,1:T(8,128)}, f32[512,768]{0,1:T(8,128)}, u32[]{:S(2)}, u32[]{:S(2)}) collective-permute-start(f32[512,768]{0,1:T(8,128)} %get-tuple-element.164), channel_id=1, source_target_pairs={{0,2},{2,0},{1,3},{3,1},{4,6},{6,4},{5,7},{7,5},{8,10},{10,8},{9,1... | collective-permute-start | bytes 4718600 | tf_op jit(solution)/shard_map/ppermute | solution.py:186
  398.2 17.1 %collective-permute-start.18 = (bf16[1024,768]{0,1:T(8,128)(2,1)}, bf16[1024,768]{0,1:T(8,128)(2,1)}, u32[]{:S(2)}, u32[]{:S(2)}) collective-permute-start(bf16[1024,768]{0,1:T(8,128)(2,1)} %fusion.18), channel_id=1, source_target_pairs={{0,1},{1,0},{2,3},{3,2},{4,5},{5,4},{6,7},{7,6},{8,9},{9,8},{10,11... | collective-permute-start | bytes 4718600 | tf_op jit(solution)/shard_map/ppermute | solution.py:182
  401.7 5.4 copy-start.12
  429.9 7.5 %collective-permute-start.19 = (f32[1,8448]{1,0:T(1,128)S(1)}, f32[1,8448]{1,0:T(1,128)S(1)}, u32[]{:S(2)}, u32[]{:S(2)}) collective-permute-start(f32[1,8448]{1,0:T(1,128)S(1)} %constant_dynamic-update-slice_fusion.3), channel_id=1, source_target_pairs={{0,1},{1,0},{2,3},{3,2},{4,5},{5,4},{6,7},{7,6},{8,9},{9,8},{10,11... | collective-permute-start | bytes 101384 | tf_op jit(solution)/shard_map/ppermute | solution.py:182
  437.4 4.0 collective-permute-start.20
  439.4 22.6 %collective-permute-start.28 = (bf16[8,48,1152]{2,1,0:T(8,128)(2,1)S(1)}, bf16[8,48,1152]{2,1,0:T(8,128)(2,1)S(1)}, u32[]{:S(2)}, u32[]{:S(2)}) collective-permute-start(bf16[8,48,1152]{2,1,0:T(8,128)(2,1)S(1)} %fusion.24), channel_id=1, source_target_pairs={{0,2},{2,0},{1,3},{3,1},{4,6},{6,4},{5,7},{7,5},{8,10},{10,8},{9,1... | collective-permute-start | bytes 2654216 | tf_op jit(solution)/shard_map/ppermute | solution.py:186
  441.6 20.3 %copy-start.10 = (f32[768,1152]{1,0:T(8,128)S(1)}, f32[768,1152]{1,0:T(8,128)}, u32[]{:S(2)}) copy-start(f32[768,1152]{1,0:T(8,128)} %copy-done.9) | copy-start | bytes 10616836
  441.6 7.2 %collective-permute-start.22 = (f32[1,2,768]{2,1,0:T(2,128)S(1)}, f32[1,2,768]{2,1,0:T(2,128)S(1)}, u32[]{:S(2)}, u32[]{:S(2)}) collective-permute-start(f32[1,2,768]{2,1,0:T(2,128)S(1)} %fusion.66), channel_id=1, source_target_pairs={{0,16},{4,20},{8,24},{12,28},{16,0},{20,4},{24,8},{28,12},{1,17},{... | collective-permute-start | bytes 18440 | tf_op jit(solution)/shard_map/ppermute | solution.py:190
  445.0 5.8 %collective-permute-start.25 = (f32[4,1,960]{2,1,0:T(1,128)S(1)}, f32[4,1,960]{2,1,0:T(1,128)S(1)}, u32[]{:S(2)}, u32[]{:S(2)}) collective-permute-start(f32[4,1,960]{2,1,0:T(1,128)S(1)} %fusion.54), channel_id=1, source_target_pairs={{0,4},{4,0},{8,12},{12,8},{16,20},{20,16},{24,28},{28,24},{1,5},{5... | collective-permute-start | bytes 46088 | tf_op jit(solution)/shard_map/ppermute | solution.py:190
  447.7 53.2 %collective-permute-start.21 = (bf16[512,768]{0,1:T(8,128)(2,1)S(1)}, bf16[512,768]{0,1:T(8,128)(2,1)S(1)}, u32[]{:S(2)}, u32[]{:S(2)}) collective-permute-start(bf16[512,768]{0,1:T(8,128)(2,1)S(1)} %slice.670), channel_id=1, source_target_pairs={{0,2},{2,0},{1,3},{3,1},{4,6},{6,4},{5,7},{7,5},{8,10},{10,8},{9,1... | collective-permute-start | bytes 2359304 | tf_op jit(solution)/shard_map/ppermute | solution.py:186
  448.9 4.9 collective-permute-start.23
  450.8 4.7 collective-permute-start.26
  455.6 4.9 collective-permute-start.27
  456.7 9.0 %collective-permute-start.24 = (f32[4,2,768]{2,1,0:T(2,128)S(1)}, f32[4,2,768]{2,1,0:T(2,128)S(1)}, u32[]{:S(2)}, u32[]{:S(2)}) collective-permute-start(f32[4,2,768]{2,1,0:T(2,128)S(1)} %bitcast.396), channel_id=1, source_target_pairs={{0,4},{4,0},{8,12},{12,8},{16,20},{20,16},{24,28},{28,24},{1,5},{5... | collective-permute-start | bytes 73736 | tf_op jit(solution)/shard_map/ppermute | solution.py:190
  462.4 25.8 %copy-start.51 = (bf16[8,2,96]{2,0,1:T(8,128)(2,1)S(1)}, bf16[8,2,96]{2,0,1:T(8,128)(2,1)}, u32[]{:S(2)}) copy-start(bf16[8,2,96]{2,0,1:T(8,128)(2,1)} %copy-done.50) | copy-start | bytes 9220
  462.4 19.1 %collective-permute-start.29 = (bf16[4,48,1152]{2,1,0:T(8,128)(2,1)S(1)}, bf16[4,48,1152]{2,1,0:T(8,128)(2,1)S(1)}, u32[]{:S(2)}, u32[]{:S(2)}) collective-permute-start(bf16[4,48,1152]{2,1,0:T(8,128)(2,1)S(1)} %fusion.27), channel_id=1, source_target_pairs={{0,4},{4,0},{8,12},{12,8},{16,20},{20,16},{24,28},{28,24},{1,5},{5... | collective-permute-start | bytes 1327112 | tf_op jit(solution)/shard_map/ppermute | solution.py:190
  481.6 6.4 %collective-permute-start.30 = (bf16[2,48,1152]{2,1,0:T(8,128)(2,1)S(1)}, bf16[2,48,1152]{2,1,0:T(8,128)(2,1)S(1)}, u32[]{:S(2)}, u32[]{:S(2)}) collective-permute-start(bf16[2,48,1152]{2,1,0:T(8,128)(2,1)S(1)} %fusion.32), channel_id=1, source_target_pairs={{0,8},{4,12},{8,0},{12,4},{16,24},{20,28},{24,16},{28,20},{1,9},{5... | collective-permute-start | bytes 663560 | tf_op jit(solution)/shard_map/ppermute | solution.py:190
  488.1 6.6 %collective-permute-start.31 = (bf16[1,48,1152]{2,1,0:T(8,128)(2,1)S(1)}, bf16[1,48,1152]{2,1,0:T(8,128)(2,1)S(1)}, u32[]{:S(2)}, u32[]{:S(2)}) collective-permute-start(bf16[1,48,1152]{2,1,0:T(8,128)(2,1)S(1)} %fusion.41), channel_id=1, source_target_pairs={{0,16},{4,20},{8,24},{12,28},{16,0},{20,4},{24,8},{28,12},{1,17},{... | collective-permute-start | bytes 331784 | tf_op jit(solution)/shard_map/ppermute | solution.py:190
  494.8 6.0 %collective-permute-start.32 = (f32[48,1152]{1,0:T(8,128)S(1)}, f32[48,1152]{1,0:T(8,128)S(1)}, u32[]{:S(2)}, u32[]{:S(2)}) collective-permute-start(f32[48,1152]{1,0:T(8,128)S(1)} %fusion.33), channel_id=1, source_target_pairs={{0,2},{2,0},{1,3},{3,1},{4,6},{6,4},{5,7},{7,5},{8,10},{10,8},{9,1... | collective-permute-start | bytes 663560 | tf_op jit(solution)/shard_map/ppermute | solution.py:186
  500.8 27.0 %collective-permute-start.33 = (f32[96,1152]{1,0:T(8,128)S(1)}, f32[96,1152]{1,0:T(8,128)S(1)}, u32[]{:S(2)}, u32[]{:S(2)}) collective-permute-start(f32[96,1152]{1,0:T(8,128)S(1)} %maximum_select_fusion.8), channel_id=1, source_target_pairs={{0,1},{1,0},{2,3},{3,2},{4,5},{5,4},{6,7},{7,6},{8,9},{9,8},{10,11... | collective-permute-start | bytes 1327112 | tf_op jit(solution)/shard_map/ppermute | solution.py:182
  526.3 16.5 %copy-start.32 = (bf16[1,432,768]{2,1,0:T(8,128)(2,1)S(1)}, bf16[1,432,768]{2,1,0:T(8,128)(2,1)}, u32[]{:S(2)}) copy-start(bf16[1,432,768]{2,1,0:T(8,128)(2,1)} %reduce-scatter.2.cloned.1.call-done) | copy-start | bytes 1990660
  526.3 16.5 %collective-permute-start.34 = (bf16[432,768]{1,0:T(8,128)(2,1)}, bf16[432,768]{1,0:T(8,128)(2,1)S(1)}, u32[]{:S(2)}, u32[]{:S(2)}) collective-permute-start(bf16[432,768]{1,0:T(8,128)(2,1)} %bitcast.380), channel_id=1, source_target_pairs={{0,2},{2,0},{1,3},{3,1},{4,6},{6,4},{5,7},{7,5},{8,10},{10,8},{9,1... | collective-permute-start | bytes 1990664 | tf_op jit(solution)/shard_map/ppermute | solution.py:186
  543.8 3.7 collective-permute-start.35
  548.0 7.1 %copy-start.1 = (f32[384,768]{1,0:T(8,128)S(1)}, f32[384,768]{1,0:T(8,128)}, u32[]{:S(2)}) copy-start(f32[384,768]{1,0:T(8,128)} %param.29) | copy-start | bytes 3538948
  (31 other events, 81.4 us)
Sparse Core Ops, SparseCore 0:
  32.2 107.8 all-gather.2
  415.4 110.8 reduce-scatter.1
where the time goes:
time: 568 us; the launch traced here: 562 us
  waiting for transfers between devices  159 us (28%)
  Pallas kernels  124 us (22%)
  matrix products  90.8 us (16%)
  local copies, waits for them, and re-layouts  69.4 us (12%)
  other arithmetic  64 us (11%)
  starting transfers between devices  39.9 us (7%)
  between operations  15.9 us (3%)
    ppermute x18, waiting for transfers between devices, swap_bit(): return lax.ppermute(values, 'dp', [(i, i ^ bit) for i in range(size)])  87.9 us
    pallas_call x1, Pallas kernels, attention_backward(): pl.pallas_call(functools.partial(attention_backward_kernel, chunk=min(chu...  73.7 us
    dot_general x17, matrix products, dot32(): lax.dot_general(left, right, dims, preferred_element_type=jnp.float32)  60.1 us
    ppermute x8, waiting for transfers between devices, swap_chip(): return lax.ppermute(values, 'seq', CHIP_SWAP)  51.4 us
    pallas_call x2, Pallas kernels, attention_forward(): pl.pallas_call(functools.partial(attention_forward_kernel, chunk=min(chun...  50 us
    ppermute x18, starting transfers between devices, swap_bit(): return lax.ppermute(values, 'dp', [(i, i ^ bit) for i in range(size)])  27.4 us
    reduce_scatter x1, waiting for transfers between devices, layer(): shards = lax.psum_scatter(summed, 'dp', scatter_dimension=0, tiled=False)  19.2 us
    unnamed x119, local copies, waits for them, and re-layouts  17.8 us
  transfers between devices with their start and end apart: 38, of which 19 were waited for; matrix products, arithmetic and copies ran while one was open for 26% of the time, Pallas kernels for 22%

commit v1 on v0

--- a/solution.py
+++ b/solution.py
@@ -2,6 +2,7 @@
 import jax, jax.numpy as jnp
 from jax import lax
 from jax.experimental import pallas as pl
+from jax.experimental.layout import Layout, with_layout_constraint
 from jax.experimental.pallas import tpu as pltpu
 from jax.sharding import PartitionSpec as P
 
@@ -194,15 +195,18 @@
     return [1 << b for b in range(size.bit_length() - 1)]
 
 
+def gather_step(held, size, bit):
+    upper = (lax.axis_index("dp") & bit) != 0
+    got = swap_bit(held, size, bit)
+    first = jnp.where(upper, got, held)
+    second = jnp.where(upper, held, got)
+    return jnp.stack([first, second], axis=1).reshape((-1,) + held.shape[1:])
+
+
 def gather_dp(values, size):
-    me = lax.axis_index("dp")
     held = values[None]
     for bit in reversed(bits_of(size)):
-        got = swap_bit(held, size, bit)
-        upper = (me & bit) != 0
-        first = jnp.where(upper, got, held)
-        second = jnp.where(upper, held, got)
-        held = jnp.stack([first, second], axis=1).reshape((-1,) + values.shape)
+        held = gather_step(held, size, bit)
     return held
 
 
@@ -214,8 +218,13 @@
         halves = held.reshape((held.shape[0] // 2, 2) + held.shape[1:])
         send = jnp.where(upper, halves[:, 0], halves[:, 1]).astype(wire)
         keep = jnp.where(upper, halves[:, 1], halves[:, 0])
-        held = keep + swap_bit(send, size, bit).astype(F32)
+        got = swap_bit(send, size, bit)
+        held = keep + got.astype(F32)
     return held[0]
+
+
+def row_major(values):
+    return with_layout_constraint(values, Layout(tuple(range(values.ndim))))
 
 
 def sinusoid(steps_given, width):
@@ -272,6 +281,7 @@
     chip = spot // 2
     core = spot % 2
     on_one = core == 1
+    on_chip_one = chip == 1
 
     def natural(own, other, axis):
         return jnp.where(
@@ -293,7 +303,6 @@
             (qkv_shard, vectors, tokens, time_weight, up_weight, down_weight, out_weight)
         )
     )
-    qkv_own = gather_dp(qkv_shard, size).reshape(width, 3 * half)
 
     up_pairs = up_weight.astype(LOW).reshape(shard, size, 2, deep // 2)
     up_shard = lax.dynamic_index_in_dim(up_pairs, core, 2, False).reshape(shard, wide // 2)
@@ -308,6 +317,12 @@
         ],
         axis=0,
     )
+    held = qkv_shard[None]
+    for bit in reversed(bits_of(size)):
+        if bit == 1:
+            held, packed = lax.optimization_barrier((held, packed))
+        held = gather_step(held, size, bit)
+    qkv_own = held.reshape(width, 3 * half)
     own_pack = lax.all_gather(packed, "dp", axis=0, tiled=False)
 
     def unpack(pack):
@@ -315,14 +330,14 @@
         b = pack[:, shard : 2 * shard].reshape(width, width)
         up = jnp.concatenate([a, b], axis=1)
         down = pack[:, 2 * shard : 2 * shard + deep // 2].reshape(wide // 2, width)
-        last = pack[:, 2 * shard + deep // 2 :]
-        out = jnp.concatenate([last[:, :, :half], last[:, :, half:]], axis=1).reshape(width, half)
-        return up, down, out
+        return up, down
+
+    def unpack_out(last):
+        return jnp.concatenate([last[:, :, :half], last[:, :, half:]], axis=1).reshape(width, half)
 
     mine = lax.dynamic_index_in_dim(tokens, chip, 0, False)
-    source = jnp.concatenate(
-        [mine, swap_chip(lax.dynamic_index_in_dim(tokens, 1 - chip, 0, False))], axis=0
-    )
+    there = lax.dynamic_index_in_dim(tokens, 1 - chip, 0, False)
+    source = jnp.concatenate([mine, swap_chip(there)], axis=0)
     small = gather_dp(vectors, size)[:, 0]
     steps = small[:, :2]
     gain_a, shift_a, bias_out, gain_m, shift_m, bias_down = [
@@ -349,7 +364,7 @@
         jnp.concatenate([own_places, positions(1 - core)]) < length, 0.0, -1e30
     ).astype(F32)[:, None]
 
-    hidden = source + time_shift
+    hidden = row_major(row_major(source) + time_shift)
     xhat_a, rate_a = norm_parts(hidden)
     normed_own = (xhat_a * gain_a + shift_a).astype(LOW)
     normed_all = jnp.concatenate([normed_own, swap_core(normed_own)], axis=0)
@@ -359,7 +374,9 @@
     lead = half // PAIR - 1
     mixed_one, wide_one, logs_one = attention_forward(projected, bias, 0, lead)
     mixed_one, own_pack, projected_late = lax.optimization_barrier((mixed_one, own_pack, projected))
-    other_pack = swap_core(own_pack)
+    rest = 2 * shard + deep // 2
+    other_out = swap_core(own_pack[:, rest:])
+    other_pack = swap_core(own_pack[:, :rest])
     sent_one = swap_core(mixed_one[count:])
     mixed_two, wide_two, logs_two = attention_forward(projected_late, bias, lead, 1)
     attended = natural(
@@ -373,13 +390,15 @@
     cot_mine = lax.dynamic_index_in_dim(cotangent, chip, 0, False)
     cot_send = lax.dynamic_index_in_dim(cotangent, 1 - chip, 0, False)
     cot = jnp.concatenate([cot_mine, swap_chip(cot_send)], axis=0)
-    up_a, down_a, out_a = unpack(own_pack)
-    up_b, down_b, out_b = unpack(other_pack)
+    cot = row_major(cot)
+    out_full = natural(unpack_out(own_pack[:, rest:]), unpack_out(other_out), 1)
+    up_a, down_a = unpack(own_pack)
+    up_b, down_b = unpack(other_pack)
     bias_up_a = lax.dynamic_index_in_dim(bias_up, core, 1, False).reshape(wide // 2)
     bias_up_b = lax.dynamic_index_in_dim(bias_up, 1 - core, 1, False).reshape(wide // 2)
-    out_full = natural(out_a, out_b, 1)
 
     middle = hidden + jnp.dot(attended, out_full, preferred_element_type=F32) + bias_out
+    middle = row_major(middle)
     xhat_m, rate_m = norm_parts(middle)
     normed_two = (xhat_m * gain_m + shift_m).astype(LOW)
     act_a, slope_a = gelu_both(jnp.dot(normed_two, up_a, preferred_element_type=F32) + bias_up_a)
@@ -389,15 +408,16 @@
         + jnp.dot(act_b, down_b, preferred_element_type=F32)
         + bias_down
     )
-    result = jnp.where(valid, middle + branch, 0.0)
+    result = row_major(jnp.where(valid, middle + branch, 0.0))
+    result_got = swap_chip(result[local:])
 
     grad_out = jnp.where(valid, cot, 0.0)
     grad_low = grad_out.astype(LOW)
     pre_a = (dot32(grad_low, down_a, NT) * slope_a.astype(F32)).astype(LOW)
     pre_b = (dot32(grad_low, down_b, NT) * slope_b.astype(F32)).astype(LOW)
     pre_a, pre_b = lax.optimization_barrier((pre_a, pre_b))
-    grad_normed_two = dot32(pre_a, up_a, NT) + dot32(pre_b, up_b, NT)
-    grad_middle = grad_out + norm_pull(grad_normed_two, xhat_m, rate_m, gain_m)
+    grad_normed_two = row_major(dot32(pre_a, up_a, NT) + dot32(pre_b, up_b, NT))
+    grad_middle = row_major(grad_out + norm_pull(grad_normed_two, xhat_m, rate_m, gain_m))
     grad_branch = grad_middle.astype(LOW)
     grad_attended = dot32(grad_branch, out_full, NT).astype(LOW)
     low_half, high_half = grad_attended[:, :half], grad_attended[:, half:]
@@ -429,18 +449,14 @@
     dq, dk, dv = attention_backward(projected, wide_mixed, grad_heads, logs, bias, 0)
     grad_projected = jnp.concatenate([dq, dk, dv], axis=1)
     part_other = swap_core(dot32(grad_projected[count:], qkv_own, NT).astype(LOW))
-    grad_projected, part_other = lax.optimization_barrier((grad_projected, part_other))
-    qkv_grad = rows_dot(normed_all, grad_projected).reshape(size, 2, shard // 2, 3 * half)
-    on_chip_one = chip == 1
-    qkv_keep = jnp.where(on_chip_one, qkv_grad[:, 1], qkv_grad[:, 0])
-    qkv_send = jnp.where(on_chip_one, qkv_grad[:, 0], qkv_grad[:, 1]).astype(LOW)
-    qkv_mine = scatter_dp(qkv_keep + swap_chip(qkv_send).astype(F32), size, LOW)
-    qkv_more = swap_chip(qkv_mine)
-    qkv_mine = jnp.where(
-        on_chip_one,
-        jnp.concatenate([qkv_more, qkv_mine], axis=0),
-        jnp.concatenate([qkv_mine, qkv_more], axis=0),
-    )
+    qkv_grad = rows_dot(normed_all, grad_projected).reshape(size, shard, 3 * half)
+    (
+        qkv_grad, grad_projected, pre_a, pre_b, grad_branch, grad_low, grad_normed_two,
+    ) = lax.optimization_barrier(
+        (qkv_grad, grad_projected, pre_a, pre_b, grad_branch, grad_low, grad_normed_two)
+    )
+    qkv_mine = scatter_dp(qkv_grad, size, LOW)
+    qkv_mine = qkv_mine + swap_chip(qkv_mine.astype(LOW)).astype(F32)
     qkv_other = swap_core(qkv_mine)
     qkv_out = jnp.concatenate(
         [
@@ -453,8 +469,10 @@
     )
 
     part_own = dot32(grad_projected[:count], qkv_own, NT)
-    grad_normed_one = part_own + part_other.astype(F32)
-    tokens_grad = grad_middle + norm_pull(grad_normed_one, xhat_a, rate_a, gain_a)
+    grad_normed_one = row_major(part_own + part_other.astype(F32))
+    tokens_grad = row_major(
+        grad_middle + norm_pull(grad_normed_one, xhat_a, rate_a, gain_a)
+    )
 
     sum_bias_up = natural(
         column_sums(pre_a).reshape(size, 1, deep // 2),
@@ -477,7 +495,10 @@
     sums = jnp.concatenate([vector_sums.reshape(1, -1), token_sum], axis=1)
     sums = sums + swap_core(sums)
     sums_there = swap_chip(sums)
-    tokens_grad, sums_there = lax.optimization_barrier((tokens_grad, sums_there))
+    tokens_grad, sums_there, result_got, result = lax.optimization_barrier(
+        (tokens_grad, sums_there, result_got, result)
+    )
+    tokens_got = swap_chip(tokens_grad[local:].astype(LOW)).astype(F32)
     vector_sums = (sums + sums_there)[:, : vector_sums.size].reshape(vector_sums.shape)
     vector_mine = scatter_dp(vector_sums[:, None], size, F32)[0]
     vector_out = [vector_mine[k * shard : (k + 1) * shard] for k in range(6)]
@@ -507,14 +528,14 @@
         up_ga.reshape(shard, size, 1, deep // 2), up_gb.reshape(shard, size, 1, deep // 2), 2
     ).reshape(shard, wide)
 
-    def hand_back(values, wire):
-        kept = values[:local]
-        got = swap_chip(values[local:].astype(wire)).astype(F32)
-        return jnp.where(chip == 1, jnp.stack([got, kept]), jnp.stack([kept, got]))
+    def hand_back(kept, got):
+        return row_major(
+            jnp.where(on_chip_one, jnp.stack([got, kept]), jnp.stack([kept, got]))
+        )
 
     return (
-        hand_back(result, F32),
-        hand_back(tokens_grad, LOW),
+        hand_back(result[:local], result_got),
+        hand_back(tokens_grad[:local], tokens_got),
         time_grad,
         vector_out[0],
         vector_out[1],

time: 568 us -> 502 us (0.88)
  waiting for transfers between devices: 159 us -> 106 us
  local copies, waits for them, and re-layouts: 69.4 us -> 52.8 us
  other arithmetic: 64 us -> 72.3 us
    ppermute x8 -> x7, waiting for transfers between devices: 51.4 us -> 12.2 us  [swap_chip(): return lax.ppermute(values, 'seq', CHIP_SWAP)]
    dynamic_slice x6 -> x0, local copies, waits for them, and re-layouts: 16.5 us -> none  [the longest x2 6.77 us: layer(): cot_mine = lax.dynamic_index_in_dim(cotangent, chip, 0, False)]
    reduce_scatter x1, waiting for transfers between devices: 19.2 us -> 7.42 us  [layer(): shards = lax.psum_scatter(summed, 'dp', scatter_dimension=0, tiled=False)]
    ppermute x18, waiting for transfers between devices: 87.9 us -> 79.1 us  [swap_bit(): return lax.ppermute(values, 'dp', [(i, i ^ bit) for i in range(size)])]
    unnamed x119 -> x145, local copies, waits for them, and re-layouts: 17.8 us -> 10 us
    ppermute x10 -> x11, waiting for transfers between devices: 0.03 us -> 5.98 us  [swap_core(): return lax.ppermute(values, 'seq', CORE_SWAP)]
  transfers between devices with their start and end apart: 38 -> 38, of which waited for: 19 -> 20; matrix products, arithmetic and copies ran while one was open for 26% -> 30% of each run, Pallas kernels for 22% -> 25%
where the time goes in v1:
time: 502 us; the launch traced here: 493 us
  Pallas kernels  123 us (25%)
  waiting for transfers between devices  106 us (21%)
  matrix products  85.4 us (17%)
  other arithmetic  72.3 us (14%)
  local copies, waits for them, and re-layouts  52.8 us (11%)
  starting transfers between devices  37.7 us (8%)
  between operations  15.9 us (3%)
    ppermute x18, waiting for transfers between devices, swap_bit(): return lax.ppermute(values, 'dp', [(i, i ^ bit) for i in range(size)])  79.1 us
    pallas_call x1, Pallas kernels, attention_backward(): pl.pallas_call(functools.partial(attention_backward_kernel, chunk=min(chu...  73.7 us
    dot_general x17, matrix products, dot32(): lax.dot_general(left, right, dims, preferred_element_type=jnp.float32)  58.1 us
    pallas_call x2, Pallas kernels, attention_forward(): pl.pallas_call(functools.partial(attention_forward_kernel, chunk=min(chun...  49.7 us
    ppermute x18, starting transfers between devices, swap_bit(): return lax.ppermute(values, 'dp', [(i, i ^ bit) for i in range(size)])  25.9 us
    ppermute x7, waiting for transfers between devices, swap_chip(): return lax.ppermute(values, 'seq', CHIP_SWAP)  12.2 us
    unnamed x145, local copies, waits for them, and re-layouts  10 us
  transfers between devices with their start and end apart: 38, of which 20 were waited for; matrix products, arithmetic and copies ran while one was open for 30% of the time, Pallas kernels for 25%

profile of v1, /device:TPU:0, one launch (start us, length us, event | category | flops | bytes accessed | tf_op | source)
XLA Modules:
  0.0 493.4 jit_solution(10426330454008118384)
XLA Ops:
  14.9 4.1 collective-permute-start.1
  18.9 3.2 dynamic-slice_bitcast_fusion.3
  22.2 1.8 collective-permute-start
  24.0 2.2 convert_element_type.173
  26.1 2.9 reshape.612
  29.0 3.2 dynamic-slice_reduce_fusion
  38.3 8.5 %collective-permute-done.9 = bf16[2,96,1152]{2,1,0:T(8,128)(2,1)S(1)} collective-permute-done((bf16[2,96,1152]{2,1,0:T(8,128)(2,1)S(1)}, bf16[2,96,1152]{2,1,0:T(8,128)(2,1)S(1)}, u32[]{:S(2)}, u32[]{:S(2)}) %collective-permute-start.9) | collective-permute-done | bytes 442400 | tf_op jit(solution)/shard_map/ppermute | solution.py:191
  48.8 2.1 collective-permute-done.2
  52.6 2.2 collective-permute-done.3
  57.1 2.3 collective-permute-done.4
  61.6 2.0 collective-permute-done.5
  63.6 2.3 collective-permute-start.6
  66.2 2.6 collective-permute-done.6
  68.8 1.9 collective-permute-start.10
  72.4 2.0 multiply_reduce_fusion.5
  74.4 3.2 add_convert_fusion.2
  81.1 3.8 collective-permute-done.10
  87.9 8.9 %convolution_convert_fusion.q_ref.k_ref.v_ref = bf16[2048,1152]{1,0:T(8,128)(2,1)} fusion(bf16[768,1152]{1,0:T(8,128)(2,1)S(1)} %bitcast.346, bf16[1024,768]{1,0:T(8,128)(2,1)S(1)} %collective-permute-done.7, bf16[1024,768]{1,0:T(8,128)(2,1)} %add_convert_fusion.2), kind=kOutput, calls=%fused_computation.3 | convolution fusion | flops 3632529408 | bytes 9633792 | tf_op jit(solution)/shard_map/dot_general | solution.py:371
  99.6 32.3 %attention_forward.2 = (bf16[2048,256]{1,0:T(8,128)(2,1)}, f32[2,128,2048]{2,1,0:T(8,128)}, f32[2,2,2048]{2,1,0:T(2,128)}) custom-call(f32[2048,1]{1,0:T(8,128)} %broadcast_select_fusion.2.bias_ref, bf16[2048,1152]{1,0:T(8,128)(2,1)} %convolution_convert_fusion.q_ref.k_ref.v_ref, bf16[2048,1152]{1,0:T(8,128)(2,1)} %convolution_convert_fusion.q_ref.k_ref.v_ref, ...), custom_call_target="tpu_custom_call" | custom-call | flops 17179869184 | bytes 8388608 | tf_op jit(solution)/shard_map/attention_forward/pallas_call | solution.py:115
  135.8 5.0 %slice.403 = bf16[8,384,768]{2,1,0:T(8,128)(2,1)} slice(bf16[8,432,768]{2,1,0:T(8,128)(2,1)} %bitcast.324), slice={[0:8], [0:384], [0:768]} | slice | bytes 9437184 | tf_op jit(solution)/shard_map/slice | solution.py:379
  142.4 17.4 %attention_forward.3 = (bf16[2048,128]{1,0:T(8,128)(2,1)}, f32[1,128,2048]{2,1,0:T(8,128)}, f32[1,2,2048]{2,1,0:T(2,128)}) custom-call(f32[2048,1]{1,0:T(8,128)} %broadcast_select_fusion.2.bias_ref, bf16[2048,1152]{1,0:T(8,128)(2,1)} %convolution_convert_fusion.q_ref.k_ref.v_ref, bf16[2048,1152]{1,0:T(8,128)(2,1)} %convolution_convert_fusion.q_ref.k_ref.v_ref, ...), custom_call_target="tpu_custom_call" | custom-call | flops 8589934592 | bytes 4194304 | tf_op jit(solution)/shard_map/attention_forward/pallas_call | solution.py:115
  159.8 1.8 fusion.97
  162.9 2.0 slice.397
  165.6 2.7 collective-permute-done.13
  169.1 3.4 fusion.118
  173.6 5.4 %multiply_convert_fusion.1 = (bf16[1024,1536]{1,0:T(8,128)(2,1)}, f32[1024,1536]{1,0:T(8,128)S(1)}) fusion(f32[1536]{0:T(1024)S(1)} %add.301, bf16[1024,768]{1,0:T(8,128)(2,1)S(1)} %add_convert_fusion.1, bf16[768,768]{1,0:T(8,128)(2,1)S(1)} %bitcast.351, bf16[768,768]{1,0:T(8,128)(2,1)S(1)} %bitcast.349), kind=kOutput, calls=%fused_computation.15 | convolution fusion | flops 2430074880 | bytes 13375488 | tf_op jit(solution)/shard_map/dot_general | solution.py:404
  179.0 5.4 %multiply_convert_fusion.3 = bf16[1024,1536]{1,0:T(8,128)(2,1)S(1)} fusion(bf16[1024,768]{1,0:T(8,128)(2,1)S(1)} %copy-done.15, bf16[1536,768]{1,0:T(8,128)(2,1)S(1)} %bitcast.340, f32[1024,1536]{1,0:T(8,128)S(1)} %get-tuple-element.198, f32[1536]{0:T(1024)S(1)} %add.301), kind=kOutput, calls=%fused_computation.18 | convolution fusion | flops 2436366336 | bytes 13375488 | tf_op jit(solution)/shard_map/dot_general | solution.py:18
  184.6 2.9 multiply_convert_fusion
  187.5 3.0 convolution_convert_fusion.1
  190.6 5.4 %multiply_convert_fusion.2 = bf16[1024,1536]{1,0:T(8,128)(2,1)S(1)} fusion(bf16[1024,768]{1,0:T(8,128)(2,1)S(1)} %copy-done.15, bf16[1536,768]{1,0:T(8,128)(2,1)S(1)} %bitcast.342, f32[1024,1536]{1,0:T(8,128)S(1)} %get-tuple-element.196, f32[1536]{0:T(1024)S(1)} %add.307), kind=kOutput, calls=%fused_computation.16 | convolution fusion | flops 2436366336 | bytes 13375488 | tf_op jit(solution)/shard_map/dot_general | solution.py:18
  196.1 2.6 fusion.24
  198.7 3.2 convolution_convert_fusion.2
  202.0 3.2 multiply_reduce_fusion.7
  205.2 3.5 fusion.96
  208.7 2.7 fusion.92
  212.6 4.4 maximum_maximum_fusion
  217.9 4.1 pad_maximum_fusion.1.mixed_ref
  222.0 3.4 convolution_convert_fusion.3
  225.4 2.6 fusion.119
  231.3 2.6 add_select_fusion
  237.5 2.9 convolution_convert_fusion.4
  241.9 7.2 %add_convert_fusion = bf16[8,432,768]{2,1,0:T(8,128)(2,1)} fusion(bf16[8,432,768]{2,1,0:T(8,128)(2,1)} %collective-permute-done.17, bf16[8,48,384]{2,1,0:T(8,128)(2,1)S(1)} %get-tuple-element.145, bf16[8,48,384]{2,1,0:T(8,128)(2,1)S(1)} %get-tuple-element.144, bf16[8,192,768]{2,1,0:T(8,128)(2,1)S(1)} %bitcast.344, bf16[8,96,768]{2,1,0:T(8,128)(2,1)S(1)} %bitcast.335, ...), kind=kLoop, calls=%fused_computation | loop fusion | flops 34504704 | bytes 15925248 | tf_op jit(solution)/shard_map/convert_element_type | solution.py:446
  249.2 73.7 %attention_backward.1 = (bf16[2048,384]{1,0:T(8,128)(2,1)}, bf16[2048,384]{1,0:T(8,128)(2,1)}, bf16[2048,384]{1,0:T(8,128)(2,1)}) custom-call(f32[2048,1]{1,0:T(8,128)} %broadcast_select_fusion.2.bias_ref, bf16[2048,1152]{1,0:T(8,128)(2,1)} %convolution_convert_fusion.q_ref.k_ref.v_ref, bf16[2048,1152]{1,0:T(8,128)(2,1)} %convolution_convert_fusion.q_ref.k_ref.v_ref, ...), custom_call_target="tpu_custom_call" | custom-call | flops 64424509440 | bytes 12582912 | tf_op jit(solution)/shard_map/attention_backward/pallas_call | solution.py:146
  326.2 7.0 %fusion.15 = f32[768,1152]{1,0:T(8,128)S(1)} fusion(bf16[2048,1152]{1,0:T(8,128)(2,1)S(1)} %constant_dynamic-update-slice_fusion, bf16[1024,768]{1,0:T(8,128)(2,1)S(1)} %copy-done.64, bf16[1024,768]{1,0:T(8,128)(2,1)} %add_convert_fusion.2), kind=kOutput, calls=%fused_computation.55 | convolution fusion | flops 3630170112 | bytes 11403264 | tf_op jit(solution)/shard_map/dot_general | solution.py:18
  333.3 1.9 copy-done.11
  336.7 3.4 fusion.20
  340.3 1.9 convolution_reduce_fusion.3
  342.2 2.4 convolution_reduce_fusion.1
  345.3 20.3 %collective-permute-done.29 = bf16[4,96,1152]{2,1,0:T(8,128)(2,1)} collective-permute-done((bf16[4,96,1152]{2,1,0:T(8,128)(2,1)}, bf16[4,96,1152]{2,1,0:T(8,128)(2,1)}, u32[]{:S(2)}, u32[]{:S(2)}) %collective-permute-start.29) | collective-permute-done | bytes 884768 | tf_op jit(solution)/shard_map/ppermute | solution.py:191
  369.2 2.6 convolution_reduce_fusion
  372.0 29.8 %collective-permute-done.30 = bf16[2,96,1152]{2,1,0:T(8,128)(2,1)} collective-permute-done((bf16[2,96,1152]{2,1,0:T(8,128)(2,1)}, bf16[2,96,1152]{2,1,0:T(8,128)(2,1)}, u32[]{:S(2)}, u32[]{:S(2)}) %collective-permute-start.30) | collective-permute-done | bytes 442400 | tf_op jit(solution)/shard_map/ppermute | solution.py:191
  404.4 7.3 %multiply_reduce_fusion.1 = (f32[768]{0:T(1024)S(1)}, f32[1024]{0:T(1024)S(1)}, f32[1024]{0:T(1024)S(1)}, f32[768]{0:T(1024)S(1)}, f32[1024,768]{1,0:T(8,128)}) fusion(f32[1024]{0:T(1024)S(1)} %copy-done.58, f32[1024]{0:T(1024)S(1)} %copy-done.54, f32[768]{0:T(1024)S(1)} %copy-done.52, f32[512,768]{1,0:T(8,128)} %collective-permute-done, ...), kind=kOutput, calls=%fused_computation.33 | convolution fusion | flops 1822159360 | bytes 12021760 | tf_op jit(solution)/shard_map/dot_general | solution.py:18
  412.0 5.6 %fusion.95 = (f32[768]{0:T(1024)S(1)}, f32[1024,768]{1,0:T(8,128)}) fusion(f32[1024,768]{1,0:T(8,128)} %get-tuple-element.103, f32[1024]{0:T(1024)S(1)} %get-tuple-element.202, f32[1024]{0:T(1024)S(1)} %copy-done.54, f32[768]{0:T(1024)S(1)} %copy-done.52, f32[512,768]{1,0:T(8,128)} %collective-permute-done, f32[512,768]{1,0:T(8,128)S(1)} %copy-done.4, ...), kind=kLoop, calls=%fused_computation.259 | loop fusion | flops 8649984 | bytes 12608512 | tf_op jit(solution)/shard_map/reduce_sum | solution.py:494
  422.9 2.7 collective-permute-start.23
  426.4 1.8 slice.656
  431.3 4.2 maximum_select_fusion.1
  435.6 2.1 collective-permute-start.27
  437.7 2.7 collective-permute-done.24
  443.6 2.2 collective-permute-done.28
  450.6 7.4 %reduce-scatter.2.cloned.1.call-done = bf16[1,432,768]{2,1,0:T(8,128)(2,1)} async-done(((bf16[8,432,768]{2,1,0:T(8,128)(2,1)}), bf16[1,432,768]{2,1,0:T(8,128)(2,1)}) %reduce-scatter.2.cloned.1.call-update) | async-done | bytes 663568 | tf_op jit(solution)/shard_map/reduce_scatter | solution.py:448
  461.7 1.9 maximum_select_fusion.2
  463.6 11.1 %collective-permute-done.34 = bf16[432,768]{1,0:T(8,128)(2,1)S(1)} collective-permute-done((bf16[432,768]{1,0:T(8,128)(2,1)}, bf16[432,768]{1,0:T(8,128)(2,1)S(1)}, u32[]{:S(2)}, u32[]{:S(2)}) %collective-permute-start.34) | collective-permute-done | bytes 663584 | tf_op jit(solution)/shard_map/ppermute | solution.py:187
  480.6 2.6 select_n.662
  483.2 2.4 maximum_select_fusion.6
  (371 shorter events, 92.5 us)
Async XLA Ops:
  7.2 27.3 %copy-start = (f32[384,768]{1,0:T(8,128)S(1)}, f32[384,768]{1,0:T(8,128)}, u32[]{:S(2)}) copy-start(f32[384,768]{1,0:T(8,128)} %param.29) | copy-start | bytes 3538948
  7.2 127.5 %all-gather.3.cloned.1.call-start = ((), (), s32[]{:S(2)}) async-start(), calls=%async_computation.2 | async-start | bytes 5971968 | tf_op jit(solution)/shard_map/all_gather | solution.py:326
  14.9 32.3 %collective-permute-start.1 = (f32[1,1,962]{2,1,0:T(1,128)S(1)}, f32[1,1,962]{2,1,0:T(1,128)S(1)}, u32[]{:S(2)}, u32[]{:S(2)}) collective-permute-start(f32[1,1,962]{2,1,0:T(1,128)S(1)} %bitcast.376), channel_id=1, source_target_pairs={{0,16},{4,20},{8,24},{12,28},{16,0},{20,4},{24,8},{28,12},{1,17},{... | collective-permute-start | bytes 11552 | tf_op jit(solution)/shard_map/ppermute | solution.py:191
  18.9 15.7 %collective-permute-start.8 = (bf16[1,96,1152]{2,1,0:T(8,128)(2,1)}, bf16[1,96,1152]{2,1,0:T(8,128)(2,1)}, u32[]{:S(2)}, u32[]{:S(2)}) collective-permute-start(bf16[1,96,1152]{2,1,0:T(8,128)(2,1)} %bitcast.30), channel_id=1, source_target_pairs={{0,16},{4,20},{8,24},{12,28},{16,0},{20,4},{24,8},{28,12},{1,17},{... | collective-permute-start | bytes 663560 | tf_op jit(solution)/shard_map/ppermute | solution.py:191
  22.2 52.2 %copy-start.2 = (f32[512,768]{1,0:T(8,128)}, f32[512,768]{1,0:T(8,128)S(1)}, u32[]{:S(2)}) copy-start(f32[512,768]{1,0:T(8,128)S(1)} %get-tuple-element.112) | copy-start | bytes 4718596
  22.2 48.5 %collective-permute-start = (f32[512,768]{1,0:T(8,128)}, f32[512,768]{1,0:T(8,128)}, u32[]{:S(2)}, u32[]{:S(2)}) collective-permute-start(f32[512,768]{1,0:T(8,128)} %get-tuple-element.113), channel_id=1, source_target_pairs={{0,2},{2,0},{1,3},{3,1},{4,6},{6,4},{5,7},{7,5},{8,10},{10,8},{9,1... | collective-permute-start | bytes 4718600 | tf_op jit(solution)/shard_map/ppermute | solution.py:187
  35.7 11.1 %collective-permute-start.9 = (bf16[2,96,1152]{2,1,0:T(8,128)(2,1)S(1)}, bf16[2,96,1152]{2,1,0:T(8,128)(2,1)S(1)}, u32[]{:S(2)}, u32[]{:S(2)}) collective-permute-start(bf16[2,96,1152]{2,1,0:T(8,128)(2,1)S(1)} %maximum_bitcast_fusion), channel_id=1, source_target_pairs={{0,8},{4,12},{8,0},{12,4},{16,24},{20,28},{24,16},{28,20},{1,9},{5... | collective-permute-start | bytes 1327112 | tf_op jit(solution)/shard_map/ppermute | solution.py:191
  37.4 17.9 %copy-start.47 = (f32[96,768]{1,0:T(8,128)S(1)}, f32[96,768]{1,0:T(8,128)}, u32[]{:S(2)}) copy-start(f32[96,768]{1,0:T(8,128)} %param.19) | copy-start | bytes 884740
  37.4 23.6 %copy-start.67 = (s32[2]{0:T(128)S(1)}, s32[2]{0:T(128)}, u32[]{:S(2)}) copy-start(s32[2]{0:T(128)} %param.18) | copy-start | bytes 28
  47.1 410.9 %reduce-scatter.2.cloned.1.call-start = ((), (), s32[]{:S(2)}) async-start(), calls=%async_computation.1 | async-start | bytes 5971968 | tf_op jit(solution)/shard_map/reduce_scatter | solution.py:448
  47.2 3.7 collective-permute-start.2
  51.0 3.8 collective-permute-start.3
  55.5 3.9 collective-permute-start.4
  59.4 4.1 collective-permute-start.5
  63.6 5.2 %collective-permute-start.6 = (f32[1,1,768]{2,1,0:T(1,128)S(1)}, f32[1,1,768]{2,1,0:T(1,128)S(1)}, u32[]{:S(2)}, u32[]{:S(2)}) collective-permute-start(f32[1,1,768]{2,1,0:T(1,128)S(1)} %fusion.75), channel_id=1, source_target_pairs={{0,16},{4,20},{8,24},{12,28},{16,0},{20,4},{24,8},{28,12},{1,17},{... | collective-permute-start | bytes 9224 | tf_op jit(solution)/shard_map/ppermute | solution.py:191
  66.1 8.3 %copy-start.55 = (f32[768]{0:T(1024)}, f32[768]{0:T(1024)S(1)}, u32[]{:S(2)}) copy-start(f32[768]{0:T(1024)S(1)} %mul.198) | copy-start | bytes 9220
  68.8 100.3 %copy-start.51 = (f32[768]{0:T(1024)}, f32[768]{0:T(1024)S(1)}, u32[]{:S(2)}) copy-start(f32[768]{0:T(1024)S(1)} %fusion.74) | copy-start | bytes 9220
  68.8 16.2 %collective-permute-start.10 = (bf16[4,96,1152]{2,1,0:T(8,128)(2,1)S(1)}, bf16[4,96,1152]{2,1,0:T(8,128)(2,1)}, u32[]{:S(2)}, u32[]{:S(2)}) collective-permute-start(bf16[4,96,1152]{2,1,0:T(8,128)(2,1)S(1)} %bitcast.336), channel_id=1, source_target_pairs={{0,4},{4,0},{8,12},{12,8},{16,20},{20,16},{24,28},{28,24},{1,5},{5... | collective-permute-start | bytes 2654216 | tf_op jit(solution)/shard_map/ppermute | solution.py:191
  77.7 9.0 %collective-permute-start.7 = (bf16[1024,768]{1,0:T(8,128)(2,1)}, bf16[1024,768]{1,0:T(8,128)(2,1)S(1)}, u32[]{:S(2)}, u32[]{:S(2)}) collective-permute-start(bf16[1024,768]{1,0:T(8,128)(2,1)} %add_convert_fusion.2), channel_id=1, source_target_pairs={{0,1},{1,0},{2,3},{3,2},{4,5},{5,4},{6,7},{7,6},{8,9},{9,8},{10,11... | collective-permute-start | bytes 4718600 | tf_op jit(solution)/shard_map/ppermute | solution.py:183
  86.6 10.1 %copy-start.31 = (bf16[4,2,96,1152]{3,2,1,0:T(8,128)(2,1)}, bf16[4,2,96,1152]{3,2,1,0:T(8,128)(2,1)S(1)}, u32[]{:S(2)}) copy-start(bf16[4,2,96,1152]{3,2,1,0:T(8,128)(2,1)S(1)} %copy.191) | copy-start | bytes 5308420
  87.9 8.9 %copy-start.25 = (f32[2,512,768]{2,1,0:T(8,128)S(1)}, f32[2,512,768]{2,1,0:T(8,128)}, u32[]{:S(2)}) copy-start(f32[2,512,768]{2,1,0:T(8,128)} %param.31) | copy-start | bytes 9437188
  98.1 33.8 %copy-start.5 = (f32[512,768]{1,0:T(8,128)}, f32[512,768]{1,0:T(8,128)S(1)}, u32[]{:S(2)}) copy-start(f32[512,768]{1,0:T(8,128)S(1)} %get-tuple-element.110) | copy-start | bytes 4718596
  98.1 33.8 %collective-permute-start.11 = (f32[512,768]{1,0:T(8,128)}, f32[512,768]{1,0:T(8,128)S(1)}, u32[]{:S(2)}, u32[]{:S(2)}) collective-permute-start(f32[512,768]{1,0:T(8,128)} %get-tuple-element.111), channel_id=1, source_target_pairs={{0,2},{2,0},{1,3},{3,1},{4,6},{6,4},{5,7},{7,5},{8,10},{10,8},{9,1... | collective-permute-start | bytes 4718600 | tf_op jit(solution)/shard_map/ppermute | solution.py:187
  131.9 8.9 %copy-start.13 = (f32[512,768]{1,0:T(8,128)}, f32[512,768]{1,0:T(8,128)S(1)}, u32[]{:S(2)}) copy-start(f32[512,768]{1,0:T(8,128)S(1)} %collective-permute-done.11) | copy-start | bytes 4718596
  141.8 26.5 %collective-permute-start.12 = (bf16[1024,256]{1,0:T(8,128)(2,1)}, bf16[1024,256]{1,0:T(8,128)(2,1)S(1)}, u32[]{:S(2)}, u32[]{:S(2)}) collective-permute-start(bf16[1024,256]{1,0:T(8,128)(2,1)} %get-tuple-element.130), channel_id=1, source_target_pairs={{0,1},{1,0},{2,3},{3,2},{4,5},{5,4},{6,7},{7,6},{8,9},{9,8},{10,11... | collective-permute-start | bytes 1572872 | tf_op jit(solution)/shard_map/ppermute | solution.py:183
  141.8 23.6 %collective-permute-start.14 = (bf16[8,48,768]{2,1,0:T(8,128)(2,1)S(1)}, bf16[8,48,768]{2,1,0:T(8,128)(2,1)S(1)}, u32[]{:S(2)}, u32[]{:S(2)}) collective-permute-start(bf16[8,48,768]{2,1,0:T(8,128)(2,1)S(1)} %slice.391), channel_id=1, source_target_pairs={{0,1},{1,0},{2,3},{3,2},{4,5},{5,4},{6,7},{7,6},{8,9},{9,8},{10,11... | collective-permute-start | bytes 1769480 | tf_op jit(solution)/shard_map/ppermute | solution.py:183
  159.8 24.7 %collective-permute-start.15 = (bf16[8,384,768]{2,1,0:T(8,128)(2,1)}, bf16[8,384,768]{2,1,0:T(8,128)(2,1)S(1)}, u32[]{:S(2)}, u32[]{:S(2)}) collective-permute-start(bf16[8,384,768]{2,1,0:T(8,128)(2,1)} %slice.403), channel_id=1, source_target_pairs={{0,1},{1,0},{2,3},{3,2},{4,5},{5,4},{6,7},{7,6},{8,9},{9,8},{10,11... | collective-permute-start | bytes 14155784 | tf_op jit(solution)/shard_map/ppermute | solution.py:183
  164.9 14.2 %copy-start.27 = (bf16[8,192,768]{2,1,0:T(8,128)(2,1)}, bf16[8,192,768]{2,1,0:T(8,128)(2,1)S(1)}, u32[]{:S(2)}) copy-start(bf16[8,192,768]{2,1,0:T(8,128)(2,1)S(1)} %slice.397) | copy-start | bytes 7077892
  164.9 3.4 collective-permute-start.13
  173.6 25.1 %copy-start.36 = (bf16[1024,768]{1,0:T(8,128)(2,1)}, bf16[1024,768]{1,0:T(8,128)(2,1)S(1)}, u32[]{:S(2)}) copy-start(bf16[1024,768]{1,0:T(8,128)(2,1)S(1)} %add_convert_fusion.1) | copy-start | bytes 4718596
  184.4 11.7 %copy-start.22 = (bf16[1024,1536]{1,0:T(8,128)(2,1)}, bf16[1024,1536]{1,0:T(8,128)(2,1)S(1)}, u32[]{:S(2)}) copy-start(bf16[1024,1536]{1,0:T(8,128)(2,1)S(1)} %multiply_convert_fusion.3) | copy-start | bytes 9437188
  217.0 24.9 %collective-permute-start.17 = (bf16[8,432,768]{2,1,0:T(8,128)(2,1)}, bf16[8,432,768]{2,1,0:T(8,128)(2,1)}, u32[]{:S(2)}, u32[]{:S(2)}) collective-permute-start(bf16[8,432,768]{2,1,0:T(8,128)(2,1)} %maximum_maximum_fusion), channel_id=1, source_target_pairs={{0,1},{1,0},{2,3},{3,2},{4,5},{5,4},{6,7},{7,6},{8,9},{9,8},{10,11... | collective-permute-start | bytes 15925256 | tf_op jit(solution)/shard_map/ppermute | solution.py:183
  229.7 10.9 %collective-permute-start.16 = (bf16[1024,384]{1,0:T(8,128)(2,1)S(1)}, bf16[1024,384]{1,0:T(8,128)(2,1)S(1)}, u32[]{:S(2)}, u32[]{:S(2)}) collective-permute-start(bf16[1024,384]{1,0:T(8,128)(2,1)S(1)} %get-tuple-element.121), channel_id=1, source_target_pairs={{0,1},{1,0},{2,3},{3,2},{4,5},{5,4},{6,7},{7,6},{8,9},{9,8},{10,11... | collective-permute-start | bytes 2359304 | tf_op jit(solution)/shard_map/ppermute | solution.py:183
  235.2 186.5 %collective-permute-start.21 = (f32[512,768]{1,0:T(8,128)}, f32[512,768]{1,0:T(8,128)}, u32[]{:S(2)}, u32[]{:S(2)}) collective-permute-start(f32[512,768]{1,0:T(8,128)} %slice.522), channel_id=1, source_target_pairs={{0,2},{2,0},{1,3},{3,1},{4,6},{6,4},{5,7},{7,5},{8,10},{10,8},{9,1... | collective-permute-start | bytes 4718600 | tf_op jit(solution)/shard_map/ppermute | solution.py:187
  326.2 10.5 %copy-start.44 = (bf16[2048,1152]{1,0:T(8,128)(2,1)}, bf16[2048,1152]{1,0:T(8,128)(2,1)S(1)}, u32[]{:S(2)}) copy-start(bf16[2048,1152]{1,0:T(8,128)(2,1)S(1)} %constant_dynamic-update-slice_fusion) | copy-start | bytes 14155780
  326.2 10.5 %copy-start.32 = (bf16[4,2,96,1152]{3,2,1,0:T(8,128)(2,1)S(1)}, bf16[4,2,96,1152]{3,2,1,0:T(8,128)(2,1)}, u32[]{:S(2)}) copy-start(bf16[4,2,96,1152]{3,2,1,0:T(8,128)(2,1)} %copy-done.31) | copy-start | bytes 5308420
  336.2 29.4 %collective-permute-start.29 = (bf16[4,96,1152]{2,1,0:T(8,128)(2,1)}, bf16[4,96,1152]{2,1,0:T(8,128)(2,1)}, u32[]{:S(2)}, u32[]{:S(2)}) collective-permute-start(bf16[4,96,1152]{2,1,0:T(8,128)(2,1)} %fusion.26), channel_id=1, source_target_pairs={{0,4},{4,0},{8,12},{12,8},{16,20},{20,16},{24,28},{28,24},{1,5},{5... | collective-permute-start | bytes 2654216 | tf_op jit(solution)/shard_map/ppermute | solution.py:191
  340.1 64.2 %collective-permute-start.18 = (bf16[1024,768]{1,0:T(8,128)(2,1)}, bf16[1024,768]{1,0:T(8,128)(2,1)}, u32[]{:S(2)}, u32[]{:S(2)}) collective-permute-start(bf16[1024,768]{1,0:T(8,128)(2,1)} %fusion.20), channel_id=1, source_target_pairs={{0,1},{1,0},{2,3},{3,2},{4,5},{5,4},{6,7},{7,6},{8,9},{9,8},{10,11... | collective-permute-start | bytes 4718600 | tf_op jit(solution)/shard_map/ppermute | solution.py:183
  344.7 20.9 %copy-start.12 = (f32[768,1152]{1,0:T(8,128)S(1)}, f32[768,1152]{1,0:T(8,128)}, u32[]{:S(2)}) copy-start(f32[768,1152]{1,0:T(8,128)} %copy-done.11) | copy-start | bytes 10616836
  345.3 23.2 %copy-start.17 = (bf16[1024,768]{1,0:T(8,128)(2,1)S(1)}, bf16[1024,768]{1,0:T(8,128)(2,1)}, u32[]{:S(2)}) copy-start(bf16[1024,768]{1,0:T(8,128)(2,1)} %fusion.10) | copy-start | bytes 4718596
  367.8 34.0 %collective-permute-start.30 = (bf16[2,96,1152]{2,1,0:T(8,128)(2,1)}, bf16[2,96,1152]{2,1,0:T(8,128)(2,1)}, u32[]{:S(2)}, u32[]{:S(2)}) collective-permute-start(bf16[2,96,1152]{2,1,0:T(8,128)(2,1)} %fusion.30), channel_id=1, source_target_pairs={{0,8},{4,12},{8,0},{12,4},{16,24},{20,28},{24,16},{28,20},{1,9},{5... | collective-permute-start | bytes 1327112 | tf_op jit(solution)/shard_map/ppermute | solution.py:191
  369.2 35.1 %copy-start.4 = (f32[512,768]{1,0:T(8,128)S(1)}, f32[512,768]{1,0:T(8,128)}, u32[]{:S(2)}) copy-start(f32[512,768]{1,0:T(8,128)} %copy-done.2) | copy-start | bytes 4718596
  369.2 35.1 %copy-start.52 = (f32[768]{0:T(1024)S(1)}, f32[768]{0:T(1024)}, u32[]{:S(2)}) copy-start(f32[768]{0:T(1024)} %copy-done.51) | copy-start | bytes 9220
  369.2 35.1 %copy-start.54 = (f32[1024]{0:T(1024)S(1)}, f32[1024]{0:T(1024)}, u32[]{:S(2)}) copy-start(f32[1024]{0:T(1024)} %copy-done.53) | copy-start | bytes 12292
  369.2 35.1 %copy-start.56 = (f32[768]{0:T(1024)S(1)}, f32[768]{0:T(1024)}, u32[]{:S(2)}) copy-start(f32[768]{0:T(1024)} %copy-done.55) | copy-start | bytes 9220
  369.2 35.1 %copy-start.58 = (f32[1024]{0:T(1024)S(1)}, f32[1024]{0:T(1024)}, u32[]{:S(2)}) copy-start(f32[1024]{0:T(1024)} %copy-done.57) | copy-start | bytes 12292
  372.0 32.4 %copy-start.33 = (bf16[4,2,96,1152]{3,2,1,0:T(8,128)(2,1)S(1)}, bf16[4,2,96,1152]{3,2,1,0:T(8,128)(2,1)}, u32[]{:S(2)}) copy-start(bf16[4,2,96,1152]{3,2,1,0:T(8,128)(2,1)} %copy-done.31) | copy-start | bytes 5308420
  403.9 16.1 %collective-permute-start.31 = (bf16[1,96,1152]{2,1,0:T(8,128)(2,1)S(1)}, bf16[1,96,1152]{2,1,0:T(8,128)(2,1)S(1)}, u32[]{:S(2)}, u32[]{:S(2)}) collective-permute-start(bf16[1,96,1152]{2,1,0:T(8,128)(2,1)S(1)} %fusion.32), channel_id=1, source_target_pairs={{0,16},{4,20},{8,24},{12,28},{16,0},{20,4},{24,8},{28,12},{1,17},{... | collective-permute-start | bytes 663560 | tf_op jit(solution)/shard_map/ppermute | solution.py:191
  412.0 8.0 %copy-start.10 = (f32[1,2,96,1152]{3,2,1,0:T(8,128)S(1)}, f32[1,2,96,1152]{3,2,1,0:T(8,128)}, u32[]{:S(2)}) copy-start(f32[1,2,96,1152]{3,2,1,0:T(8,128)} %copy-done.9) | copy-start | bytes 2654212
  417.6 1.2 collective-permute-start.19
  418.9 4.0 collective-permute-start.20
  420.7 26.8 %collective-permute-start.32 = (bf16[96,1152]{1,0:T(8,128)(2,1)}, bf16[96,1152]{1,0:T(8,128)(2,1)}, u32[]{:S(2)}, u32[]{:S(2)}) collective-permute-start(bf16[96,1152]{1,0:T(8,128)(2,1)} %bitcast_convert_fusion.1), channel_id=1, source_target_pairs={{0,2},{2,0},{1,3},{3,1},{4,6},{6,4},{5,7},{7,5},{8,10},{10,8},{9,1... | collective-permute-start | bytes 663560 | tf_op jit(solution)/shard_map/ppermute | solution.py:187
  422.9 12.6 %collective-permute-start.23 = (f32[1,2,768]{2,1,0:T(2,128)S(1)}, f32[1,2,768]{2,1,0:T(2,128)S(1)}, u32[]{:S(2)}, u32[]{:S(2)}) collective-permute-start(f32[1,2,768]{2,1,0:T(2,128)S(1)} %fusion.64), channel_id=1, source_target_pairs={{0,16},{4,20},{8,24},{12,28},{16,0},{20,4},{24,8},{28,12},{1,17},{... | collective-permute-start | bytes 18440 | tf_op jit(solution)/shard_map/ppermute | solution.py:191
  425.8 9.8 %collective-permute-start.26 = (f32[4,1,960]{2,1,0:T(1,128)S(1)}, f32[4,1,960]{2,1,0:T(1,128)S(1)}, u32[]{:S(2)}, u32[]{:S(2)}) collective-permute-start(f32[4,1,960]{2,1,0:T(1,128)S(1)} %fusion.52), channel_id=1, source_target_pairs={{0,4},{4,0},{8,12},{12,8},{16,20},{20,16},{24,28},{28,24},{1,5},{5... | collective-permute-start | bytes 46088 | tf_op jit(solution)/shard_map/ppermute | solution.py:191
  428.2 32.3 %collective-permute-start.22 = (bf16[512,768]{1,0:T(8,128)(2,1)S(1)}, bf16[512,768]{1,0:T(8,128)(2,1)}, u32[]{:S(2)}, u32[]{:S(2)}) collective-permute-start(bf16[512,768]{1,0:T(8,128)(2,1)S(1)} %slice.656), channel_id=1, source_target_pairs={{0,2},{2,0},{1,3},{3,1},{4,6},{6,4},{5,7},{7,5},{8,10},{10,8},{9,1... | collective-permute-start | bytes 2359304 | tf_op jit(solution)/shard_map/ppermute | solution.py:187
  431.3 16.0 %copy-start.61 = (bf16[8,2,96]{2,0,1:T(8,128)(2,1)S(1)}, bf16[8,2,96]{2,0,1:T(8,128)(2,1)}, u32[]{:S(2)}) copy-start(bf16[8,2,96]{2,0,1:T(8,128)(2,1)} %copy-done.60) | copy-start | bytes 9220
  435.5 4.9 collective-permute-start.24
  435.6 5.3 %collective-permute-start.27 = (f32[2,1,960]{2,1,0:T(1,128)S(1)}, f32[2,1,960]{2,1,0:T(1,128)S(1)}, u32[]{:S(2)}, u32[]{:S(2)}) collective-permute-start(f32[2,1,960]{2,1,0:T(1,128)S(1)} %fusion.59), channel_id=1, source_target_pairs={{0,8},{4,12},{8,0},{12,4},{16,24},{20,28},{24,16},{28,20},{1,9},{5... | collective-permute-start | bytes 23048 | tf_op jit(solution)/shard_map/ppermute | solution.py:191
  441.0 4.9 collective-permute-start.28
  442.4 4.7 collective-permute-start.25
  448.6 1.9 collective-permute-start.33
  458.0 16.6 %collective-permute-start.34 = (bf16[432,768]{1,0:T(8,128)(2,1)}, bf16[432,768]{1,0:T(8,128)(2,1)S(1)}, u32[]{:S(2)}, u32[]{:S(2)}) collective-permute-start(bf16[432,768]{1,0:T(8,128)(2,1)} %bitcast.357), channel_id=1, source_target_pairs={{0,2},{2,0},{1,3},{3,1},{4,6},{6,4},{5,7},{7,5},{8,10},{10,8},{9,1... | collective-permute-start | bytes 1990664 | tf_op jit(solution)/shard_map/ppermute | solution.py:187
  461.7 12.9 %copy-start.39 = (bf16[1,432,768]{2,1,0:T(8,128)(2,1)S(1)}, bf16[1,432,768]{2,1,0:T(8,128)(2,1)}, u32[]{:S(2)}) copy-start(bf16[1,432,768]{2,1,0:T(8,128)(2,1)} %reduce-scatter.2.cloned.1.call-done) | copy-start | bytes 1990660
  476.5 2.3 collective-permute-start.35
  (45 other events, 169.6 us)
Sparse Core Ops, SparseCore 0:
  47.2 87.4 all-gather.2
  340.2 117.7 reduce-scatter.1

commit v2 on v1

--- a/solution.py
+++ b/solution.py
@@ -205,12 +205,14 @@
 
 def gather_dp(values, size):
     held = values[None]
-    for bit in reversed(bits_of(size)):
-        held = gather_step(held, size, bit)
+    for bit in bits_of(size):
+        upper = (lax.axis_index("dp") & bit) != 0
+        got = swap_bit(held, size, bit)
+        held = jnp.concatenate([jnp.where(upper, got, held), jnp.where(upper, held, got)], axis=0)
     return held
 
 
-def scatter_dp(values, size, wire):
+def scatter_dp(values, size, wire, gate=()):
     me = lax.axis_index("dp")
     held = values
     for bit in bits_of(size):
@@ -218,9 +220,11 @@
         halves = held.reshape((held.shape[0] // 2, 2) + held.shape[1:])
         send = jnp.where(upper, halves[:, 0], halves[:, 1]).astype(wire)
         keep = jnp.where(upper, halves[:, 1], halves[:, 0])
+        if bit == 1 and gate:
+            send, *gate = lax.optimization_barrier((send, *gate))
         got = swap_bit(send, size, bit)
         held = keep + got.astype(F32)
-    return held[0]
+    return (held[0], *gate) if gate else held[0]
 
 
 def row_major(values):
@@ -304,23 +308,31 @@
         )
     )
 
-    up_pairs = up_weight.astype(LOW).reshape(shard, size, 2, deep // 2)
-    up_shard = lax.dynamic_index_in_dim(up_pairs, core, 2, False).reshape(shard, wide // 2)
-    down_shard = take_half(down_weight.astype(LOW), core, 0)
-    out_shard = take_half(out_weight.astype(LOW), core, 1)
-    packed = jnp.concatenate(
-        [
-            up_shard[:, :width],
-            up_shard[:, width:],
-            down_shard,
-            jnp.concatenate([out_shard[: shard // 2], out_shard[shard // 2 :]], axis=1),
-        ],
-        axis=0,
-    )
+    def pack_weights(up_weight, down_weight, out_weight):
+        up_pairs = up_weight.astype(LOW).reshape(shard, size, 2, deep // 2)
+        up_shard = lax.dynamic_index_in_dim(up_pairs, core, 2, False).reshape(shard, wide // 2)
+        down_shard = take_half(down_weight.astype(LOW), core, 0)
+        out_shard = take_half(out_weight.astype(LOW), core, 1)
+        return jnp.concatenate(
+            [
+                up_shard[:, :width],
+                up_shard[:, width:],
+                down_shard,
+                jnp.concatenate([out_shard[: shard // 2], out_shard[shard // 2 :]], axis=1),
+            ],
+            axis=0,
+        )
+
     held = qkv_shard[None]
     for bit in reversed(bits_of(size)):
+        if bit == 2:
+            held, up_weight, down_weight, out_weight = lax.optimization_barrier(
+                (held, up_weight, down_weight, out_weight)
+            )
         if bit == 1:
-            held, packed = lax.optimization_barrier((held, packed))
+            held, packed = lax.optimization_barrier(
+                (held, pack_weights(up_weight, down_weight, out_weight))
+            )
         held = gather_step(held, size, bit)
     qkv_own = held.reshape(width, 3 * half)
     own_pack = lax.all_gather(packed, "dp", axis=0, tiled=False)
@@ -376,7 +388,7 @@
     mixed_one, own_pack, projected_late = lax.optimization_barrier((mixed_one, own_pack, projected))
     rest = 2 * shard + deep // 2
     other_out = swap_core(own_pack[:, rest:])
-    other_pack = swap_core(own_pack[:, :rest])
+    other_pack = swap_core(own_pack)
     sent_one = swap_core(mixed_one[count:])
     mixed_two, wide_two, logs_two = attention_forward(projected_late, bias, lead, 1)
     attended = natural(
@@ -384,8 +396,6 @@
         jnp.concatenate([sent_one, swap_core(mixed_two[count:])], axis=1),
         1,
     )
-    wide_mixed = jnp.concatenate([wide_one, wide_two], axis=0)
-    logs = jnp.concatenate([logs_one, logs_two], axis=0)
 
     cot_mine = lax.dynamic_index_in_dim(cotangent, chip, 0, False)
     cot_send = lax.dynamic_index_in_dim(cotangent, 1 - chip, 0, False)
@@ -446,17 +456,45 @@
     summed = (grads_a.astype(F32) + swap_core(grads_b).astype(F32)).astype(LOW)
     grad_heads, summed = lax.optimization_barrier((grad_heads, summed))
     shards = lax.psum_scatter(summed, "dp", scatter_dimension=0, tiled=False)
-    dq, dk, dv = attention_backward(projected, wide_mixed, grad_heads, logs, bias, 0)
-    grad_projected = jnp.concatenate([dq, dk, dv], axis=1)
-    part_other = swap_core(dot32(grad_projected[count:], qkv_own, NT).astype(LOW))
-    qkv_grad = rows_dot(normed_all, grad_projected).reshape(size, shard, 3 * half)
-    (
-        qkv_grad, grad_projected, pre_a, pre_b, grad_branch, grad_low, grad_normed_two,
-    ) = lax.optimization_barrier(
-        (qkv_grad, grad_projected, pre_a, pre_b, grad_branch, grad_low, grad_normed_two)
-    )
-    qkv_mine = scatter_dp(qkv_grad, size, LOW)
-    qkv_mine = qkv_mine + swap_chip(qkv_mine.astype(LOW)).astype(F32)
+    cut = lead * PAIR
+    grad_a = jnp.concatenate(
+        attention_backward(projected, wide_one, grad_heads, logs_one, bias, 0), axis=1
+    )
+    qkv_a = rows_dot(normed_all, grad_a).reshape(size, 2, shard // 2, 3 * cut)
+    qkv_keep = jnp.where(on_chip_one, qkv_a[:, 1], qkv_a[:, 0])
+    qkv_send = jnp.where(on_chip_one, qkv_a[:, 0], qkv_a[:, 1]).astype(LOW)
+    qkv_got = swap_chip(qkv_send)
+    grad_b = jnp.concatenate(
+        attention_backward(projected, wide_two, grad_heads, logs_two, bias, lead), axis=1
+    )
+    columns = [qkv_own[:, k * half : (k + 1) * half] for k in range(3)]
+    weight_a = jnp.concatenate([part[:, :cut] for part in columns], axis=1)
+    weight_b = jnp.concatenate([part[:, cut:] for part in columns], axis=1)
+    part_other = dot32(grad_a[count:], weight_a, NT) + dot32(grad_b[count:], weight_b, NT)
+    part_other = swap_core(part_other.astype(LOW))
+    qkv_b = rows_dot(normed_all, grad_b).reshape(size, shard, 3 * (half - cut))
+    qkv_b, grad_a, grad_b, pre_a, pre_b, grad_branch, grad_low, grad_normed_two = scatter_dp(
+        qkv_b, size, LOW, (grad_a, grad_b, pre_a, pre_b, grad_branch, grad_low, grad_normed_two)
+    )
+    qkv_a = scatter_dp(qkv_keep + qkv_got.astype(F32), size, LOW)
+    qkv_more = swap_chip(qkv_a)
+    qkv_a = jnp.where(
+        on_chip_one,
+        jnp.concatenate([qkv_more, qkv_a], axis=0),
+        jnp.concatenate([qkv_a, qkv_more], axis=0),
+    )
+    qkv_b = qkv_b + swap_chip(qkv_b.astype(LOW)).astype(F32)
+    qkv_mine = jnp.concatenate(
+        [
+            piece
+            for k in range(3)
+            for piece in (
+                qkv_a[:, k * cut : (k + 1) * cut],
+                qkv_b[:, k * (half - cut) : (k + 1) * (half - cut)],
+            )
+        ],
+        axis=1,
+    )
     qkv_other = swap_core(qkv_mine)
     qkv_out = jnp.concatenate(
         [
@@ -468,7 +506,7 @@
         axis=1,
     )
 
-    part_own = dot32(grad_projected[:count], qkv_own, NT)
+    part_own = dot32(grad_a[:count], weight_a, NT) + dot32(grad_b[:count], weight_b, NT)
     grad_normed_one = row_major(part_own + part_other.astype(F32))
     tokens_grad = row_major(
         grad_middle + norm_pull(grad_normed_one, xhat_a, rate_a, gain_a)
@@ -495,9 +533,7 @@
     sums = jnp.concatenate([vector_sums.reshape(1, -1), token_sum], axis=1)
     sums = sums + swap_core(sums)
     sums_there = swap_chip(sums)
-    tokens_grad, sums_there, result_got, result = lax.optimization_barrier(
-        (tokens_grad, sums_there, result_got, result)
-    )
+    sums_there, result_got, result = lax.optimization_barrier((sums_there, result_got, result))
     tokens_got = swap_chip(tokens_grad[local:].astype(LOW)).astype(F32)
     vector_sums = (sums + sums_there)[:, : vector_sums.size].reshape(vector_sums.shape)
     vector_mine = scatter_dp(vector_sums[:, None], size, F32)[0]

time: 502 us -> 473 us (0.942)
  waiting for transfers between devices: 106 us -> 53.1 us
  local copies, waits for them, and re-layouts: 52.8 us -> 74.3 us
  starting transfers between devices: 37.7 us -> 44.4 us
    ppermute x18 -> x21, waiting for transfers between devices: 79.1 us -> 35.1 us  [swap_bit(): return lax.ppermute(values, 'dp', [(i, i ^ bit) for i in range(size)])]
    reduce_scatter x1, waiting for transfers between devices: 7.42 us -> 0.02 us  [layer(): shards = lax.psum_scatter(summed, 'dp', scatter_dimension=0, tiled=False)]
    ppermute x18 -> x21, starting transfers between devices: 25.9 us -> 32.5 us  [swap_bit(): return lax.ppermute(values, 'dp', [(i, i ^ bit) for i in range(size)])]
    unnamed x145 -> x185, local copies, waits for them, and re-layouts: 10 us -> 15.9 us
    ppermute x7 -> x9, waiting for transfers between devices: 12.2 us -> 15.6 us  [swap_chip(): return lax.ppermute(values, 'seq', CHIP_SWAP)]
    pallas_call x1 -> x2, Pallas kernels: 73.7 us -> 76.9 us  [attention_backward(): pl.pallas_call(functools.partial(attention_backward_kernel, chunk=min(chu...]
    dot_general x17 -> x20, matrix products: 58.1 us -> 55.4 us  [dot32(): lax.dot_general(left, right, dims, preferred_element_type=jnp.float32)]
  transfers between devices with their start and end apart: 38 -> 43, of which waited for: 20 -> 21; matrix products, arithmetic and copies ran while one was open for 30% -> 33% of each run, Pallas kernels for 25% -> 27%
where the time goes in v2:
time: 473 us; the launch traced here: 464 us
  Pallas kernels  127 us (27%)
  matrix products  82.2 us (17%)
  local copies, waits for them, and re-layouts  74.3 us (16%)
  other arithmetic  67.5 us (14%)
  waiting for transfers between devices  53.1 us (11%)
  starting transfers between devices  44.4 us (9%)
  between operations  16.1 us (3%)
    pallas_call x2, Pallas kernels, attention_backward(): pl.pallas_call(functools.partial(attention_backward_kernel, chunk=min(chu...  76.9 us
    dot_general x20, matrix products, dot32(): lax.dot_general(left, right, dims, preferred_element_type=jnp.float32)  55.4 us
    pallas_call x2, Pallas kernels, attention_forward(): pl.pallas_call(functools.partial(attention_forward_kernel, chunk=min(chun...  49.7 us
    ppermute x21, waiting for transfers between devices, swap_bit(): return lax.ppermute(values, 'dp', [(i, i ^ bit) for i in range(size)])  35.1 us
    ppermute x21, starting transfers between devices, swap_bit(): return lax.ppermute(values, 'dp', [(i, i ^ bit) for i in range(size)])  32.5 us
    unnamed x185, local copies, waits for them, and re-layouts  15.9 us
    ppermute x9, waiting for transfers between devices, swap_chip(): return lax.ppermute(values, 'seq', CHIP_SWAP)  15.6 us
    ppermute x9, starting transfers between devices, swap_chip(): return lax.ppermute(values, 'seq', CHIP_SWAP)  9.51 us
  transfers between devices with their start and end apart: 43, of which 21 were waited for; matrix products, arithmetic and copies ran while one was open for 33% of the time, Pallas kernels for 27%

profile of v2, /device:TPU:0, one launch (start us, length us, event | category | flops | bytes accessed | tf_op | source)
XLA Modules:
  0.0 464.2 jit_solution(8258855433164213602)
XLA Ops:
  14.2 3.1 collective-permute-start.1
  17.2 2.6 collective-permute-start.8
  19.8 3.2 dynamic-slice_bitcast_fusion.3
  24.6 5.2 %collective-permute-done.8 = bf16[1,96,1152]{2,1,0:T(8,128)(2,1)S(1)} collective-permute-done((bf16[1,96,1152]{2,1,0:T(8,128)(2,1)S(1)}, bf16[1,96,1152]{2,1,0:T(8,128)(2,1)S(1)}, u32[]{:S(2)}, u32[]{:S(2)}) %collective-permute-start.8) | collective-permute-done | bytes 221216 | tf_op jit(solution)/shard_map/ppermute | solution.py:191
  32.9 2.2 convert_element_type.217
  35.0 2.9 reshape.665
  37.9 3.2 dynamic-slice_reduce_fusion
  47.1 2.3 collective-permute-done.2
  49.5 3.4 collective-permute-start.3
  55.9 3.5 collective-permute-done.4
  61.0 2.5 collective-permute-done.5
  63.5 2.9 collective-permute-start.6
  71.2 2.0 multiply_reduce_fusion.5
  73.2 3.2 add_convert_fusion.3
  79.9 6.1 %collective-permute-done.10 = bf16[4,96,1152]{2,1,0:T(8,128)(2,1)} collective-permute-done((bf16[4,96,1152]{2,1,0:T(8,128)(2,1)S(1)}, bf16[4,96,1152]{2,1,0:T(8,128)(2,1)}, u32[]{:S(2)}, u32[]{:S(2)}) %collective-permute-start.10) | collective-permute-done | bytes 884768 | tf_op jit(solution)/shard_map/ppermute | solution.py:191
  88.9 8.4 %convolution_convert_fusion.q_ref.k_ref.v_ref = bf16[2048,1152]{1,0:T(8,128)(2,1)} fusion(bf16[768,1152]{1,0:T(8,128)(2,1)S(1)} %bitcast.351, bf16[1024,768]{1,0:T(8,128)(2,1)S(1)} %collective-permute-done.7, bf16[1024,768]{1,0:T(8,128)(2,1)} %add_convert_fusion.3), kind=kOutput, calls=%fused_computation.3 | convolution fusion | flops 3632529408 | bytes 9633792 | tf_op jit(solution)/shard_map/dot_general | solution.py:383
  100.1 32.3 %attention_forward.2 = (bf16[2048,256]{1,0:T(8,128)(2,1)}, f32[2,128,2048]{2,1,0:T(8,128)}, f32[2,2,2048]{2,1,0:T(2,128)}) custom-call(f32[2048,1]{1,0:T(8,128)} %broadcast_select_fusion.2.bias_ref, bf16[2048,1152]{1,0:T(8,128)(2,1)} %convolution_convert_fusion.q_ref.k_ref.v_ref, bf16[2048,1152]{1,0:T(8,128)(2,1)} %convolution_convert_fusion.q_ref.k_ref.v_ref, ...), custom_call_target="tpu_custom_call" | custom-call | flops 17179869184 | bytes 8388608 | tf_op jit(solution)/shard_map/attention_forward/pallas_call | solution.py:115
  134.2 2.0 slice.468
  136.2 3.2 fusion.102
  140.8 17.4 %attention_forward.3 = (bf16[2048,128]{1,0:T(8,128)(2,1)}, f32[1,128,2048]{2,1,0:T(8,128)}, f32[1,2,2048]{2,1,0:T(2,128)}) custom-call(f32[2048,1]{1,0:T(8,128)} %broadcast_select_fusion.2.bias_ref, bf16[2048,1152]{1,0:T(8,128)(2,1)} %convolution_convert_fusion.q_ref.k_ref.v_ref, bf16[2048,1152]{1,0:T(8,128)(2,1)} %convolution_convert_fusion.q_ref.k_ref.v_ref, ...), custom_call_target="tpu_custom_call" | custom-call | flops 8589934592 | bytes 4194304 | tf_op jit(solution)/shard_map/attention_forward/pallas_call | solution.py:115
  160.4 2.0 slice.474
  165.0 3.4 fusion.124
  170.7 5.3 %multiply_convert_fusion.1 = (bf16[1024,1536]{1,0:T(8,128)(2,1)}, f32[1024,1536]{1,0:T(8,128)S(1)}) fusion(f32[1536]{0:T(1024)S(1)} %add.319, bf16[1024,768]{1,0:T(8,128)(2,1)S(1)} %add_convert_fusion.2, bf16[768,768]{1,0:T(8,128)(2,1)S(1)} %bitcast.376, bf16[768,768]{1,0:T(8,128)(2,1)S(1)} %bitcast.374), kind=kOutput, calls=%fused_computation.15 | convolution fusion | flops 2430074880 | bytes 13375488 | tf_op jit(solution)/shard_map/dot_general | solution.py:414
  176.1 5.4 %multiply_convert_fusion.3 = bf16[1024,1536]{1,0:T(8,128)(2,1)S(1)} fusion(bf16[1024,768]{1,0:T(8,128)(2,1)S(1)} %copy-done.13, bf16[1536,768]{1,0:T(8,128)(2,1)S(1)} %bitcast.368, f32[1024,1536]{1,0:T(8,128)S(1)} %get-tuple-element.223, f32[1536]{0:T(1024)S(1)} %add.319), kind=kOutput, calls=%fused_computation.18 | convolution fusion | flops 2436366336 | bytes 13375488 | tf_op jit(solution)/shard_map/dot_general | solution.py:18
  181.5 2.9 fusion.101
  184.4 2.9 multiply_convert_fusion
  187.4 3.0 convolution_convert_fusion.1
  190.3 1.8 slice.600
  192.2 5.4 %multiply_convert_fusion.2 = bf16[1024,1536]{1,0:T(8,128)(2,1)S(1)} fusion(bf16[1024,768]{1,0:T(8,128)(2,1)S(1)} %copy-done.13, bf16[1536,768]{1,0:T(8,128)(2,1)S(1)} %bitcast.370, f32[1024,1536]{1,0:T(8,128)S(1)} %get-tuple-element.221, f32[1536]{0:T(1024)S(1)} %add.325), kind=kOutput, calls=%fused_computation.16 | convolution fusion | flops 2436366336 | bytes 13375488 | tf_op jit(solution)/shard_map/dot_general | solution.py:18
  197.6 2.6 fusion.16
  200.3 3.4 convolution_convert_fusion.2
  203.7 3.2 multiply_reduce_fusion.7
  206.9 3.6 fusion.100
  210.6 2.7 fusion.96
  214.5 4.6 maximum_maximum_fusion
  219.6 2.1 fusion.106
  221.7 2.3 fusion.107
  224.0 4.7 %convolution_convert_fusion.3 = bf16[1536,768]{1,0:T(8,128)(2,1)S(1)} fusion(bf16[1024,1536]{1,0:T(8,128)(2,1)} %get-tuple-element.222, bf16[1024,768]{1,0:T(8,128)(2,1)S(1)} %copy-done.14), kind=kOutput, calls=%fused_computation.23 | convolution fusion | flops 2417098752 | bytes 7077888 | tf_op jit(solution)/shard_map/dot_general | solution.py:18
  228.8 2.6 fusion.125
  234.6 2.6 add_select_fusion
  240.9 2.9 convolution_convert_fusion.4
  245.3 7.3 %add_convert_fusion = bf16[8,432,768]{2,1,0:T(8,128)(2,1)} fusion(bf16[8,432,768]{2,1,0:T(8,128)(2,1)} %collective-permute-done.17, bf16[8,48,384]{2,1,0:T(8,128)(2,1)S(1)} %get-tuple-element.165, bf16[8,48,384]{2,1,0:T(8,128)(2,1)S(1)} %get-tuple-element.164, bf16[8,192,768]{2,1,0:T(8,128)(2,1)S(1)} %bitcast.372, bf16[8,96,768]{2,1,0:T(8,128)(2,1)S(1)} %bitcast.359, ...), kind=kLoop, calls=%fused_computation | loop fusion | flops 34504704 | bytes 15925248 | tf_op jit(solution)/shard_map/convert_element_type | solution.py:456
  252.6 26.5 %attention_backward.2 = (bf16[2048,128]{1,0:T(8,128)(2,1)}, bf16[2048,128]{1,0:T(8,128)(2,1)}, bf16[2048,128]{1,0:T(8,128)(2,1)}) custom-call(f32[2048,1]{1,0:T(8,128)} %broadcast_select_fusion.2.bias_ref, bf16[2048,1152]{1,0:T(8,128)(2,1)} %convolution_convert_fusion.q_ref.k_ref.v_ref, bf16[2048,1152]{1,0:T(8,128)(2,1)} %convolution_convert_fusion.q_ref.k_ref.v_ref, ...), custom_call_target="tpu_custom_call" | custom-call | flops 21474836480 | bytes 4194304 | tf_op jit(solution)/shard_map/attention_backward/pallas_call | solution.py:146
  282.7 3.9 fusion.19
  288.4 50.5 %attention_backward.3 = (bf16[2048,256]{1,0:T(8,128)(2,1)}, bf16[2048,256]{1,0:T(8,128)(2,1)}, bf16[2048,256]{1,0:T(8,128)(2,1)}) custom-call(f32[2048,1]{1,0:T(8,128)} %broadcast_select_fusion.2.bias_ref, bf16[2048,1152]{1,0:T(8,128)(2,1)} %convolution_convert_fusion.q_ref.k_ref.v_ref, bf16[2048,1152]{1,0:T(8,128)(2,1)} %convolution_convert_fusion.q_ref.k_ref.v_ref, ...), custom_call_target="tpu_custom_call" | custom-call | flops 42949672960 | bytes 8388608 | tf_op jit(solution)/shard_map/attention_backward/pallas_call | solution.py:146
  346.9 4.1 fusion.18
  353.9 3.1 fusion.13
  357.0 2.2 add_convert_fusion.1
  361.9 1.9 bitcast_add_fusion.1
  373.1 3.5 collective-permute-done.30
  377.5 2.4 collective-permute-start.36
  379.9 2.1 collective-permute-done.31
  382.1 2.9 collective-permute-start.32
  390.0 3.4 collective-permute-done.33
  395.7 3.0 multiply_reduce_fusion
  398.7 3.0 fusion.99
  407.7 1.8 collective-permute-start.22
  413.5 3.9 maximum_select_fusion.1
  417.7 2.0 collective-permute-start.27
  421.5 2.7 collective-permute-start.28
  434.3 1.9 maximum_select_fusion.2
  436.2 9.3 %collective-permute-done.39 = bf16[432,768]{1,0:T(8,128)(2,1)S(1)} collective-permute-done((bf16[432,768]{1,0:T(8,128)(2,1)}, bf16[432,768]{1,0:T(8,128)(2,1)S(1)}, u32[]{:S(2)}, u32[]{:S(2)}) %collective-permute-start.39) | collective-permute-done | bytes 663584 | tf_op jit(solution)/shard_map/ppermute | solution.py:187
  451.4 2.6 select_n.766
  454.1 2.4 maximum_select_fusion.6
  (432 shorter events, 120.8 us)
Async XLA Ops:
  7.2 35.3 %copy-start = (f32[384,768]{1,0:T(8,128)S(1)}, f32[384,768]{1,0:T(8,128)}, u32[]{:S(2)}) copy-start(f32[384,768]{1,0:T(8,128)} %param.29) | copy-start | bytes 3538948
  7.2 127.0 %all-gather.3.cloned.1.call-start = ((), (), s32[]{:S(2)}) async-start(), calls=%async_computation.2 | async-start | bytes 5971968 | tf_op jit(solution)/shard_map/all_gather | solution.py:338
  14.2 31.5 %collective-permute-start.1 = (f32[1,1,962]{2,1,0:T(1,128)S(1)}, f32[1,1,962]{2,1,0:T(1,128)S(1)}, u32[]{:S(2)}, u32[]{:S(2)}) collective-permute-start(f32[1,1,962]{2,1,0:T(1,128)S(1)} %bitcast.403), channel_id=1, source_target_pairs={{0,4},{4,0},{8,12},{12,8},{16,20},{20,16},{24,28},{28,24},{1,5},{5... | collective-permute-start | bytes 11552 | tf_op jit(solution)/shard_map/ppermute | solution.py:191
  17.2 12.5 %collective-permute-start.8 = (bf16[1,96,1152]{2,1,0:T(8,128)(2,1)S(1)}, bf16[1,96,1152]{2,1,0:T(8,128)(2,1)S(1)}, u32[]{:S(2)}, u32[]{:S(2)}) collective-permute-start(bf16[1,96,1152]{2,1,0:T(8,128)(2,1)S(1)} %bitcast.382), channel_id=1, source_target_pairs={{0,16},{4,20},{8,24},{12,28},{16,0},{20,4},{24,8},{28,12},{1,17},{... | collective-permute-start | bytes 663560 | tf_op jit(solution)/shard_map/ppermute | solution.py:191
  23.1 50.2 %copy-start.2 = (f32[512,768]{1,0:T(8,128)}, f32[512,768]{1,0:T(8,128)S(1)}, u32[]{:S(2)}) copy-start(f32[512,768]{1,0:T(8,128)S(1)} %get-tuple-element.126) | copy-start | bytes 4718596
  23.1 46.5 %collective-permute-start = (f32[512,768]{1,0:T(8,128)}, f32[512,768]{1,0:T(8,128)}, u32[]{:S(2)}, u32[]{:S(2)}) collective-permute-start(f32[512,768]{1,0:T(8,128)} %get-tuple-element.127), channel_id=1, source_target_pairs={{0,2},{2,0},{1,3},{3,1},{4,6},{6,4},{5,7},{7,5},{8,10},{10,8},{9,1... | collective-permute-start | bytes 4718600 | tf_op jit(solution)/shard_map/ppermute | solution.py:187
  32.2 12.1 %collective-permute-start.9 = (bf16[2,96,1152]{2,1,0:T(8,128)(2,1)}, bf16[2,96,1152]{2,1,0:T(8,128)(2,1)}, u32[]{:S(2)}, u32[]{:S(2)}) collective-permute-start(bf16[2,96,1152]{2,1,0:T(8,128)(2,1)} %maximum_bitcast_fusion), channel_id=1, source_target_pairs={{0,8},{4,12},{8,0},{12,4},{16,24},{20,28},{24,16},{28,20},{1,9},{5... | collective-permute-start | bytes 1327112 | tf_op jit(solution)/shard_map/ppermute | solution.py:191
  42.5 17.9 %copy-start.83 = (s32[2]{0:T(128)S(1)}, s32[2]{0:T(128)}, u32[]{:S(2)}) copy-start(s32[2]{0:T(128)} %param.18) | copy-start | bytes 28
  45.6 386.1 %reduce-scatter.2.cloned.1.call-start = ((), (), s32[]{:S(2)}) async-start(), calls=%async_computation.1 | async-start | bytes 5971968 | tf_op jit(solution)/shard_map/reduce_scatter | solution.py:458
  45.7 3.7 collective-permute-start.2
  49.5 5.2 %collective-permute-start.3 = (f32[4,1,962]{2,1,0:T(1,128)S(1)}, f32[4,1,962]{2,1,0:T(1,128)S(1)}, u32[]{:S(2)}, u32[]{:S(2)}) collective-permute-start(f32[4,1,962]{2,1,0:T(1,128)S(1)} %pad_maximum_fusion.28), channel_id=1, source_target_pairs={{0,16},{4,20},{8,24},{12,28},{16,0},{20,4},{24,8},{28,12},{1,17},{... | collective-permute-start | bytes 46184 | tf_op jit(solution)/shard_map/ppermute | solution.py:191
  55.1 18.0 %copy-start.73 = (bf16[8,2,96]{2,0,1:T(8,128)(2,1)}, bf16[8,2,96]{2,0,1:T(8,128)(2,1)S(1)}, u32[]{:S(2)}) copy-start(bf16[8,2,96]{2,0,1:T(8,128)(2,1)S(1)} %fusion.70) | copy-start | bytes 9220
  55.3 4.1 collective-permute-start.4
  59.5 4.0 collective-permute-start.5
  63.5 5.0 %collective-permute-start.6 = (f32[1,1,768]{2,1,0:T(1,128)S(1)}, f32[1,1,768]{2,1,0:T(1,128)S(1)}, u32[]{:S(2)}, u32[]{:S(2)}) collective-permute-start(f32[1,1,768]{2,1,0:T(1,128)S(1)} %fusion.74), channel_id=1, source_target_pairs={{0,16},{4,20},{8,24},{12,28},{16,0},{20,4},{24,8},{28,12},{1,17},{... | collective-permute-start | bytes 9224 | tf_op jit(solution)/shard_map/ppermute | solution.py:191
  68.5 96.4 %copy-start.64 = (f32[768]{0:T(1024)}, f32[768]{0:T(1024)S(1)}, u32[]{:S(2)}) copy-start(f32[768]{0:T(1024)S(1)} %fusion.73) | copy-start | bytes 9220
  68.5 17.5 %collective-permute-start.10 = (bf16[4,96,1152]{2,1,0:T(8,128)(2,1)S(1)}, bf16[4,96,1152]{2,1,0:T(8,128)(2,1)}, u32[]{:S(2)}, u32[]{:S(2)}) collective-permute-start(bf16[4,96,1152]{2,1,0:T(8,128)(2,1)S(1)} %bitcast.362), channel_id=1, source_target_pairs={{0,4},{4,0},{8,12},{12,8},{16,20},{20,16},{24,28},{28,24},{1,5},{5... | collective-permute-start | bytes 2654216 | tf_op jit(solution)/shard_map/ppermute | solution.py:191
  76.4 11.2 %collective-permute-start.7 = (bf16[1024,768]{1,0:T(8,128)(2,1)}, bf16[1024,768]{1,0:T(8,128)(2,1)S(1)}, u32[]{:S(2)}, u32[]{:S(2)}) collective-permute-start(bf16[1024,768]{1,0:T(8,128)(2,1)} %add_convert_fusion.3), channel_id=1, source_target_pairs={{0,1},{1,0},{2,3},{3,2},{4,5},{5,4},{6,7},{7,6},{8,9},{9,8},{10,11... | collective-permute-start | bytes 4718600 | tf_op jit(solution)/shard_map/ppermute | solution.py:183
  98.6 33.9 %copy-start.5 = (f32[512,768]{1,0:T(8,128)}, f32[512,768]{1,0:T(8,128)S(1)}, u32[]{:S(2)}) copy-start(f32[512,768]{1,0:T(8,128)S(1)} %get-tuple-element.124) | copy-start | bytes 4718596
  98.6 33.8 %collective-permute-start.11 = (f32[512,768]{1,0:T(8,128)}, f32[512,768]{1,0:T(8,128)S(1)}, u32[]{:S(2)}, u32[]{:S(2)}) collective-permute-start(f32[512,768]{1,0:T(8,128)} %get-tuple-element.125), channel_id=1, source_target_pairs={{0,2},{2,0},{1,3},{3,1},{4,6},{6,4},{5,7},{7,5},{8,10},{10,8},{9,1... | collective-permute-start | bytes 4718600 | tf_op jit(solution)/shard_map/ppermute | solution.py:187
  139.4 42.1 %collective-permute-start.15 = (bf16[8,432,768]{2,1,0:T(8,128)(2,1)}, bf16[8,432,768]{2,1,0:T(8,128)(2,1)}, u32[]{:S(2)}, u32[]{:S(2)}) collective-permute-start(bf16[8,432,768]{2,1,0:T(8,128)(2,1)} %bitcast.38), channel_id=1, source_target_pairs={{0,1},{1,0},{2,3},{3,2},{4,5},{5,4},{6,7},{7,6},{8,9},{9,8},{10,11... | collective-permute-start | bytes 15925256 | tf_op jit(solution)/shard_map/ppermute | solution.py:183
  139.4 23.7 %collective-permute-start.14 = (bf16[8,48,768]{2,1,0:T(8,128)(2,1)}, bf16[8,48,768]{2,1,0:T(8,128)(2,1)S(1)}, u32[]{:S(2)}, u32[]{:S(2)}) collective-permute-start(bf16[8,48,768]{2,1,0:T(8,128)(2,1)} %slice.468), channel_id=1, source_target_pairs={{0,1},{1,0},{2,3},{3,2},{4,5},{5,4},{6,7},{7,6},{8,9},{9,8},{10,11... | collective-permute-start | bytes 1769480 | tf_op jit(solution)/shard_map/ppermute | solution.py:183
  140.8 23.4 %collective-permute-start.12 = (bf16[1024,256]{1,0:T(8,128)(2,1)S(1)}, bf16[1024,256]{1,0:T(8,128)(2,1)S(1)}, u32[]{:S(2)}, u32[]{:S(2)}) collective-permute-start(bf16[1024,256]{1,0:T(8,128)(2,1)S(1)} %get-tuple-element.150), channel_id=1, source_target_pairs={{0,1},{1,0},{2,3},{3,2},{4,5},{5,4},{6,7},{7,6},{8,9},{9,8},{10,11... | collective-permute-start | bytes 1572872 | tf_op jit(solution)/shard_map/ppermute | solution.py:183
  162.4 1.7 collective-permute-start.13
  169.5 30.8 %copy-start.34 = (bf16[1024,768]{1,0:T(8,128)(2,1)}, bf16[1024,768]{1,0:T(8,128)(2,1)S(1)}, u32[]{:S(2)}) copy-start(bf16[1024,768]{1,0:T(8,128)(2,1)S(1)} %add_convert_fusion.2) | copy-start | bytes 4718596
  219.1 26.2 %collective-permute-start.17 = (bf16[8,432,768]{2,1,0:T(8,128)(2,1)}, bf16[8,432,768]{2,1,0:T(8,128)(2,1)}, u32[]{:S(2)}, u32[]{:S(2)}) collective-permute-start(bf16[8,432,768]{2,1,0:T(8,128)(2,1)} %maximum_maximum_fusion), channel_id=1, source_target_pairs={{0,1},{1,0},{2,3},{3,2},{4,5},{5,4},{6,7},{7,6},{8,9},{9,8},{10,11... | collective-permute-start | bytes 15925256 | tf_op jit(solution)/shard_map/ppermute | solution.py:183
  233.0 10.9 %collective-permute-start.16 = (bf16[1024,384]{1,0:T(8,128)(2,1)S(1)}, bf16[1024,384]{1,0:T(8,128)(2,1)S(1)}, u32[]{:S(2)}, u32[]{:S(2)}) collective-permute-start(bf16[1024,384]{1,0:T(8,128)(2,1)S(1)} %get-tuple-element.141), channel_id=1, source_target_pairs={{0,1},{1,0},{2,3},{3,2},{4,5},{5,4},{6,7},{7,6},{8,9},{9,8},{10,11... | collective-permute-start | bytes 2359304 | tf_op jit(solution)/shard_map/ppermute | solution.py:183
  238.6 171.0 %collective-permute-start.21 = (f32[512,768]{1,0:T(8,128)}, f32[512,768]{1,0:T(8,128)}, u32[]{:S(2)}, u32[]{:S(2)}) collective-permute-start(f32[512,768]{1,0:T(8,128)} %slice.626), channel_id=1, source_target_pairs={{0,2},{2,0},{1,3},{3,1},{4,6},{6,4},{5,7},{7,5},{8,10},{10,8},{9,1... | collective-permute-start | bytes 4718600 | tf_op jit(solution)/shard_map/ppermute | solution.py:187
  346.3 15.5 %collective-permute-start.34 = (bf16[4,96,384]{2,1,0:T(8,128)(2,1)}, bf16[4,96,384]{2,1,0:T(8,128)(2,1)}, u32[]{:S(2)}, u32[]{:S(2)}) collective-permute-start(bf16[4,96,384]{2,1,0:T(8,128)(2,1)} %fusion.26), channel_id=1, source_target_pairs={{0,4},{4,0},{8,12},{12,8},{16,20},{20,16},{24,28},{28,24},{1,5},{5... | collective-permute-start | bytes 884744 | tf_op jit(solution)/shard_map/ppermute | solution.py:191
  351.9 15.4 %collective-permute-start.29 = (bf16[8,48,768]{2,1,0:T(8,128)(2,1)}, bf16[8,48,768]{2,1,0:T(8,128)(2,1)}, u32[]{:S(2)}, u32[]{:S(2)}) collective-permute-start(bf16[8,48,768]{2,1,0:T(8,128)(2,1)} %fusion.22), channel_id=1, source_target_pairs={{0,2},{2,0},{1,3},{3,1},{4,6},{6,4},{5,7},{7,5},{8,10},{10,8},{9,1... | collective-permute-start | bytes 1769480 | tf_op jit(solution)/shard_map/ppermute | solution.py:187
  365.5 6.4 %collective-permute-start.35 = (bf16[2,96,384]{2,1,0:T(8,128)(2,1)}, bf16[2,96,384]{2,1,0:T(8,128)(2,1)}, u32[]{:S(2)}, u32[]{:S(2)}) collective-permute-start(bf16[2,96,384]{2,1,0:T(8,128)(2,1)} %fusion.33), channel_id=1, source_target_pairs={{0,8},{4,12},{8,0},{12,4},{16,24},{20,28},{24,16},{28,20},{1,9},{5... | collective-permute-start | bytes 442376 | tf_op jit(solution)/shard_map/ppermute | solution.py:191
  368.6 7.9 %collective-permute-start.30 = (bf16[4,48,768]{2,1,0:T(8,128)(2,1)S(1)}, bf16[4,48,768]{2,1,0:T(8,128)(2,1)S(1)}, u32[]{:S(2)}, u32[]{:S(2)}) collective-permute-start(bf16[4,48,768]{2,1,0:T(8,128)(2,1)S(1)} %fusion.27), channel_id=1, source_target_pairs={{0,4},{4,0},{8,12},{12,8},{16,20},{20,16},{24,28},{28,24},{1,5},{5... | collective-permute-start | bytes 884744 | tf_op jit(solution)/shard_map/ppermute | solution.py:191
  371.9 23.7 %collective-permute-start.18 = (bf16[1024,768]{1,0:T(8,128)(2,1)}, bf16[1024,768]{1,0:T(8,128)(2,1)S(1)}, u32[]{:S(2)}, u32[]{:S(2)}) collective-permute-start(bf16[1024,768]{1,0:T(8,128)(2,1)} %add_convert_fusion.1), channel_id=1, source_target_pairs={{0,1},{1,0},{2,3},{3,2},{4,5},{5,4},{6,7},{7,6},{8,9},{9,8},{10,11... | collective-permute-start | bytes 4718600 | tf_op jit(solution)/shard_map/ppermute | solution.py:183
  376.6 19.0 %copy-start.84 = (f32[1024,768]{1,0:T(8,128)S(1)}, f32[1024,768]{1,0:T(8,128)}, u32[]{:S(2)}) copy-start(f32[1024,768]{1,0:T(8,128)} %fusion.13) | copy-start | bytes 9437188
  376.6 18.9 %copy-start.4 = (f32[512,768]{1,0:T(8,128)S(1)}, f32[512,768]{1,0:T(8,128)}, u32[]{:S(2)}) copy-start(f32[512,768]{1,0:T(8,128)} %copy-done.2) | copy-start | bytes 4718596
  376.7 18.9 %copy-start.40 = (bf16[2048,384]{1,0:T(8,128)(2,1)S(1)}, bf16[2048,384]{1,0:T(8,128)(2,1)}, u32[]{:S(2)}) copy-start(bf16[2048,384]{1,0:T(8,128)(2,1)} %copy-done.38) | copy-start | bytes 4718596
  376.7 18.9 %copy-start.44 = (bf16[768,128]{1,0:T(8,128)(2,1)S(1)}, bf16[768,128]{1,0:T(8,128)(2,1)}, u32[]{:S(2)}) copy-start(bf16[768,128]{1,0:T(8,128)(2,1)} %get-tuple-element.132) | copy-start | bytes 589828
  376.7 18.9 %copy-start.46 = (bf16[768,128]{1,0:T(8,128)(2,1)S(1)}, bf16[768,128]{1,0:T(8,128)(2,1)}, u32[]{:S(2)}) copy-start(bf16[768,128]{1,0:T(8,128)(2,1)} %get-tuple-element.133) | copy-start | bytes 589828
  376.7 18.9 %copy-start.48 = (bf16[768,128]{1,0:T(8,128)(2,1)S(1)}, bf16[768,128]{1,0:T(8,128)(2,1)}, u32[]{:S(2)}) copy-start(bf16[768,128]{1,0:T(8,128)(2,1)} %get-tuple-element.134) | copy-start | bytes 589828
  376.7 18.9 %copy-start.65 = (f32[768]{0:T(1024)S(1)}, f32[768]{0:T(1024)}, u32[]{:S(2)}) copy-start(f32[768]{0:T(1024)} %copy-done.64) | copy-start | bytes 9220
  376.7 18.9 %copy-start.67 = (f32[1024]{0:T(1024)S(1)}, f32[1024]{0:T(1024)}, u32[]{:S(2)}) copy-start(f32[1024]{0:T(1024)} %copy-done.66) | copy-start | bytes 12292
  376.7 18.9 %copy-start.69 = (f32[768]{0:T(1024)S(1)}, f32[768]{0:T(1024)}, u32[]{:S(2)}) copy-start(f32[768]{0:T(1024)} %copy-done.68) | copy-start | bytes 9220
  376.7 18.9 %copy-start.71 = (f32[1024]{0:T(1024)S(1)}, f32[1024]{0:T(1024)}, u32[]{:S(2)}) copy-start(f32[1024]{0:T(1024)} %copy-done.70) | copy-start | bytes 12292
  376.8 5.2 %collective-permute-start.31 = (bf16[2,48,768]{2,1,0:T(8,128)(2,1)S(1)}, bf16[2,48,768]{2,1,0:T(8,128)(2,1)S(1)}, u32[]{:S(2)}, u32[]{:S(2)}) collective-permute-start(bf16[2,48,768]{2,1,0:T(8,128)(2,1)S(1)} %fusion.32), channel_id=1, source_target_pairs={{0,8},{4,12},{8,0},{12,4},{16,24},{20,28},{24,16},{28,20},{1,9},{5... | collective-permute-start | bytes 442376 | tf_op jit(solution)/shard_map/ppermute | solution.py:191
  377.5 7.5 %collective-permute-start.36 = (bf16[1,96,384]{2,1,0:T(8,128)(2,1)S(1)}, bf16[1,96,384]{2,1,0:T(8,128)(2,1)S(1)}, u32[]{:S(2)}, u32[]{:S(2)}) collective-permute-start(bf16[1,96,384]{2,1,0:T(8,128)(2,1)S(1)} %fusion.43), channel_id=1, source_target_pairs={{0,16},{4,20},{8,24},{12,28},{16,0},{20,4},{24,8},{28,12},{1,17},{... | collective-permute-start | bytes 221192 | tf_op jit(solution)/shard_map/ppermute | solution.py:191
  382.1 6.1 %collective-permute-start.32 = (bf16[1,48,768]{2,1,0:T(8,128)(2,1)S(1)}, bf16[1,48,768]{2,1,0:T(8,128)(2,1)S(1)}, u32[]{:S(2)}, u32[]{:S(2)}) collective-permute-start(bf16[1,48,768]{2,1,0:T(8,128)(2,1)S(1)} %fusion.42), channel_id=1, source_target_pairs={{0,16},{4,20},{8,24},{12,28},{16,0},{20,4},{24,8},{28,12},{1,17},{... | collective-permute-start | bytes 221192 | tf_op jit(solution)/shard_map/ppermute | solution.py:191
  385.0 4.9 %collective-permute-start.37 = (bf16[96,384]{1,0:T(8,128)(2,1)S(1)}, bf16[96,384]{1,0:T(8,128)(2,1)S(1)}, u32[]{:S(2)}, u32[]{:S(2)}) collective-permute-start(bf16[96,384]{1,0:T(8,128)(2,1)S(1)} %bitcast_convert_fusion.1), channel_id=1, source_target_pairs={{0,2},{2,0},{1,3},{3,1},{4,6},{6,4},{5,7},{7,5},{8,10},{10,8},{9,1... | collective-permute-start | bytes 221192 | tf_op jit(solution)/shard_map/ppermute | solution.py:187
  388.2 5.2 %collective-permute-start.33 = (f32[48,768]{1,0:T(8,128)S(1)}, f32[48,768]{1,0:T(8,128)S(1)}, u32[]{:S(2)}, u32[]{:S(2)}) collective-permute-start(f32[48,768]{1,0:T(8,128)S(1)} %fusion.34), channel_id=1, source_target_pairs={{0,2},{2,0},{1,3},{3,1},{4,6},{6,4},{5,7},{7,5},{8,10},{10,8},{9,1... | collective-permute-start | bytes 442376 | tf_op jit(solution)/shard_map/ppermute | solution.py:187
  404.0 1.2 collective-permute-start.19
  404.6 25.8 %collective-permute-start.38 = (f32[96,1152]{1,0:T(8,128)}, f32[96,1152]{1,0:T(8,128)}, u32[]{:S(2)}, u32[]{:S(2)}) collective-permute-start(f32[96,1152]{1,0:T(8,128)} %constant_dynamic-update-slice_fusion.8), channel_id=1, source_target_pairs={{0,1},{1,0},{2,3},{3,2},{4,5},{5,4},{6,7},{7,6},{8,9},{9,8},{10,11... | collective-permute-start | bytes 1327112 | tf_op jit(solution)/shard_map/ppermute | solution.py:183
  405.2 4.3 collective-permute-start.20
  407.7 26.4 %collective-permute-start.22 = (bf16[512,768]{1,0:T(8,128)(2,1)}, bf16[512,768]{1,0:T(8,128)(2,1)S(1)}, u32[]{:S(2)}, u32[]{:S(2)}) collective-permute-start(bf16[512,768]{1,0:T(8,128)(2,1)} %slice.832), channel_id=1, source_target_pairs={{0,2},{2,0},{1,3},{3,1},{4,6},{6,4},{5,7},{7,5},{8,10},{10,8},{9,1... | collective-permute-start | bytes 2359304 | tf_op jit(solution)/shard_map/ppermute | solution.py:187
  409.6 7.8 %collective-permute-start.23 = (f32[1,2,768]{2,1,0:T(2,128)S(1)}, f32[1,2,768]{2,1,0:T(2,128)S(1)}, u32[]{:S(2)}, u32[]{:S(2)}) collective-permute-start(f32[1,2,768]{2,1,0:T(2,128)S(1)} %fusion.65), channel_id=1, source_target_pairs={{0,4},{4,0},{8,12},{12,8},{16,20},{20,16},{24,28},{28,24},{1,5},{5... | collective-permute-start | bytes 18440 | tf_op jit(solution)/shard_map/ppermute | solution.py:191
  411.3 6.4 %collective-permute-start.26 = (f32[4,1,960]{2,1,0:T(1,128)S(1)}, f32[4,1,960]{2,1,0:T(1,128)S(1)}, u32[]{:S(2)}, u32[]{:S(2)}) collective-permute-start(f32[4,1,960]{2,1,0:T(1,128)S(1)} %fusion.55), channel_id=1, source_target_pairs={{0,4},{4,0},{8,12},{12,8},{16,20},{20,16},{24,28},{28,24},{1,5},{5... | collective-permute-start | bytes 46088 | tf_op jit(solution)/shard_map/ppermute | solution.py:191
  413.5 18.0 %copy-start.58 = (f32[96,256]{1,0:T(8,128)S(1)}, f32[96,256]{1,0:T(8,128)}, u32[]{:S(2)}) copy-start(f32[96,256]{1,0:T(8,128)} %get-tuple-element.179) | copy-start | bytes 294916
  413.5 18.0 %copy-start.63 = (f32[96,128]{1,0:T(8,128)S(1)}, f32[96,128]{1,0:T(8,128)}, u32[]{:S(2)}) copy-start(f32[96,128]{1,0:T(8,128)} %get-tuple-element.185) | copy-start | bytes 147460
  413.5 18.1 %copy-start.61 = (f32[96,128]{1,0:T(8,128)S(1)}, f32[96,128]{1,0:T(8,128)}, u32[]{:S(2)}) copy-start(f32[96,128]{1,0:T(8,128)} %get-tuple-element.183) | copy-start | bytes 147460
  413.5 18.1 %copy-start.62 = (f32[96,128]{1,0:T(8,128)S(1)}, f32[96,128]{1,0:T(8,128)}, u32[]{:S(2)}) copy-start(f32[96,128]{1,0:T(8,128)} %get-tuple-element.186) | copy-start | bytes 147460
  417.5 3.8 collective-permute-start.24
  417.7 3.7 collective-permute-start.27
  421.5 4.6 collective-permute-start.28
  424.2 4.8 %collective-permute-start.25 = (f32[4,2,768]{2,1,0:T(2,128)S(1)}, f32[4,2,768]{2,1,0:T(2,128)S(1)}, u32[]{:S(2)}, u32[]{:S(2)}) collective-permute-start(f32[4,2,768]{2,1,0:T(2,128)S(1)} %pad_maximum_fusion.27), channel_id=1, source_target_pairs={{0,16},{4,20},{8,24},{12,28},{16,0},{20,4},{24,8},{28,12},{1,17},{... | collective-permute-start | bytes 73736 | tf_op jit(solution)/shard_map/ppermute | solution.py:191
  431.7 13.8 %collective-permute-start.39 = (bf16[432,768]{1,0:T(8,128)(2,1)}, bf16[432,768]{1,0:T(8,128)(2,1)S(1)}, u32[]{:S(2)}, u32[]{:S(2)}) collective-permute-start(bf16[432,768]{1,0:T(8,128)(2,1)} %bitcast.383), channel_id=1, source_target_pairs={{0,2},{2,0},{1,3},{3,1},{4,6},{6,4},{5,7},{7,5},{8,10},{10,8},{9,1... | collective-permute-start | bytes 1990664 | tf_op jit(solution)/shard_map/ppermute | solution.py:187
  447.4 2.3 collective-permute-start.40
  (67 other events, 318.6 us)
Sparse Core Ops, SparseCore 0:
  45.7 87.4 all-gather.2
  252.7 102.7 reduce-scatter.1

commit v3 on v2

--- a/solution.py
+++ b/solution.py
@@ -212,19 +212,21 @@
     return held
 
 
-def scatter_dp(values, size, wire, gate=()):
-    me = lax.axis_index("dp")
+def scatter_step(held, size, bit, wire):
+    upper = (lax.axis_index("dp") & bit) != 0
+    halves = held.reshape((held.shape[0] // 2, 2) + held.shape[1:])
+    send = jnp.where(upper, halves[:, 0], halves[:, 1]).astype(wire)
+    keep = jnp.where(upper, halves[:, 1], halves[:, 0])
+    got = swap_bit(send, size, bit)
+    return keep, got
+
+
+def scatter_dp(values, size, wire, skip=0):
     held = values
-    for bit in bits_of(size):
-        upper = (me & bit) != 0
-        halves = held.reshape((held.shape[0] // 2, 2) + held.shape[1:])
-        send = jnp.where(upper, halves[:, 0], halves[:, 1]).astype(wire)
-        keep = jnp.where(upper, halves[:, 1], halves[:, 0])
-        if bit == 1 and gate:
-            send, *gate = lax.optimization_barrier((send, *gate))
-        got = swap_bit(send, size, bit)
+    for bit in bits_of(size)[skip:]:
+        keep, got = scatter_step(held, size, bit, wire)
         held = keep + got.astype(F32)
-    return (held[0], *gate) if gate else held[0]
+    return held[0]
 
 
 def row_major(values):
@@ -308,30 +310,30 @@
         )
     )
 
-    def pack_weights(up_weight, down_weight, out_weight):
-        up_pairs = up_weight.astype(LOW).reshape(shard, size, 2, deep // 2)
-        up_shard = lax.dynamic_index_in_dim(up_pairs, core, 2, False).reshape(shard, wide // 2)
-        down_shard = take_half(down_weight.astype(LOW), core, 0)
-        out_shard = take_half(out_weight.astype(LOW), core, 1)
+    def column_half(values, which):
+        half_deep = deep // 2
+        return jnp.concatenate(
+            [values[:, d * deep + which * half_deep :][:, :half_deep] for d in range(size)], axis=1
+        )
+
+    def own_halves(up_weight, down_weight, out_weight):
+        up_shard = jnp.where(on_one, column_half(up_weight, 1), column_half(up_weight, 0))
+        out_shard = jnp.where(on_one, out_weight[:, half:], out_weight[:, :half])
         return jnp.concatenate(
             [
                 up_shard[:, :width],
                 up_shard[:, width:],
-                down_shard,
+                take_half(down_weight, core, 0),
                 jnp.concatenate([out_shard[: shard // 2], out_shard[shard // 2 :]], axis=1),
             ],
             axis=0,
-        )
+        ).astype(LOW)
 
     held = qkv_shard[None]
     for bit in reversed(bits_of(size)):
-        if bit == 2:
-            held, up_weight, down_weight, out_weight = lax.optimization_barrier(
-                (held, up_weight, down_weight, out_weight)
-            )
         if bit == 1:
             held, packed = lax.optimization_barrier(
-                (held, pack_weights(up_weight, down_weight, out_weight))
+                (held, own_halves(up_weight, down_weight, out_weight))
             )
         held = gather_step(held, size, bit)
     qkv_own = held.reshape(width, 3 * half)
@@ -340,9 +342,8 @@
     def unpack(pack):
         a = pack[:, :shard].reshape(width, width)
         b = pack[:, shard : 2 * shard].reshape(width, width)
-        up = jnp.concatenate([a, b], axis=1)
         down = pack[:, 2 * shard : 2 * shard + deep // 2].reshape(wide // 2, width)
-        return up, down
+        return jnp.concatenate([a, b], axis=1), down
 
     def unpack_out(last):
         return jnp.concatenate([last[:, :, :half], last[:, :, half:]], axis=1).reshape(width, half)
@@ -473,38 +474,16 @@
     part_other = dot32(grad_a[count:], weight_a, NT) + dot32(grad_b[count:], weight_b, NT)
     part_other = swap_core(part_other.astype(LOW))
     qkv_b = rows_dot(normed_all, grad_b).reshape(size, shard, 3 * (half - cut))
-    qkv_b, grad_a, grad_b, pre_a, pre_b, grad_branch, grad_low, grad_normed_two = scatter_dp(
-        qkv_b, size, LOW, (grad_a, grad_b, pre_a, pre_b, grad_branch, grad_low, grad_normed_two)
-    )
-    qkv_a = scatter_dp(qkv_keep + qkv_got.astype(F32), size, LOW)
-    qkv_more = swap_chip(qkv_a)
-    qkv_a = jnp.where(
-        on_chip_one,
-        jnp.concatenate([qkv_more, qkv_a], axis=0),
-        jnp.concatenate([qkv_a, qkv_more], axis=0),
-    )
-    qkv_b = qkv_b + swap_chip(qkv_b.astype(LOW)).astype(F32)
-    qkv_mine = jnp.concatenate(
-        [
-            piece
-            for k in range(3)
-            for piece in (
-                qkv_a[:, k * cut : (k + 1) * cut],
-                qkv_b[:, k * (half - cut) : (k + 1) * (half - cut)],
+    qkv_a, qkv_b, grad_a, grad_b, pre_a, pre_b, grad_branch, grad_low, grad_normed_two = (
+        lax.optimization_barrier(
+            (
+                qkv_keep + qkv_got.astype(F32),
+                qkv_b, grad_a, grad_b, pre_a, pre_b, grad_branch, grad_low, grad_normed_two,
             )
-        ],
-        axis=1,
-    )
-    qkv_other = swap_core(qkv_mine)
-    qkv_out = jnp.concatenate(
-        [
-            natural(
-                qkv_mine[:, k * half : (k + 1) * half], qkv_other[:, k * half : (k + 1) * half], 1
-            )
-            for k in range(3)
-        ],
-        axis=1,
-    )
+        )
+    )
+    keep_b, got_b = scatter_step(qkv_b, size, 1, LOW)
+    keep_a, got_a = scatter_step(qkv_a, size, 1, LOW)
 
     part_own = dot32(grad_a[:count], weight_a, NT) + dot32(grad_b[:count], weight_b, NT)
     grad_normed_one = row_major(part_own + part_other.astype(F32))
@@ -531,6 +510,7 @@
     )
     token_sum = jnp.sum(tokens_grad, axis=0, keepdims=True)
     sums = jnp.concatenate([vector_sums.reshape(1, -1), token_sum], axis=1)
+    sums, got_a, got_b = lax.optimization_barrier((sums, got_a, got_b))
     sums = sums + swap_core(sums)
     sums_there = swap_chip(sums)
     sums_there, result_got, result = lax.optimization_barrier((sums_there, result_got, result))
@@ -542,6 +522,37 @@
     gathered = gather_dp(both, size)
     sums_own = gathered[:, 0]
     sums_other = gathered[:, 1]
+    qkv_a = scatter_dp(keep_a + got_a.astype(F32), size, LOW, 1)
+    qkv_b = scatter_dp(keep_b + got_b.astype(F32), size, LOW, 1)
+    qkv_more = swap_chip(qkv_a)
+    qkv_a = jnp.where(
+        on_chip_one,
+        jnp.concatenate([qkv_more, qkv_a], axis=0),
+        jnp.concatenate([qkv_a, qkv_more], axis=0),
+    )
+    qkv_b = qkv_b + swap_chip(qkv_b.astype(LOW)).astype(F32)
+    qkv_mine = jnp.concatenate(
+        [
+            piece
+            for k in range(3)
+            for piece in (
+                qkv_a[:, k * cut : (k + 1) * cut],
+                qkv_b[:, k * (half - cut) : (k + 1) * (half - cut)],
+            )
+        ],
+        axis=1,
+    )
+    qkv_other = swap_core(qkv_mine)
+    qkv_out = jnp.concatenate(
+        [
+            natural(
+                qkv_mine[:, k * half : (k + 1) * half], qkv_other[:, k * half : (k + 1) * half], 1
+            )
+            for k in range(3)
+        ],
+        axis=1,
+    )
+
     exact = dict(precision=lax.Precision.HIGHEST, preferred_element_type=F32)
     contract = (((0,), (0,)), ((), ()))
     time_grad = lax.dot_general(
@@ -560,9 +571,16 @@
 
     up_ga, down_ga, out_ga = unpack_grads(shards)
     up_gb, down_gb, out_gb = unpack_grads(shards_other)
-    up_out = natural(
-        up_ga.reshape(shard, size, 1, deep // 2), up_gb.reshape(shard, size, 1, deep // 2), 2
-    ).reshape(shard, wide)
+    up_low = jnp.where(on_one, up_gb, up_ga)
+    up_high = jnp.where(on_one, up_ga, up_gb)
+    up_out = jnp.concatenate(
+        [
+            side[:, d * (deep // 2) : (d + 1) * (deep // 2)]
+            for d in range(size)
+            for side in (up_low, up_high)
+        ],
+        axis=1,
+    )
 
     def hand_back(kept, got):
         return row_major(

time: 473 us -> 473 us (level)
  local copies, waits for them, and re-layouts: 74.3 us -> 62.8 us
  matrix products: 82.2 us -> 90.9 us
  waiting for transfers between devices: 53.1 us -> 61 us
    ppermute x9, waiting for transfers between devices: 15.6 us -> 22.7 us  [swap_chip(): return lax.ppermute(values, 'seq', CHIP_SWAP)]
    dot_general x20, matrix products: 55.4 us -> 61.9 us  [dot32(): lax.dot_general(left, right, dims, preferred_element_type=jnp.float32)]
    unnamed x185 -> x176, local copies, waits for them, and re-layouts: 15.9 us -> 13.7 us
  transfers between devices with their start and end apart: 43 -> 43, of which waited for: 21 -> 20; matrix products, arithmetic and copies ran while one was open for 33% -> 34% of each run, Pallas kernels for 27% -> 27%
where the time goes in v3:
time: 473 us; the launch traced here: 466 us
  Pallas kernels  127 us (27%)
  matrix products  90.9 us (19%)
  other arithmetic  64.4 us (14%)
  local copies, waits for them, and re-layouts  62.8 us (13%)
  waiting for transfers between devices  61 us (13%)
  starting transfers between devices  44.2 us (9%)
  between operations  16.1 us (3%)
    pallas_call x2, Pallas kernels, attention_backward(): pl.pallas_call(functools.partial(attention_backward_kernel, chunk=min(chu...  76.8 us
    dot_general x20, matrix products, dot32(): lax.dot_general(left, right, dims, preferred_element_type=jnp.float32)  61.9 us
    pallas_call x2, Pallas kernels, attention_forward(): pl.pallas_call(functools.partial(attention_forward_kernel, chunk=min(chun...  50 us
    ppermute x21, waiting for transfers between devices, swap_bit(): return lax.ppermute(values, 'dp', [(i, i ^ bit) for i in range(size)])  36.3 us
    ppermute x21, starting transfers between devices, swap_bit(): return lax.ppermute(values, 'dp', [(i, i ^ bit) for i in range(size)])  32.4 us
    ppermute x9, waiting for transfers between devices, swap_chip(): return lax.ppermute(values, 'seq', CHIP_SWAP)  22.7 us
    unnamed x176, local copies, waits for them, and re-layouts  13.7 us
    dot_general x1, matrix products, layer(): jnp.dot(normed_all, qkv_own, preferred_element_type=F32).astype(LOW)  9.66 us
  transfers between devices with their start and end apart: 43, of which 20 were waited for; matrix products, arithmetic and copies ran while one was open for 34% of the time, Pallas kernels for 27%

profile of v3, /device:TPU:0, one launch (start us, length us, event | category | flops | bytes accessed | tf_op | source)
XLA Modules:
  0.0 466.3 jit_solution(9879813067562548594)
XLA Ops:
  14.2 3.1 collective-permute-start.1
  17.2 2.6 collective-permute-start.8
  19.8 3.3 dynamic-slice_bitcast_fusion.3
  24.6 2.5 fusion.112
  33.0 9.1 %collective-permute-done.9 = bf16[2,96,1152]{2,1,0:T(8,128)(2,1)} collective-permute-done((bf16[2,96,1152]{2,1,0:T(8,128)(2,1)S(1)}, bf16[2,96,1152]{2,1,0:T(8,128)(2,1)}, u32[]{:S(2)}, u32[]{:S(2)}) %collective-permute-start.9) | collective-permute-done | bytes 442400 | tf_op jit(solution)/shard_map/ppermute | solution.py:191
  45.1 2.1 collective-permute-done.2
  47.3 3.4 collective-permute-start.3
  50.7 1.7 collective-permute-done.3
  54.6 3.6 collective-permute-done.4
  58.2 1.8 collective-permute-start.5
  60.6 1.8 collective-permute-done.5
  62.4 2.8 collective-permute-start.6
  65.4 2.2 collective-permute-done.6
  68.0 1.7 fusion.99
  69.8 2.0 multiply_reduce_fusion.5
  71.8 3.2 add_convert_fusion.3
  78.5 5.9 %collective-permute-done.10 = bf16[4,96,1152]{2,1,0:T(8,128)(2,1)} collective-permute-done((bf16[4,96,1152]{2,1,0:T(8,128)(2,1)S(1)}, bf16[4,96,1152]{2,1,0:T(8,128)(2,1)}, u32[]{:S(2)}, u32[]{:S(2)}) %collective-permute-start.10) | collective-permute-done | bytes 884768 | tf_op jit(solution)/shard_map/ppermute | solution.py:191
  86.1 9.7 %convolution_convert_fusion.q_ref.k_ref.v_ref = bf16[2048,1152]{1,0:T(8,128)(2,1)} fusion(bf16[768,1152]{1,0:T(8,128)(2,1)S(1)} %bitcast.352, bf16[1024,768]{1,0:T(8,128)(2,1)} %collective-permute-done.7, bf16[1024,768]{1,0:T(8,128)(2,1)} %add_convert_fusion.3), kind=kOutput, calls=%fused_computation.3 | convolution fusion | flops 3632529408 | bytes 9633792 | tf_op jit(solution)/shard_map/dot_general | solution.py:384
  98.6 32.3 %attention_forward.2 = (bf16[2048,256]{1,0:T(8,128)(2,1)}, f32[2,128,2048]{2,1,0:T(8,128)}, f32[2,2,2048]{2,1,0:T(2,128)}) custom-call(f32[2048,1]{1,0:T(8,128)} %broadcast_select_fusion.2.bias_ref, bf16[2048,1152]{1,0:T(8,128)(2,1)} %convolution_convert_fusion.q_ref.k_ref.v_ref, bf16[2048,1152]{1,0:T(8,128)(2,1)} %convolution_convert_fusion.q_ref.k_ref.v_ref, ...), custom_call_target="tpu_custom_call" | custom-call | flops 17179869184 | bytes 8388608 | tf_op jit(solution)/shard_map/attention_forward/pallas_call | solution.py:115
  132.6 2.0 slice.620
  134.6 3.2 fusion.104
  139.1 17.7 %attention_forward.3 = (bf16[2048,128]{1,0:T(8,128)(2,1)}, f32[1,128,2048]{2,1,0:T(8,128)}, f32[1,2,2048]{2,1,0:T(2,128)}) custom-call(f32[2048,1]{1,0:T(8,128)} %broadcast_select_fusion.2.bias_ref, bf16[2048,1152]{1,0:T(8,128)(2,1)} %convolution_convert_fusion.q_ref.k_ref.v_ref, bf16[2048,1152]{1,0:T(8,128)(2,1)} %convolution_convert_fusion.q_ref.k_ref.v_ref, ...), custom_call_target="tpu_custom_call" | custom-call | flops 8589934592 | bytes 4194304 | tf_op jit(solution)/shard_map/attention_forward/pallas_call | solution.py:115
  159.1 2.0 slice.626
  163.6 3.4 fusion.129
  169.4 5.3 %multiply_convert_fusion.1 = (bf16[1024,1536]{1,0:T(8,128)(2,1)}, f32[1024,1536]{1,0:T(8,128)S(1)}) fusion(f32[1536]{0:T(1024)S(1)} %add.313, bf16[1024,768]{1,0:T(8,128)(2,1)S(1)} %add_convert_fusion.2, bf16[768,768]{1,0:T(8,128)(2,1)S(1)} %bitcast.379, bf16[768,768]{1,0:T(8,128)(2,1)S(1)} %bitcast.377), kind=kOutput, calls=%fused_computation.15 | convolution fusion | flops 2430074880 | bytes 13375488 | tf_op jit(solution)/shard_map/dot_general | solution.py:415
  174.8 5.4 %multiply_convert_fusion.3 = bf16[1024,1536]{1,0:T(8,128)(2,1)S(1)} fusion(bf16[1024,768]{1,0:T(8,128)(2,1)S(1)} %copy-done.14, bf16[1536,768]{1,0:T(8,128)(2,1)S(1)} %bitcast.371, f32[1024,1536]{1,0:T(8,128)S(1)} %get-tuple-element.257, f32[1536]{0:T(1024)S(1)} %add.313), kind=kOutput, calls=%fused_computation.18 | convolution fusion | flops 2436366336 | bytes 13375488 | tf_op jit(solution)/shard_map/dot_general | solution.py:18
  180.2 2.9 fusion.103
  183.1 2.9 multiply_convert_fusion
  186.0 3.0 convolution_convert_fusion.1
  189.0 1.8 slice.768
  190.9 5.4 %multiply_convert_fusion.2 = bf16[1024,1536]{1,0:T(8,128)(2,1)S(1)} fusion(bf16[1024,768]{1,0:T(8,128)(2,1)S(1)} %copy-done.14, bf16[1536,768]{1,0:T(8,128)(2,1)S(1)} %bitcast.373, f32[1024,1536]{1,0:T(8,128)S(1)} %get-tuple-element.255, f32[1536]{0:T(1024)S(1)} %add.319), kind=kOutput, calls=%fused_computation.16 | convolution fusion | flops 2436366336 | bytes 13375488 | tf_op jit(solution)/shard_map/dot_general | solution.py:18
  196.3 2.6 fusion.16
  199.0 3.1 convolution_convert_fusion.2
  202.1 3.2 multiply_reduce_fusion.7
  205.4 3.6 fusion.102
  209.0 2.7 fusion.98
  212.9 4.6 maximum_maximum_fusion
  218.0 2.0 fusion.108
  220.0 2.3 fusion.109
  222.3 4.7 %convolution_convert_fusion.3 = bf16[1536,768]{1,0:T(8,128)(2,1)S(1)} fusion(bf16[1024,1536]{1,0:T(8,128)(2,1)} %get-tuple-element.256, bf16[1024,768]{1,0:T(8,128)(2,1)S(1)} %copy-done.15), kind=kOutput, calls=%fused_computation.23 | convolution fusion | flops 2417098752 | bytes 7077888 | tf_op jit(solution)/shard_map/dot_general | solution.py:18
  227.1 2.6 fusion.130
  233.0 2.6 add_select_fusion
  239.2 2.9 convolution_convert_fusion.4
  243.6 7.2 %add_convert_fusion = bf16[8,432,768]{2,1,0:T(8,128)(2,1)} fusion(bf16[8,432,768]{2,1,0:T(8,128)(2,1)} %collective-permute-done.17, bf16[8,48,384]{2,1,0:T(8,128)(2,1)S(1)} %get-tuple-element.199, bf16[8,48,384]{2,1,0:T(8,128)(2,1)S(1)} %get-tuple-element.198, bf16[8,192,768]{2,1,0:T(8,128)(2,1)S(1)} %bitcast.375, bf16[8,96,768]{2,1,0:T(8,128)(2,1)S(1)} %bitcast.360, ...), kind=kLoop, calls=%fused_computation | loop fusion | flops 34504704 | bytes 15925248 | tf_op jit(solution)/shard_map/convert_element_type | solution.py:457
  250.9 26.7 %attention_backward.3 = (bf16[2048,128]{1,0:T(8,128)(2,1)}, bf16[2048,128]{1,0:T(8,128)(2,1)}, bf16[2048,128]{1,0:T(8,128)(2,1)}) custom-call(f32[2048,1]{1,0:T(8,128)} %broadcast_select_fusion.2.bias_ref, bf16[2048,1152]{1,0:T(8,128)(2,1)} %convolution_convert_fusion.q_ref.k_ref.v_ref, bf16[2048,1152]{1,0:T(8,128)(2,1)} %convolution_convert_fusion.q_ref.k_ref.v_ref, ...), custom_call_target="tpu_custom_call" | custom-call | flops 21474836480 | bytes 4194304 | tf_op jit(solution)/shard_map/attention_backward/pallas_call | solution.py:146
  277.6 1.9 constant_dynamic-update-slice_fusion.5
  279.5 50.1 %attention_backward.2 = (bf16[2048,256]{1,0:T(8,128)(2,1)}, bf16[2048,256]{1,0:T(8,128)(2,1)}, bf16[2048,256]{1,0:T(8,128)(2,1)}) custom-call(f32[2048,1]{1,0:T(8,128)} %broadcast_select_fusion.2.bias_ref, bf16[2048,1152]{1,0:T(8,128)(2,1)} %convolution_convert_fusion.q_ref.k_ref.v_ref, bf16[2048,1152]{1,0:T(8,128)(2,1)} %convolution_convert_fusion.q_ref.k_ref.v_ref, ...), custom_call_target="tpu_custom_call" | custom-call | flops 42949672960 | bytes 8388608 | tf_op jit(solution)/shard_map/attention_backward/pallas_call | solution.py:146
  332.7 5.7 %fusion.19 = f32[768,768]{1,0:T(8,128)S(1)} fusion(bf16[2048,768]{1,0:T(8,128)(2,1)S(1)} %constant_dynamic-update-slice_fusion, bf16[1024,768]{1,0:T(8,128)(2,1)} %collective-permute-done.7, bf16[1024,768]{1,0:T(8,128)(2,1)} %add_convert_fusion.3), kind=kOutput, calls=%fused_computation.86 | convolution fusion | flops 2422210560 | bytes 8650752 | tf_op jit(solution)/shard_map/dot_general | solution.py:18
  341.2 2.2 add_convert_fusion.1
  343.5 4.7 %fusion.18 = f32[768,384]{1,0:T(8,128)} fusion(bf16[2048,384]{1,0:T(8,128)(2,1)S(1)} %constant_dynamic-update-slice_fusion.3, bf16[1024,768]{1,0:T(8,128)(2,1)} %collective-permute-done.7, bf16[1024,768]{1,0:T(8,128)(2,1)} %add_convert_fusion.3), kind=kOutput, calls=%fused_computation.85 | convolution fusion | flops 1214251008 | bytes 5898240 | tf_op jit(solution)/shard_map/dot_general | solution.py:18
  348.3 5.7 %collective-permute-done.18 = bf16[8,48,768]{2,1,0:T(8,128)(2,1)S(1)} collective-permute-done((bf16[8,48,768]{2,1,0:T(8,128)(2,1)S(1)}, bf16[8,48,768]{2,1,0:T(8,128)(2,1)S(1)}, u32[]{:S(2)}, u32[]{:S(2)}) %collective-permute-start.18) | collective-permute-done | bytes 589856 | tf_op jit(solution)/shard_map/ppermute | solution.py:187
  360.1 2.6 convolution_reduce_fusion.1
  363.4 2.4 convolution_reduce_fusion
  371.7 2.9 fusion.13
  374.7 4.8 %multiply_reduce_fusion.2 = (f32[768]{0:T(1024)S(1)}, f32[1024]{0:T(1024)S(1)}, f32[1024]{0:T(1024)S(1)}, f32[768]{0:T(1024)S(1)}, f32[1024,768]{1,0:T(8,128)}) fusion(f32[1024]{0:T(1024)S(1)} %copy-done.71, f32[1024]{0:T(1024)S(1)} %copy-done.66, f32[768]{0:T(1024)S(1)} %copy-done.63, f32[512,768]{1,0:T(8,128)} %collective-permute-done, ...), kind=kOutput, calls=%fused_computation.34 | convolution fusion | flops 616755712 | bytes 12417024 | tf_op jit(solution)/shard_map/dot_general | solution.py:18
  379.6 5.5 %fusion.101 = (f32[768]{0:T(1024)S(1)}, f32[1024,768]{1,0:T(8,128)}) fusion(f32[1024,768]{1,0:T(8,128)} %get-tuple-element.117, f32[1024]{0:T(1024)S(1)} %broadcast_multiply_fusion, f32[1024]{0:T(1024)S(1)} %copy-done.66, f32[768]{0:T(1024)S(1)} %copy-done.63, f32[512,768]{1,0:T(8,128)} %collective-permute-done, f32[512,768]{1,0:T(8,128)S(1)} %copy-done.4, ...), kind=kLoop, calls=%fused_computation.293 | loop fusion | flops 8649984 | bytes 12608512 | tf_op jit(solution)/shard_map/reduce_sum | solution.py:511
  399.3 3.9 maximum_select_fusion.1
  408.2 3.4 collective-permute-start.31
  414.5 1.9 collective-permute-done.28
  419.1 2.0 collective-permute-start.33
  421.1 3.3 collective-permute-done.36
  426.6 2.2 collective-permute-done.37
  437.0 1.9 maximum_select_fusion.2
  440.0 13.1 %collective-permute-done.39 = bf16[432,768]{1,0:T(8,128)(2,1)S(1)} collective-permute-done((bf16[432,768]{1,0:T(8,128)(2,1)}, bf16[432,768]{1,0:T(8,128)(2,1)S(1)}, u32[]{:S(2)}, u32[]{:S(2)}) %collective-permute-start.39) | collective-permute-done | bytes 663584 | tf_op jit(solution)/shard_map/ppermute | solution.py:187
  (421 shorter events, 109.4 us)
Async XLA Ops:
  7.2 19.9 %copy-start = (f32[384,768]{1,0:T(8,128)S(1)}, f32[384,768]{1,0:T(8,128)}, u32[]{:S(2)}) copy-start(f32[384,768]{1,0:T(8,128)} %param.29) | copy-start | bytes 3538948
  7.2 125.4 %all-gather.3.cloned.1.call-start = ((), (), s32[]{:S(2)}) async-start(), calls=%async_computation.2 | async-start | bytes 5971968 | tf_op jit(solution)/shard_map/all_gather | solution.py:340
  14.2 29.3 %collective-permute-start.1 = (f32[1,1,962]{2,1,0:T(1,128)S(1)}, f32[1,1,962]{2,1,0:T(1,128)S(1)}, u32[]{:S(2)}, u32[]{:S(2)}) collective-permute-start(f32[1,1,962]{2,1,0:T(1,128)S(1)} %bitcast.406), channel_id=1, source_target_pairs={{0,4},{4,0},{8,12},{12,8},{16,20},{20,16},{24,28},{28,24},{1,5},{5... | collective-permute-start | bytes 11552 | tf_op jit(solution)/shard_map/ppermute | solution.py:191
  17.2 12.6 %collective-permute-start.8 = (bf16[1,96,1152]{2,1,0:T(8,128)(2,1)S(1)}, bf16[1,96,1152]{2,1,0:T(8,128)(2,1)}, u32[]{:S(2)}, u32[]{:S(2)}) collective-permute-start(bf16[1,96,1152]{2,1,0:T(8,128)(2,1)S(1)} %bitcast.385), channel_id=1, source_target_pairs={{0,16},{4,20},{8,24},{12,28},{16,0},{20,4},{24,8},{28,12},{1,17},{... | collective-permute-start | bytes 663560 | tf_op jit(solution)/shard_map/ppermute | solution.py:191
  23.1 48.6 %copy-start.2 = (f32[512,768]{1,0:T(8,128)}, f32[512,768]{1,0:T(8,128)S(1)}, u32[]{:S(2)}) copy-start(f32[512,768]{1,0:T(8,128)S(1)} %get-tuple-element.126) | copy-start | bytes 4718596
  23.1 44.9 %collective-permute-start = (f32[512,768]{1,0:T(8,128)}, f32[512,768]{1,0:T(8,128)}, u32[]{:S(2)}, u32[]{:S(2)}) collective-permute-start(f32[512,768]{1,0:T(8,128)} %get-tuple-element.127), channel_id=1, source_target_pairs={{0,2},{2,0},{1,3},{3,1},{4,6},{6,4},{5,7},{7,5},{8,10},{10,8},{9,1... | collective-permute-start | bytes 4718600 | tf_op jit(solution)/shard_map/ppermute | solution.py:187
  30.9 11.2 %collective-permute-start.9 = (bf16[2,96,1152]{2,1,0:T(8,128)(2,1)S(1)}, bf16[2,96,1152]{2,1,0:T(8,128)(2,1)}, u32[]{:S(2)}, u32[]{:S(2)}) collective-permute-start(bf16[2,96,1152]{2,1,0:T(8,128)(2,1)S(1)} %maximum_bitcast_fusion), channel_id=1, source_target_pairs={{0,8},{4,12},{8,0},{12,4},{16,24},{20,28},{24,16},{28,20},{1,9},{5... | collective-permute-start | bytes 1327112 | tf_op jit(solution)/shard_map/ppermute | solution.py:191
  32.1 27.9 %copy-start.80 = (s32[2]{0:T(128)S(1)}, s32[2]{0:T(128)}, u32[]{:S(2)}) copy-start(s32[2]{0:T(128)} %param.18) | copy-start | bytes 28
  43.4 392.1 %reduce-scatter.2.cloned.1.call-start = ((), (), s32[]{:S(2)}) async-start(), calls=%async_computation.1 | async-start | bytes 5971968 | tf_op jit(solution)/shard_map/reduce_scatter | solution.py:459
  43.5 3.7 collective-permute-start.2
  47.3 5.1 %collective-permute-start.3 = (f32[4,1,962]{2,1,0:T(1,128)S(1)}, f32[4,1,962]{2,1,0:T(1,128)S(1)}, u32[]{:S(2)}, u32[]{:S(2)}) collective-permute-start(f32[4,1,962]{2,1,0:T(1,128)S(1)} %pad_maximum_fusion.29), channel_id=1, source_target_pairs={{0,16},{4,20},{8,24},{12,28},{16,0},{20,4},{24,8},{28,12},{1,17},{... | collective-permute-start | bytes 46184 | tf_op jit(solution)/shard_map/ppermute | solution.py:191
  54.0 4.1 collective-permute-start.4
  58.2 4.1 collective-permute-start.5
  62.4 5.2 %collective-permute-start.6 = (f32[1,1,768]{2,1,0:T(1,128)S(1)}, f32[1,1,768]{2,1,0:T(1,128)S(1)}, u32[]{:S(2)}, u32[]{:S(2)}) collective-permute-start(f32[1,1,768]{2,1,0:T(1,128)S(1)} %fusion.76), channel_id=1, source_target_pairs={{0,16},{4,20},{8,24},{12,28},{16,0},{20,4},{24,8},{28,12},{1,17},{... | collective-permute-start | bytes 9224 | tf_op jit(solution)/shard_map/ppermute | solution.py:191
  67.6 96.0 %copy-start.62 = (f32[768]{0:T(1024)}, f32[768]{0:T(1024)S(1)}, u32[]{:S(2)}) copy-start(f32[768]{0:T(1024)S(1)} %fusion.75) | copy-start | bytes 9220
  67.6 16.8 %collective-permute-start.10 = (bf16[4,96,1152]{2,1,0:T(8,128)(2,1)S(1)}, bf16[4,96,1152]{2,1,0:T(8,128)(2,1)}, u32[]{:S(2)}, u32[]{:S(2)}) collective-permute-start(bf16[4,96,1152]{2,1,0:T(8,128)(2,1)S(1)} %bitcast.365), channel_id=1, source_target_pairs={{0,4},{4,0},{8,12},{12,8},{16,20},{20,16},{24,28},{28,24},{1,5},{5... | collective-permute-start | bytes 2654216 | tf_op jit(solution)/shard_map/ppermute | solution.py:191
  75.0 11.1 %collective-permute-start.7 = (bf16[1024,768]{1,0:T(8,128)(2,1)}, bf16[1024,768]{1,0:T(8,128)(2,1)}, u32[]{:S(2)}, u32[]{:S(2)}) collective-permute-start(bf16[1024,768]{1,0:T(8,128)(2,1)} %add_convert_fusion.3), channel_id=1, source_target_pairs={{0,1},{1,0},{2,3},{3,2},{4,5},{5,4},{6,7},{7,6},{8,9},{9,8},{10,11... | collective-permute-start | bytes 4718600 | tf_op jit(solution)/shard_map/ppermute | solution.py:183
  86.1 9.7 %copy-start.11 = (bf16[4,2,96,1152]{3,2,1,0:T(8,128)(2,1)}, bf16[4,2,96,1152]{3,2,1,0:T(8,128)(2,1)S(1)}, u32[]{:S(2)}) copy-start(bf16[4,2,96,1152]{3,2,1,0:T(8,128)(2,1)S(1)} %copy.197) | copy-start | bytes 5308420
  86.1 9.7 %copy-start.29 = (f32[2,512,768]{2,1,0:T(8,128)S(1)}, f32[2,512,768]{2,1,0:T(8,128)}, u32[]{:S(2)}) copy-start(f32[2,512,768]{2,1,0:T(8,128)} %param.31) | copy-start | bytes 9437188
  97.1 33.8 %copy-start.5 = (f32[512,768]{1,0:T(8,128)}, f32[512,768]{1,0:T(8,128)S(1)}, u32[]{:S(2)}) copy-start(f32[512,768]{1,0:T(8,128)S(1)} %get-tuple-element.124) | copy-start | bytes 4718596
  97.1 33.8 %collective-permute-start.11 = (f32[512,768]{1,0:T(8,128)}, f32[512,768]{1,0:T(8,128)S(1)}, u32[]{:S(2)}, u32[]{:S(2)}) collective-permute-start(f32[512,768]{1,0:T(8,128)} %get-tuple-element.125), channel_id=1, source_target_pairs={{0,2},{2,0},{1,3},{3,1},{4,6},{6,4},{5,7},{7,5},{8,10},{10,8},{9,1... | collective-permute-start | bytes 4718600 | tf_op jit(solution)/shard_map/ppermute | solution.py:187
  137.7 42.4 %collective-permute-start.15 = (bf16[8,432,768]{2,1,0:T(8,128)(2,1)}, bf16[8,432,768]{2,1,0:T(8,128)(2,1)}, u32[]{:S(2)}, u32[]{:S(2)}) collective-permute-start(bf16[8,432,768]{2,1,0:T(8,128)(2,1)} %bitcast.40), channel_id=1, source_target_pairs={{0,1},{1,0},{2,3},{3,2},{4,5},{5,4},{6,7},{7,6},{8,9},{9,8},{10,11... | collective-permute-start | bytes 15925256 | tf_op jit(solution)/shard_map/ppermute | solution.py:183
  138.6 24.2 %collective-permute-start.12 = (bf16[1024,256]{1,0:T(8,128)(2,1)S(1)}, bf16[1024,256]{1,0:T(8,128)(2,1)S(1)}, u32[]{:S(2)}, u32[]{:S(2)}) collective-permute-start(bf16[1024,256]{1,0:T(8,128)(2,1)S(1)} %get-tuple-element.168), channel_id=1, source_target_pairs={{0,1},{1,0},{2,3},{3,2},{4,5},{5,4},{6,7},{7,6},{8,9},{9,8},{10,11... | collective-permute-start | bytes 1572872 | tf_op jit(solution)/shard_map/ppermute | solution.py:183
  139.1 22.6 %collective-permute-start.14 = (bf16[8,48,768]{2,1,0:T(8,128)(2,1)}, bf16[8,48,768]{2,1,0:T(8,128)(2,1)S(1)}, u32[]{:S(2)}, u32[]{:S(2)}) collective-permute-start(bf16[8,48,768]{2,1,0:T(8,128)(2,1)} %slice.620), channel_id=1, source_target_pairs={{0,1},{1,0},{2,3},{3,2},{4,5},{5,4},{6,7},{7,6},{8,9},{9,8},{10,11... | collective-permute-start | bytes 1769480 | tf_op jit(solution)/shard_map/ppermute | solution.py:183
  161.1 13.7 %copy-start.32 = (bf16[8,192,768]{2,1,0:T(8,128)(2,1)}, bf16[8,192,768]{2,1,0:T(8,128)(2,1)S(1)}, u32[]{:S(2)}) copy-start(bf16[8,192,768]{2,1,0:T(8,128)(2,1)S(1)} %slice.626) | copy-start | bytes 7077892
  161.1 1.7 collective-permute-start.13
  168.1 30.8 %copy-start.36 = (bf16[1024,768]{1,0:T(8,128)(2,1)}, bf16[1024,768]{1,0:T(8,128)(2,1)S(1)}, u32[]{:S(2)}) copy-start(bf16[1024,768]{1,0:T(8,128)(2,1)S(1)} %add_convert_fusion.2) | copy-start | bytes 4718596
  180.2 16.1 %copy-start.26 = (bf16[1024,1536]{1,0:T(8,128)(2,1)}, bf16[1024,1536]{1,0:T(8,128)(2,1)S(1)}, u32[]{:S(2)}) copy-start(bf16[1024,1536]{1,0:T(8,128)(2,1)S(1)} %multiply_convert_fusion.3) | copy-start | bytes 9437188
  217.5 26.1 %collective-permute-start.17 = (bf16[8,432,768]{2,1,0:T(8,128)(2,1)}, bf16[8,432,768]{2,1,0:T(8,128)(2,1)}, u32[]{:S(2)}, u32[]{:S(2)}) collective-permute-start(bf16[8,432,768]{2,1,0:T(8,128)(2,1)} %maximum_maximum_fusion), channel_id=1, source_target_pairs={{0,1},{1,0},{2,3},{3,2},{4,5},{5,4},{6,7},{7,6},{8,9},{9,8},{10,11... | collective-permute-start | bytes 15925256 | tf_op jit(solution)/shard_map/ppermute | solution.py:183
  231.4 10.9 %collective-permute-start.16 = (bf16[1024,384]{1,0:T(8,128)(2,1)S(1)}, bf16[1024,384]{1,0:T(8,128)(2,1)S(1)}, u32[]{:S(2)}, u32[]{:S(2)}) collective-permute-start(bf16[1024,384]{1,0:T(8,128)(2,1)S(1)} %get-tuple-element.141), channel_id=1, source_target_pairs={{0,1},{1,0},{2,3},{3,2},{4,5},{5,4},{6,7},{7,6},{8,9},{9,8},{10,11... | collective-permute-start | bytes 2359304 | tf_op jit(solution)/shard_map/ppermute | solution.py:183
  237.0 158.4 %collective-permute-start.24 = (f32[512,768]{1,0:T(8,128)}, f32[512,768]{1,0:T(8,128)}, u32[]{:S(2)}, u32[]{:S(2)}) collective-permute-start(f32[512,768]{1,0:T(8,128)} %slice.798), channel_id=1, source_target_pairs={{0,2},{2,0},{1,3},{3,1},{4,6},{6,4},{5,7},{7,5},{8,10},{10,8},{9,1... | collective-permute-start | bytes 4718600 | tf_op jit(solution)/shard_map/ppermute | solution.py:187
  332.7 6.9 %copy-start.60 = (bf16[2048,768]{1,0:T(8,128)(2,1)}, bf16[2048,768]{1,0:T(8,128)(2,1)S(1)}, u32[]{:S(2)}) copy-start(bf16[2048,768]{1,0:T(8,128)(2,1)S(1)} %constant_dynamic-update-slice_fusion) | copy-start | bytes 9437188
  338.6 15.4 %collective-permute-start.18 = (bf16[8,48,768]{2,1,0:T(8,128)(2,1)S(1)}, bf16[8,48,768]{2,1,0:T(8,128)(2,1)S(1)}, u32[]{:S(2)}, u32[]{:S(2)}) collective-permute-start(bf16[8,48,768]{2,1,0:T(8,128)(2,1)S(1)} %fusion.22), channel_id=1, source_target_pairs={{0,2},{2,0},{1,3},{3,1},{4,6},{6,4},{5,7},{7,5},{8,10},{10,8},{9,1... | collective-permute-start | bytes 1769480 | tf_op jit(solution)/shard_map/ppermute | solution.py:187
  343.4 31.2 %collective-permute-start.19 = (bf16[1024,768]{1,0:T(8,128)(2,1)}, bf16[1024,768]{1,0:T(8,128)(2,1)}, u32[]{:S(2)}, u32[]{:S(2)}) collective-permute-start(bf16[1024,768]{1,0:T(8,128)(2,1)} %add_convert_fusion.1), channel_id=1, source_target_pairs={{0,1},{1,0},{2,3},{3,2},{4,5},{5,4},{6,7},{7,6},{8,9},{9,8},{10,11... | collective-permute-start | bytes 4718600 | tf_op jit(solution)/shard_map/ppermute | solution.py:183
  348.3 6.9 %copy-start.8 = (f32[1024,768]{1,0:T(8,128)S(1)}, f32[1024,768]{1,0:T(8,128)}, u32[]{:S(2)}) copy-start(f32[1024,768]{1,0:T(8,128)} %copy-done.7) | copy-start | bytes 9437188
  360.1 7.9 %copy-start.30 = (f32[768,384]{1,0:T(8,128)S(1)}, f32[768,384]{1,0:T(8,128)}, u32[]{:S(2)}) copy-start(f32[768,384]{1,0:T(8,128)} %fusion.18) | copy-start | bytes 3538948
  360.1 9.3 %copy-start.10 = (f32[8,48,768]{2,1,0:T(8,128)S(1)}, f32[8,48,768]{2,1,0:T(8,128)}, u32[]{:S(2)}) copy-start(f32[8,48,768]{2,1,0:T(8,128)} %bitcast_add_fusion) | copy-start | bytes 3538948
  362.7 9.0 %copy-start.56 = (bf16[768,256]{1,0:T(8,128)(2,1)S(1)}, bf16[768,256]{1,0:T(8,128)(2,1)}, u32[]{:S(2)}) copy-start(bf16[768,256]{1,0:T(8,128)(2,1)} %get-tuple-element.135) | copy-start | bytes 1179652
  362.7 9.0 %copy-start.58 = (bf16[768,256]{1,0:T(8,128)(2,1)S(1)}, bf16[768,256]{1,0:T(8,128)(2,1)}, u32[]{:S(2)}) copy-start(bf16[768,256]{1,0:T(8,128)(2,1)} %get-tuple-element.136) | copy-start | bytes 1179652
  368.8 16.6 %collective-permute-start.21 = (bf16[4,96,384]{2,1,0:T(8,128)(2,1)}, bf16[4,96,384]{2,1,0:T(8,128)(2,1)}, u32[]{:S(2)}, u32[]{:S(2)}) collective-permute-start(bf16[4,96,384]{2,1,0:T(8,128)(2,1)} %fusion.29), channel_id=1, source_target_pairs={{0,4},{4,0},{8,12},{12,8},{16,20},{20,16},{24,28},{28,24},{1,5},{5... | collective-permute-start | bytes 884744 | tf_op jit(solution)/shard_map/ppermute | solution.py:191
  370.2 15.2 %collective-permute-start.20 = (bf16[4,48,768]{2,1,0:T(8,128)(2,1)}, bf16[4,48,768]{2,1,0:T(8,128)(2,1)}, u32[]{:S(2)}, u32[]{:S(2)}) collective-permute-start(bf16[4,48,768]{2,1,0:T(8,128)(2,1)} %fusion.28), channel_id=1, source_target_pairs={{0,4},{4,0},{8,12},{12,8},{16,20},{20,16},{24,28},{28,24},{1,5},{5... | collective-permute-start | bytes 884744 | tf_op jit(solution)/shard_map/ppermute | solution.py:191
  385.4 4.8 %collective-permute-start.22 = (f32[1,8448]{1,0:T(1,128)S(1)}, f32[1,8448]{1,0:T(1,128)S(1)}, u32[]{:S(2)}, u32[]{:S(2)}) collective-permute-start(f32[1,8448]{1,0:T(1,128)S(1)} %pad_maximum_fusion.24), channel_id=1, source_target_pairs={{0,1},{1,0},{2,3},{3,2},{4,5},{5,4},{6,7},{7,6},{8,9},{9,8},{10,11... | collective-permute-start | bytes 101384 | tf_op jit(solution)/shard_map/ppermute | solution.py:183
  390.2 5.1 %collective-permute-start.23 = (f32[1,8448]{1,0:T(1,128)S(1)}, f32[1,8448]{1,0:T(1,128)S(1)}, u32[]{:S(2)}, u32[]{:S(2)}) collective-permute-start(f32[1,8448]{1,0:T(1,128)S(1)} %add.332), channel_id=1, source_target_pairs={{0,2},{2,0},{1,3},{3,1},{4,6},{6,4},{5,7},{7,5},{8,10},{10,8},{9,1... | collective-permute-start | bytes 101384 | tf_op jit(solution)/shard_map/ppermute | solution.py:187
  391.9 27.1 %collective-permute-start.32 = (bf16[2,48,768]{2,1,0:T(8,128)(2,1)S(1)}, bf16[2,48,768]{2,1,0:T(8,128)(2,1)S(1)}, u32[]{:S(2)}, u32[]{:S(2)}) collective-permute-start(bf16[2,48,768]{2,1,0:T(8,128)(2,1)S(1)} %fusion.34), channel_id=1, source_target_pairs={{0,8},{4,12},{8,0},{12,4},{16,24},{20,28},{24,16},{28,20},{1,9},{5... | collective-permute-start | bytes 442376 | tf_op jit(solution)/shard_map/ppermute | solution.py:191
  393.3 24.5 %collective-permute-start.35 = (bf16[2,96,384]{2,1,0:T(8,128)(2,1)S(1)}, bf16[2,96,384]{2,1,0:T(8,128)(2,1)S(1)}, u32[]{:S(2)}, u32[]{:S(2)}) collective-permute-start(bf16[2,96,384]{2,1,0:T(8,128)(2,1)S(1)} %fusion.35), channel_id=1, source_target_pairs={{0,8},{4,12},{8,0},{12,4},{16,24},{20,28},{24,16},{28,20},{1,9},{5... | collective-permute-start | bytes 442376 | tf_op jit(solution)/shard_map/ppermute | solution.py:191
  393.9 40.4 %collective-permute-start.25 = (bf16[512,768]{1,0:T(8,128)(2,1)}, bf16[512,768]{1,0:T(8,128)(2,1)}, u32[]{:S(2)}, u32[]{:S(2)}) collective-permute-start(bf16[512,768]{1,0:T(8,128)(2,1)} %slice.1012), channel_id=1, source_target_pairs={{0,2},{2,0},{1,3},{3,1},{4,6},{6,4},{5,7},{7,5},{8,10},{10,8},{9,1... | collective-permute-start | bytes 2359304 | tf_op jit(solution)/shard_map/ppermute | solution.py:187
  395.4 7.9 %collective-permute-start.26 = (f32[1,2,768]{2,1,0:T(2,128)S(1)}, f32[1,2,768]{2,1,0:T(2,128)S(1)}, u32[]{:S(2)}, u32[]{:S(2)}) collective-permute-start(f32[1,2,768]{2,1,0:T(2,128)S(1)} %fusion.67), channel_id=1, source_target_pairs={{0,4},{4,0},{8,12},{12,8},{16,20},{20,16},{24,28},{28,24},{1,5},{5... | collective-permute-start | bytes 18440 | tf_op jit(solution)/shard_map/ppermute | solution.py:191
  396.5 7.9 %collective-permute-start.29 = (f32[4,1,960]{2,1,0:T(1,128)S(1)}, f32[4,1,960]{2,1,0:T(1,128)S(1)}, u32[]{:S(2)}, u32[]{:S(2)}) collective-permute-start(f32[4,1,960]{2,1,0:T(1,128)S(1)} %fusion.57), channel_id=1, source_target_pairs={{0,4},{4,0},{8,12},{12,8},{16,20},{20,16},{24,28},{28,24},{1,5},{5... | collective-permute-start | bytes 46088 | tf_op jit(solution)/shard_map/ppermute | solution.py:191
  399.3 17.2 %copy-start.73 = (bf16[8,2,96]{2,0,1:T(8,128)(2,1)S(1)}, bf16[8,2,96]{2,0,1:T(8,128)(2,1)}, u32[]{:S(2)}) copy-start(bf16[8,2,96]{2,0,1:T(8,128)(2,1)} %copy-done.72) | copy-start | bytes 9220
  399.3 18.6 %copy-start.24 = (f32[4,96,384]{2,1,0:T(8,128)S(1)}, f32[4,96,384]{2,1,0:T(8,128)}, u32[]{:S(2)}) copy-start(f32[4,96,384]{2,1,0:T(8,128)} %copy-done.23) | copy-start | bytes 1769476
  399.3 19.7 %copy-start.22 = (f32[4,48,768]{2,1,0:T(8,128)S(1)}, f32[4,48,768]{2,1,0:T(8,128)}, u32[]{:S(2)}) copy-start(f32[4,48,768]{2,1,0:T(8,128)} %copy-done.21) | copy-start | bytes 1769476
  403.3 3.8 collective-permute-start.27
  404.5 3.7 collective-permute-start.30
  408.2 5.0 %collective-permute-start.31 = (f32[1,1,960]{2,1,0:T(1,128)S(1)}, f32[1,1,960]{2,1,0:T(1,128)S(1)}, u32[]{:S(2)}, u32[]{:S(2)}) collective-permute-start(f32[1,1,960]{2,1,0:T(1,128)S(1)} %fusion.70), channel_id=1, source_target_pairs={{0,16},{4,20},{8,24},{12,28},{16,0},{20,4},{24,8},{28,12},{1,17},{... | collective-permute-start | bytes 11528 | tf_op jit(solution)/shard_map/ppermute | solution.py:191
  411.6 4.8 %collective-permute-start.28 = (f32[4,2,768]{2,1,0:T(2,128)S(1)}, f32[4,2,768]{2,1,0:T(2,128)S(1)}, u32[]{:S(2)}, u32[]{:S(2)}) collective-permute-start(f32[4,2,768]{2,1,0:T(2,128)S(1)} %pad_maximum_fusion.28), channel_id=1, source_target_pairs={{0,16},{4,20},{8,24},{12,28},{16,0},{20,4},{24,8},{28,12},{1,17},{... | collective-permute-start | bytes 73736 | tf_op jit(solution)/shard_map/ppermute | solution.py:191
  417.9 6.4 %collective-permute-start.36 = (bf16[1,96,384]{2,1,0:T(8,128)(2,1)S(1)}, bf16[1,96,384]{2,1,0:T(8,128)(2,1)S(1)}, u32[]{:S(2)}, u32[]{:S(2)}) collective-permute-start(bf16[1,96,384]{2,1,0:T(8,128)(2,1)S(1)} %fusion.45), channel_id=1, source_target_pairs={{0,16},{4,20},{8,24},{12,28},{16,0},{20,4},{24,8},{28,12},{1,17},{... | collective-permute-start | bytes 221192 | tf_op jit(solution)/shard_map/ppermute | solution.py:191
  419.0 17.9 %copy-start.20 = (f32[1,512,768]{2,1,0:T(8,128)S(1)}, f32[1,512,768]{2,1,0:T(8,128)}, u32[]{:S(2)}) copy-start(f32[1,512,768]{2,1,0:T(8,128)} %slice_bitcast_fusion) | copy-start | bytes 4718596
  419.1 6.1 %collective-permute-start.33 = (bf16[1,48,768]{2,1,0:T(8,128)(2,1)S(1)}, bf16[1,48,768]{2,1,0:T(8,128)(2,1)S(1)}, u32[]{:S(2)}, u32[]{:S(2)}) collective-permute-start(bf16[1,48,768]{2,1,0:T(8,128)(2,1)S(1)} %fusion.44), channel_id=1, source_target_pairs={{0,16},{4,20},{8,24},{12,28},{16,0},{20,4},{24,8},{28,12},{1,17},{... | collective-permute-start | bytes 221192 | tf_op jit(solution)/shard_map/ppermute | solution.py:191
  424.4 4.4 collective-permute-start.37
  425.2 5.2 %collective-permute-start.34 = (f32[48,768]{1,0:T(8,128)S(1)}, f32[48,768]{1,0:T(8,128)S(1)}, u32[]{:S(2)}, u32[]{:S(2)}) collective-permute-start(f32[48,768]{1,0:T(8,128)S(1)} %fusion.36), channel_id=1, source_target_pairs={{0,2},{2,0},{1,3},{3,1},{4,6},{6,4},{5,7},{7,5},{8,10},{10,8},{9,1... | collective-permute-start | bytes 442376 | tf_op jit(solution)/shard_map/ppermute | solution.py:187
  434.3 4.6 collective-permute-start.38
  435.6 17.6 %copy-start.47 = (bf16[1,432,768]{2,1,0:T(8,128)(2,1)S(1)}, bf16[1,432,768]{2,1,0:T(8,128)(2,1)}, u32[]{:S(2)}) copy-start(bf16[1,432,768]{2,1,0:T(8,128)(2,1)} %reduce-scatter.2.cloned.1.call-done) | copy-start | bytes 1990660
  435.6 17.6 %collective-permute-start.39 = (bf16[432,768]{1,0:T(8,128)(2,1)}, bf16[432,768]{1,0:T(8,128)(2,1)S(1)}, u32[]{:S(2)}, u32[]{:S(2)}) collective-permute-start(bf16[432,768]{1,0:T(8,128)(2,1)} %bitcast.386), channel_id=1, source_target_pairs={{0,2},{2,0},{1,3},{3,1},{4,6},{6,4},{5,7},{7,5},{8,10},{10,8},{9,1... | collective-permute-start | bytes 1990664 | tf_op jit(solution)/shard_map/ppermute | solution.py:187
  453.3 2.2 collective-permute-start.40
  (63 other events, 241.9 us)
Sparse Core Ops, SparseCore 0:
  43.5 88.1 all-gather.2
  251.0 104.2 reduce-scatter.1
